TPU v7x, 32 devices: a whole 2x2x4 slice. The times are simulated.
32 devices in a mesh: dom: 8 (over y, x, core), grp: 4 (over z).
Axes of the slice: x: 2, y: 2, z: 4, core: 2. Of those that a mesh axis runs over, the one named last changes fastest.
Arguments:
- history: bfloat16 [16, 4, 128, 4096], P('dom', None, 'grp'), may hold values from -6 to 6
- face_patch: int32 [16, 6], replicated, may hold values from -1 to 15, as said below
- refined: int32 [16], replicated, may hold values 0 or 1
- dest_slot: int32 [16], replicated, may hold values from 0 to 15, as said below
- w_in: bfloat16 [640, 512], replicated, may hold values from -0.25 to 0.25
- in_bias: float32 [512], replicated, may hold values from -3 to 3
- w_out: bfloat16 [512, 128], replicated, may hold values from -0.25 to 0.25
Outputs:
- new_states: bfloat16 [16, 2, 128, 4096], P('dom', None, 'grp')
Inputs may be any that keep to these rules, and one draw needn't show every extreme that they name: `dest_slot`: A permutation of the slots. Slot s lies on dom index s // 2; patch p starts at slot p, on index p // 2. No patch moves by more than one index of dom, from one index at most 1 patches go to each neighbouring index, and 1 is reached between some pair of indices. `face_patch`: -1 where the face lies on the window's boundary, else a patch other than p, aligned with p cell for cell on that face; its dom index is within one of p's both before and after rebalancing.
All inputs are finite; a program needn't handle non-finite values.
Results may differ from a plain program's by a relative error of at most 0.0071.
Values may be sent and summed in bfloat16 or wider, within the bound.
No kernel may reach another device: no remote copies, remote signals or barrier semaphores. Data moves between devices by JAX's collectives and lax.ppermute only.
A program may use at most 128 MiB of HBM per device.

v0:
```python
import functools

import jax
import jax.numpy as jnp
import numpy as np
from jax import lax
from jax.experimental import pallas as pl
from jax.experimental.pallas import tpu as pltpu
from jax.sharding import PartitionSpec as P

SIDE = 16
HIST = 4
PLANE = SIDE * SIDE


OPPOSITE = np.array([1, 0, 3, 2, 5, 4])


def padded(array, sides, width):
    for axis, dim in sides:
        size, length = (lax.axis_size(axis), array.shape[dim])
        up = [(i, (i + 1) % size) for i in range(size - 1)]
        down = [(j, i) for i, j in up]
        last = lax.slice_in_dim(array, length - width, length, axis=dim)
        first = lax.slice_in_dim(array, 0, width, axis=dim)
        before = lax.ppermute(last, axis, up)
        after = lax.ppermute(first, axis, down)
        array = jnp.concatenate([before, array, after], axis=dim)
    return array


def select_table(side_len, stride, offset):
    rows = jnp.arange(side_len)[:, None]
    cols = jnp.arange(side_len * side_len)[None, :]
    return (cols == rows * stride + offset).astype(jnp.bfloat16)


def take_face(grid_rows, table):
    return jnp.einsum("ncxq,kq->ncxk", grid_rows, table, preferred_element_type=jnp.float32).astype(
        jnp.bfloat16
    )


def place_face(face_rows, table):
    return jnp.einsum("ncxk,kq->ncxq", face_rows, table, preferred_element_type=jnp.float32)


def laplace_cells(newest, positions, usable):
    how_many, channels, cell_count = newest.shape
    plane = SIDE * SIDE
    grid_rows = newest.reshape(how_many, channels, SIDE, plane)
    y_low = select_table(SIDE, 1, 0)
    y_high = select_table(SIDE, 1, plane - SIDE)
    z_low = select_table(SIDE, SIDE, 0)
    z_high = select_table(SIDE, SIDE, SIDE - 1)
    layers = jnp.stack(
        [
            grid_rows[:, :, 0, :],
            grid_rows[:, :, -1, :],
            take_face(grid_rows, y_low).reshape(how_many, channels, plane),
            take_face(grid_rows, y_high).reshape(how_many, channels, plane),
            take_face(grid_rows, z_low).reshape(how_many, channels, plane),
            take_face(grid_rows, z_high).reshape(how_many, channels, plane),
        ],
        1,
    )
    layers = layers[:, OPPOSITE]
    beside_all = padded(layers, (("dom", 0),), how_many)
    picked = beside_all[positions, jnp.arange(6)[None, :]]
    picked = jnp.where(usable[:, :, None, None], picked, jnp.zeros_like(picked))
    field = grid_rows.astype(jnp.float32)
    picked_wide = picked.astype(jnp.float32)
    x_plus = jnp.concatenate([field[:, :, 1:, :], picked_wide[:, 1][:, :, None, :]], 2)
    x_minus = jnp.concatenate([picked_wide[:, 0][:, :, None, :], field[:, :, :-1, :]], 2)
    zero_row = jnp.zeros((how_many, channels, SIDE, SIDE), jnp.float32)
    y_plus = jnp.concatenate([field[..., SIDE:], zero_row], 3)
    y_plus = y_plus + place_face(picked[:, 3].reshape(how_many, channels, SIDE, SIDE), y_high)
    y_minus = jnp.concatenate([zero_row, field[..., :-SIDE]], 3)
    y_minus = y_minus + place_face(picked[:, 2].reshape(how_many, channels, SIDE, SIDE), y_low)
    z_index = jnp.arange(plane) % SIDE
    zero_cell = jnp.zeros((how_many, channels, SIDE, 1), jnp.float32)
    z_plus = jnp.concatenate([field[..., 1:], zero_cell], 3)
    z_plus = jnp.where(z_index == SIDE - 1, 0.0, z_plus)
    z_plus = z_plus + place_face(picked[:, 5].reshape(how_many, channels, SIDE, SIDE), z_high)
    z_minus = jnp.concatenate([zero_cell, field[..., :-1]], 3)
    z_minus = jnp.where(z_index == 0, 0.0, z_minus)
    z_minus = z_minus + place_face(picked[:, 4].reshape(how_many, channels, SIDE, SIDE), z_low)
    neighbour_sum = x_plus + x_minus + y_plus + y_minus + z_plus + z_minus
    spread = neighbour_sum - 6.0 * field
    return spread.reshape(how_many, channels, cell_count).astype(jnp.bfloat16)


def local_general(history, face_patch, refined, dest_slot, w_in, in_bias, w_out):
    per_dev = history.shape[0]
    my_index = lax.axis_index("dom")
    lowest = (my_index - 1) * per_dev
    my_slots = my_index * per_dev + jnp.arange(per_dev, dtype=jnp.int32)
    patch_ids = jnp.arange(dest_slot.shape[0], dtype=jnp.int32)
    inverse = jnp.zeros_like(dest_slot).at[dest_slot].set(patch_ids)

    def advance(inputs):
        how_many = inputs.shape[0]
        cell_count = inputs.shape[3]
        stacked = inputs.reshape(how_many, -1, cell_count)
        preact = (
            jnp.einsum("nkc,kh->nch", stacked, w_in, preferred_element_type=jnp.float32) + in_bias
        )
        hidden = jax.nn.silu(preact).astype(jnp.bfloat16)
        update = jnp.einsum(
            "nch,hk->nkc", hidden, w_out, preferred_element_type=jnp.float32
        ).astype(jnp.bfloat16)
        back = lax.all_to_all(update, "grp", split_axis=1, concat_axis=2, tiled=True)
        return (back, update, inputs[:, : HIST - 1])

    first_nb = face_patch[my_slots]
    first_pos = jnp.clip(first_nb - lowest, 0, 3 * per_dev - 1)
    first_ok = first_nb >= 0
    first_spread = laplace_cells(history[:, 0], first_pos, first_ok)
    first_in = jnp.concatenate([history, first_spread[:, None]], 1)
    first_back, _, _ = advance(
        lax.all_to_all(first_in, "grp", split_axis=3, concat_axis=2, tiled=True)
    )
    first_step = 1.0 - 0.5 * refined[my_slots].astype(jnp.float32)
    first_state = (
        history[:, 0].astype(jnp.float32)
        + first_step[:, None, None] * first_back.astype(jnp.float32)
    ).astype(jnp.bfloat16)
    carried = jnp.concatenate([first_state[:, None], history[:, : HIST - 1]], 1)
    owners = inverse[my_slots]
    second_nb = face_patch[owners]
    second_pos = jnp.clip(dest_slot[jnp.maximum(second_nb, 0)] - lowest, 0, 3 * per_dev - 1)
    second_ok = second_nb >= 0
    second_step = 1.0 - 0.5 * refined[owners].astype(jnp.float32)
    sources = inverse[my_slots]
    beside_all = padded(carried.reshape(per_dev, -1), (("dom", 0),), per_dev)
    moved_carried = jnp.take(beside_all, sources - lowest, axis=0).reshape(carried.shape)
    newest = moved_carried[:, 0]
    second_spread = laplace_cells(newest, second_pos, second_ok)
    second_in = jnp.concatenate([moved_carried, second_spread[:, None]], 1)
    second_back, _, _ = advance(
        lax.all_to_all(second_in, "grp", split_axis=3, concat_axis=2, tiled=True)
    )
    second_state = (
        newest.astype(jnp.float32) + second_step[:, None, None] * second_back.astype(jnp.float32)
    ).astype(jnp.bfloat16)
    return jnp.stack([moved_carried[:, 0], second_state], 1)


SLAB = 4 * PLANE
HALF = 2 * PLANE
FACE_LANES = 3 * PLANE
PLAN_SIZE = 64
VMEM = pltpu.VMEM
SMEM = pltpu.SMEM


def face_tables():
    lay = np.zeros((SLAB, PLANE), np.float32)
    put = np.zeros((PLANE, SLAB), np.float32)
    source = {2: lambda m: 240 + m, 3: lambda m: m, 4: lambda m: 16 * m + 15, 5: lambda m: 16 * m}
    target = {2: lambda m: m, 3: lambda m: 240 + m, 4: lambda m: 16 * m, 5: lambda m: 16 * m + 15}
    for face in (2, 3, 4, 5):
        for plane in range(4):
            for m in range(SIDE):
                lane = (face - 2) * 64 + plane * 16 + m
                lay[plane * PLANE + source[face](m), lane] = 1
                put[lane, plane * PLANE + target[face](m)] = 1
    flat = np.zeros((PLANE, PLANE), np.float32)
    for y in range(SIDE):
        for z in range(SIDE):
            flat[y * SIDE + z, y * SIDE + z] = -6
            for dy, dz in ((1, 0), (-1, 0), (0, 1), (0, -1)):
                if 0 <= y + dy < SIDE and 0 <= z + dz < SIDE:
                    flat[(y + dy) * SIDE + z + dz, y * SIDE + z] = 1
    return lay, put, flat


def vmem_specs(count):
    return [pl.BlockSpec(memory_space=VMEM)] * count


def plan_kernel(per_dev, place, face_patch, refined, dest_slot, *refs):
    plan = refs[-1]
    dom, grp = place[0], place[1]
    patches = dest_slot.shape[0]
    plan[0] = dom
    plan[1] = grp
    up, down = jnp.int32(0), jnp.int32(0)
    for s in range(per_dev):
        new_dom = dest_slot[dom * per_dev + s] // per_dev
        up = jnp.where(new_dom == dom + 1, s, up)
        down = jnp.where(new_dom == dom - 1, s, down)
    plan[2] = up
    plan[3] = down
    for j in range(per_dev):
        code, patch = jnp.int32(0), jnp.int32(0)
        for o in (-1, 0, 1):
            for s in range(per_dev):
                p = (dom + o) * per_dev + s
                ok = (p >= 0) & (p < patches)
                p = jnp.clip(p, 0, patches - 1)
                ok = ok & (dest_slot[p] == dom * per_dev + j)
                code = jnp.where(ok, s if o == 0 else per_dev + (o + 1) // 2, code)
                patch = jnp.where(ok, p, patch)
        plan[4 + j] = code
        plan[6 + j] = refined[patch]
        for f in range(6):
            beside = face_patch[f, patch]
            slot = dest_slot[jnp.maximum(beside, 0)]
            plan[8 + 6 * j + f] = jnp.where(beside < 0, -1, slot - (dom - 1) * per_dev)


def slab_lanes(slab, size):
    low = pl.multiple_of(slab * HALF, HALF)
    high = pl.multiple_of((2 * size - 1 - slab) * HALF, HALF)
    return ((slice(0, HALF), pl.ds(low, HALF)), (slice(HALF, SLAB), pl.ds(high, HALF)))


def channel_rows(grp, k, size, width, first=0):
    row = lax.rem(grp - k + size, size) * width
    return pl.ds(pl.multiple_of(first + row, width), width)


def settle(plan, j, own, below, above, store):
    per_dev = own.shape[0]
    code = plan[4 + j]

    @pl.when(code < per_dev)
    def _():
        store(own.at[jnp.minimum(code, per_dev - 1)])

    @pl.when(code == per_dev)
    def _():
        store(below)

    @pl.when(code == per_dev + 1)
    def _():
        store(above)


def send_kernel(plan, up_in, down_in, up_out, down_out):
    up_out[...] = up_in[0]
    down_out[...] = down_in[0]


def early_pack_kernel(size, states, place, *refs):
    for k in range(1, size + 1):
        k = k % size
        out = refs[k - size]
        for here, there in slab_lanes(lax.rem(place[1] + k, size), size):
            for t in range(states):
                for j in range(out.shape[0]):
                    out[j, t, :, here] = refs[t][j, 0, :, there]


def pack_kernel(size, states, plan, below, above, *refs):
    outs = refs[-size:]
    for t in range(states):
        for j in range(refs[t].shape[0]):

            def store(source):
                for k in range(1, size + 1):
                    k = k % size
                    for here, there in slab_lanes(lax.rem(plan[1] + k, size), size):
                        outs[k][j, t, :, here] = source[0, :, there]

            settle(plan, j, refs[t], below.at[pl.ds(t, 1)], above.at[pl.ds(t, 1)], store)


def emit_edges(plan, slab, lay, a_out, b_out, f_out):
    even = lax.rem(plan[1], 2) == 0
    for j in range(slab.shape[0]):
        @pl.when(even)
        def _():
            a_out[j] = slab[j, :, PLANE : 3 * PLANE]
            b_out[j, :, 0:PLANE] = slab[j, :, 0:PLANE]
            b_out[j, :, PLANE:HALF] = slab[j, :, 3 * PLANE : SLAB]

        @pl.when(jnp.logical_not(even))
        def _():
            b_out[j] = slab[j, :, PLANE : 3 * PLANE]
            a_out[j, :, 0:PLANE] = slab[j, :, 0:PLANE]
            a_out[j, :, PLANE:HALF] = slab[j, :, 3 * PLANE : SLAB]

        f_out[j, :, 0:PLANE] = jnp.dot(
            slab[j], lay[...], preferred_element_type=jnp.float32
        ).astype(jnp.bfloat16)
        f_out[j, :, PLANE:HALF] = slab[j, :, 0:PLANE]
        f_out[j, :, HALF:FACE_LANES] = slab[j, :, 3 * PLANE : SLAB]


def gather_kernel(size, plan, *refs):
    pieces, (slab, up, down) = refs[:size], refs[-3:]
    per_dev, states, width = pieces[0].shape[:3]
    for k in range(size):
        rows = channel_rows(plan[1], k, size, width)
        for t in range(states):
            up[t, rows] = pieces[k][plan[2], t]
            down[t, rows] = pieces[k][plan[3], t]
            for j in range(per_dev):
                slab[j, t, rows] = pieces[k][j, t]


def edge_kernel(plan, lay, old, below, above, *refs):
    slab, a_out, b_out, f_out = refs[-4:]
    for j in range(slab.shape[0]):

        def store(source):
            slab[j] = source[0]

        settle(plan, j, old, below, above, store)
    emit_edges(plan, slab, lay, a_out, b_out, f_out)


def laplacian(plan, slab, a_in, b_in, mine, below, above, put, flat, spread, first_row):
    f32 = jnp.float32
    grp = plan[1]
    per_dev, channels = slab.shape[0], slab.shape[1]
    even = lax.rem(grp, 2) == 0
    lowest, highest = grp == 0, grp == 3
    cands = [ref.at[s] for ref in (below, mine, above) for s in range(per_dev)]
    face_of_lane = lax.broadcasted_iota(jnp.int32, (channels, PLANE), 1) // 64
    for j in range(per_dev):
        layer = [slab[j, :, i * PLANE : (i + 1) * PLANE] for i in range(4)]
        wide = [x.astype(f32) for x in layer]
        a, b = a_in[j].astype(f32), b_in[j].astype(f32)
        inner = jnp.where(even, a, b)
        outer = jnp.where(even, b, a)
        inner0 = jnp.where(highest, wide[2], inner[:, :PLANE])
        inner1 = jnp.where(highest, wide[1], inner[:, PLANE:])
        code = [plan[8 + 6 * j + f] for f in range(6)]
        lane_code = jnp.where(
            face_of_lane < 2,
            jnp.where(face_of_lane == 0, code[2], code[3]),
            jnp.where(face_of_lane == 2, code[4], code[5]),
        )
        face0 = jnp.zeros((channels, PLANE), f32)
        face1 = jnp.zeros((channels, PLANE), f32)
        rest = jnp.zeros((channels, PLANE), f32)
        for c, cand in enumerate(cands):
            face0 = jnp.where(code[0] == c, cand[:, HALF:FACE_LANES].astype(f32), face0)
            face1 = jnp.where(code[1] == c, cand[:, PLANE:HALF].astype(f32), face1)
            rest = jnp.where(lane_code == c, cand[:, 0:PLANE].astype(f32), rest)
        outer0 = jnp.where(lowest, face0, outer[:, :PLANE])
        outer1 = jnp.where(lowest, face1, outer[:, PLANE:])
        placed = jnp.dot(rest.astype(jnp.bfloat16), put[...], preferred_element_type=f32)
        sides = (
            (outer0, wide[1]),
            (wide[0], inner0),
            (inner1, wide[3]),
            (wide[2], outer1),
        )
        for i in range(4):
            total = jnp.dot(layer[i], flat[...], preferred_element_type=f32)
            total = total + placed[:, i * PLANE : (i + 1) * PLANE] + sides[i][0] + sides[i][1]
            spread[first_row : first_row + channels, j * SLAB + i * PLANE : j * SLAB + (i + 1) * PLANE] = (
                total.astype(jnp.bfloat16)
            )


TILE = 512


def network(plan, inputs, slab, w_in, bias, w_out, state):
    per_dev = slab.shape[0]
    per_slab = SLAB // TILE
    steps = [1.0 - 0.5 * plan[6 + j].astype(jnp.float32) for j in range(per_dev)]
    for j in range(per_dev):
        for n in range(per_slab):
            lanes = slice(j * SLAB + n * TILE, j * SLAB + (n + 1) * TILE)
            pre = jnp.dot(w_in[...], inputs[:, lanes], preferred_element_type=jnp.float32) + bias[...]
            half = 0.5 * pre
            hidden = (half + half * jnp.tanh(half)).astype(jnp.bfloat16)
            update = jnp.dot(w_out[...], hidden, preferred_element_type=jnp.float32)
            update = update.astype(jnp.bfloat16).astype(jnp.float32)
            here = slice(n * TILE, (n + 1) * TILE)
            state[j, :, here] = (slab[j, :, here].astype(jnp.float32) + steps[j] * update).astype(
                jnp.bfloat16
            )


def emit_back(plan, state, backs):
    grp, size = plan[1], len(backs)
    width = backs[0].shape[1]
    for k in range(size):
        rows = pl.ds(pl.multiple_of(lax.rem(grp - k + size, size) * width, width), width)
        for j in range(state.shape[0]):
            backs[k][j] = state[j, rows, :]


def first_kernel(size, plan, lay, put, flat, w_in, bias, w_out, slab, a_in, b_in, mine, below, above, old, old_below, old_above, *refs):
    pieces = refs[:size]
    kept, state, a_out, b_out, f_out = refs[size : size + 5]
    backs = refs[size + 5 : 2 * size + 5]
    inputs = refs[2 * size + 5]
    per_dev, channels = slab.shape[0], slab.shape[1]
    width, early = pieces[0].shape[2], old.shape[1]
    for j in range(per_dev):
        lanes = slice(j * SLAB, (j + 1) * SLAB)
        for k in range(size):
            for t in range(pieces[k].shape[1]):
                rows = channel_rows(plan[1], k, size, width, (1 + early + t) * channels)
                inputs[rows, lanes] = pieces[k][j, t]
        inputs[0:channels, lanes] = slab[j]

        def store(source):
            for t in range(early):
                inputs[(1 + t) * channels : (2 + t) * channels, lanes] = source[t]

        settle(plan, j, old, old_below, old_above, store)
    laplacian(plan, slab, a_in, b_in, mine, below, above, put, flat, inputs, HIST * channels)
    network(plan, inputs, slab, w_in, bias, w_out, state)
    emit_edges(plan, state, lay, a_out, b_out, f_out)
    emit_back(plan, state, backs)
    kept[...] = inputs[0 : (HIST - 1) * channels, :]


def second_kernel(size, plan, put, flat, w_in, bias, w_out, slab, a_in, b_in, mine, below, above, kept, *refs):
    backs = refs[:size]
    state, inputs = refs[size : size + 2]
    per_dev, channels = slab.shape[0], slab.shape[1]
    inputs[channels : HIST * channels, :] = kept[...]
    for j in range(per_dev):
        inputs[0:channels, j * SLAB : (j + 1) * SLAB] = slab[j]
    laplacian(plan, slab, a_in, b_in, mine, below, above, put, flat, inputs, HIST * channels)
    network(plan, inputs, slab, w_in, bias, w_out, state)
    emit_back(plan, state, backs)


def finish_kernel(size, plan, *refs):
    out = refs[-1]
    for k in range(size):
        for here, there in slab_lanes(lax.rem(plan[1] + k, size), size):
            for j in range(out.shape[0]):
                out[j, 0, :, there] = refs[k][j, :, here]


def local_folded(history, face_patch, refined, dest_slot, w_in, in_bias, w_out):
    bf16 = jnp.bfloat16
    per_dev, hist, width, cells = history.shape
    size = lax.axis_size("grp")
    channels = width * size
    doms = lax.axis_size("dom")
    smem = pl.BlockSpec(memory_space=SMEM)
    anywhere = pl.BlockSpec(memory_space=pl.ANY)
    shape = jax.ShapeDtypeStruct
    place = jnp.stack([lax.axis_index("dom"), lax.axis_index("grp")]).astype(jnp.int32)
    up_ring = [(i, (i + 1) % doms) for i in range(doms)]
    down_ring = [(i, (i - 1) % doms) for i in range(doms)]

    def state_block(t):
        return pl.BlockSpec((per_dev, 1, width, cells), lambda i: (0, t, 0, 0))

    def early_pack(first, states, *after):
        return pl.pallas_call(
            functools.partial(early_pack_kernel, size, states),
            grid=(1,),
            out_shape=[shape((per_dev, states, width, SLAB), bf16)] * size,
            in_specs=[smem] + [state_block(first + t) for t in range(states)] + [anywhere] * len(after),
            out_specs=[pl.BlockSpec((per_dev, states, width, SLAB), lambda i: (0, 0, 0, 0))] * size,
        )(place, *([history] * states), *after)

    early = 1
    late = hist - 1 - early
    newest = early_pack(0, 1)
    plan = pl.pallas_call(
        functools.partial(plan_kernel, per_dev),
        out_shape=shape((PLAN_SIZE,), jnp.int32),
        in_specs=[smem] * 4 + [anywhere] * size,
        out_specs=smem,
        name="plan",
    )(place, face_patch.T, refined, dest_slot, *newest)

    def movers(first, states):
        block = (1, 1, width, cells)
        return pl.pallas_call(
            send_kernel,
            grid_spec=pltpu.PrefetchScalarGridSpec(
                num_scalar_prefetch=1,
                grid=(states,),
                in_specs=[
                    pl.BlockSpec(block, lambda i, plan: (plan[2], first + i, 0, 0)),
                    pl.BlockSpec(block, lambda i, plan: (plan[3], first + i, 0, 0)),
                ],
                out_specs=[pl.BlockSpec((1, width, cells), lambda i, plan: (i, 0, 0))] * 2,
            ),
            out_shape=[shape((states, width, cells), bf16)] * 2,
        )(plan, history, history)

    def across_dom(up, down):
        return lax.ppermute(up, "dom", up_ring), lax.ppermute(down, "dom", down_ring)

    def pack(first, states, below, above, *after):
        whole = pl.BlockSpec((states, width, cells), lambda i: (0, 0, 0))
        block = (per_dev, states, width, SLAB)
        return pl.pallas_call(
            functools.partial(pack_kernel, size, states),
            grid=(1,),
            out_shape=[shape(block, bf16)] * size,
            in_specs=[smem, whole, whole]
            + [state_block(first + t) for t in range(states)]
            + [anywhere] * len(after),
            out_specs=[pl.BlockSpec(block, lambda i: (0, 0, 0, 0))] * size,
        )(plan, below, above, *([history] * states), *after)

    def across_grp(pieces, sign):
        moved = [pieces[0]]
        for k in range(1, size):
            moved.append(lax.ppermute(pieces[k], "grp", [(i, (i + sign * k) % size) for i in range(size)]))
        return moved

    pair_a = [(i, i ^ 1) for i in range(size)]
    pair_b = [(i, i if i in (0, size - 1) else ((i + 1) ^ 1) - 1) for i in range(size)]

    def exchange(a_out, b_out, f_out):
        a_in = lax.ppermute(a_out, "grp", pair_a)
        b_in = lax.ppermute(b_out, "grp", pair_b)
        below, above = across_dom(f_out, f_out)
        return a_in, b_in, f_out, below, above

    lay, put, flat = (jnp.asarray(table, bf16) for table in face_tables())
    w_in_t, w_out_t = w_in.T, w_out.T
    bias = in_bias[:, None]

    slab_shape = shape((per_dev, channels, SLAB), bf16)
    edge_shapes = [
        shape((per_dev, channels, HALF), bf16),
        shape((per_dev, channels, HALF), bf16),
        shape((per_dev, channels, FACE_LANES), bf16),
    ]
    back_shapes = [shape((per_dev, width, SLAB), bf16)] * size

    def gather(pieces, *after):
        states = pieces[0].shape[1]
        return pl.pallas_call(
            functools.partial(gather_kernel, size),
            out_shape=[shape((per_dev, states, channels, SLAB), bf16)]
            + [shape((states, channels, SLAB), bf16)] * 2,
            in_specs=[smem] + vmem_specs(size) + [anywhere] * len(after),
            out_specs=vmem_specs(3),
        )(plan, *pieces, *after)

    newest = across_grp(newest, 1)
    up, down = movers(1 + early, late)
    below, above = across_dom(up, down)
    middle = early_pack(1, early, up)
    old0, up0, down0 = gather(newest, *middle)
    middle = across_grp(middle, 1)
    below0, above0 = across_dom(up0, down0)
    packed = pack(1 + early, late, below, above, up0)
    oldest = across_grp(packed, 1)
    slab0, *edges = pl.pallas_call(
        edge_kernel,
        out_shape=[slab_shape] + edge_shapes,
        in_specs=[smem] + vmem_specs(4) + [anywhere] * size,
        out_specs=vmem_specs(4),
        name="edges",
    )(plan, lay, old0, below0, above0, *packed)
    old1, up1, down1 = gather(middle, *edges)
    below1, above1 = across_dom(up1, down1)

    inputs = pltpu.VMEM(((hist + 1) * channels, per_dev * SLAB), bf16)
    kept, slab1, *rest = pl.pallas_call(
        functools.partial(first_kernel, size),
        out_shape=[shape(((hist - 1) * channels, per_dev * SLAB), bf16), slab_shape] + edge_shapes + back_shapes,
        in_specs=[smem] + vmem_specs(15 + size),
        out_specs=vmem_specs(5 + size),
        scratch_shapes=[inputs],
        name="first",
    )(
        plan, lay, put, flat, w_in_t, bias, w_out_t, slab0, *exchange(*edges),
        old1, below1, above1, *oldest,
    )

    parts = exchange(*rest[:3])
    back1 = across_grp(rest[3:], -1)
    state = pltpu.VMEM((per_dev, channels, SLAB), bf16)
    back2 = pl.pallas_call(
        functools.partial(second_kernel, size),
        out_shape=back_shapes,
        in_specs=[smem] + vmem_specs(12),
        out_specs=vmem_specs(size),
        scratch_shapes=[state, inputs],
        name="second",
    )(plan, put, flat, w_in_t, bias, w_out_t, slab1, *parts, kept)

    def finish(state, pieces, *before):
        return pl.pallas_call(
            functools.partial(finish_kernel, size),
            grid=(1,),
            out_shape=shape((per_dev, 2, width, cells), bf16),
            in_specs=[smem]
            + [pl.BlockSpec((per_dev, width, SLAB), lambda i: (0, 0, 0))] * size
            + [anywhere] * len(before),
            out_specs=state_block(state),
            input_output_aliases={1 + size: 0} if before else {},
        )(plan, *pieces, *before)

    out = finish(0, back1)
    back2 = across_grp(back2, -1)
    return finish(1, back2, out)


def solution(mesh):
    placed = (P("dom", None, "grp", None), P(), P(), P(), P(), P(), P())
    folded = mesh.shape["grp"] == 4

    def body(*arrays):
        return (local_folded if folded else local_general)(*arrays)

    return jax.shard_map(
        body, mesh=mesh, in_specs=placed, out_specs=P("dom", None, "grp", None), check_vma=False
    )
```

profile of v0, /device:TPU:0, one launch (start us, length us, event | category | flops | bytes accessed | tf_op | source)
XLA Modules:
  0.0 129.3 jit_solution(9756966337511190834)
XLA Ops:
  0.6 1.9 %shard_map.100 = (bf16[2,1,32,1024]{3,2,1,0:T(8,128)(2,1)}, bf16[2,1,32,1024]{3,2,1,0:T(8,128)(2,1)}, bf16[2,1,32,1024]{3,2,1,0:T(8,128)(2,1)}, bf16[2,1,32,1024]{3,2,1,0:T(8,128)(2,1)}) custom-call(s32[2]{0:T(128)} %pad_add_fusion.place, bf16[2,4,32,4096]{3,2,1,0:T(8,128)(2,1)} %refs_1_.1), custom_call_target="tpu_custom_call" | custom-call | tf_op jit(solution)/shard_map/pallas_call | solution.py:455
  4.0 2.9 %shard_map.101 = (bf16[2,32,4096]{2,1,0:T(8,128)(2,1)}, bf16[2,32,4096]{2,1,0:T(8,128)(2,1)}) custom-call(s32[64]{0:T(128)} %plan.1, bf16[2,4,32,4096]{3,2,1,0:T(8,128)(2,1)} %refs_1_.1, bf16[2,4,32,4096]{3,2,1,0:T(8,128)(2,1)} %refs_1_.1), custom_call_target="tpu_custom_call" | custom-call | tf_op jit(solution)/shard_map/pallas_call | solution.py:476
  6.8 3.6 %collective-permute-start.6 = (bf16[2,32,4096]{2,1,0:T(8,128)(2,1)}, bf16[2,32,4096]{2,1,0:T(8,128)(2,1)S(1)}, u32[]{:S(2)}, u32[]{:S(2)}) collective-permute-start(bf16[2,32,4096]{2,1,0:T(8,128)(2,1)} %get-tuple-element.54), channel_id=1, source_target_pairs={{0,28},{4,0},{8,4},{12,8},{16,12},{20,16},{24,20},{28,24},{1,29},{... | collective-permute-start | bytes 1572872 | tf_op jit(solution)/shard_map/ppermute | solution.py:491
  12.0 2.6 %collective-permute-start.1 = (bf16[2,1,32,1024]{3,2,1,0:T(8,128)(2,1)S(1)}, bf16[2,1,32,1024]{3,2,1,0:T(8,128)(2,1)S(1)}, u32[]{:S(2)}, u32[]{:S(2)}) collective-permute-start(bf16[2,1,32,1024]{3,2,1,0:T(8,128)(2,1)S(1)} %copy-done.27), channel_id=1, source_target_pairs={{0,2},{1,3},{2,0},{3,1},{4,6},{5,7},{6,4},{7,5},{8,10},{9,11},{10,... | collective-permute-start | bytes 393224 | tf_op jit(solution)/shard_map/ppermute | solution.py:509
  16.0 1.9 %shard_map.102 = (bf16[2,1,32,1024]{3,2,1,0:T(8,128)(2,1)}, bf16[2,1,32,1024]{3,2,1,0:T(8,128)(2,1)}, bf16[2,1,32,1024]{3,2,1,0:T(8,128)(2,1)}, bf16[2,1,32,1024]{3,2,1,0:T(8,128)(2,1)}) custom-call(s32[2]{0:T(128)} %pad_add_fusion.place, bf16[2,4,32,4096]{3,2,1,0:T(8,128)(2,1)} %refs_1_.1, bf16[2,32,4096]{2,1,0:T(8,128)(2,1)} %get-tuple-element.46.refs_1_), custom_call_target="tpu_custom_call" | custom-call | tf_op jit(solution)/shard_map/pallas_call | solution.py:455
  18.8 4.1 %collective-permute-done.1.refs_2_ = bf16[2,1,32,1024]{3,2,1,0:T(8,128)(2,1)S(1)} collective-permute-done((bf16[2,1,32,1024]{3,2,1,0:T(8,128)(2,1)S(1)}, bf16[2,1,32,1024]{3,2,1,0:T(8,128)(2,1)S(1)}, u32[]{:S(2)}, u32[]{:S(2)}) %collective-permute-start.1) | collective-permute-done | bytes 131104 | tf_op jit(solution)/shard_map/ppermute | solution.py:509
  23.6 2.2 %shard_map.103 = (bf16[2,1,128,1024]{3,2,1,0:T(8,128)(2,1)}, bf16[1,128,1024]{2,1,0:T(8,128)(2,1)}, bf16[1,128,1024]{2,1,0:T(8,128)(2,1)}) custom-call(s32[64]{0:T(128)} %plan.1, bf16[2,1,32,1024]{3,2,1,0:T(8,128)(2,1)} %get-tuple-element.42.refs_0_, bf16[2,1,32,1024]{3,2,1,0:T(8,128)(2,1)} %copy-done.33, bf16[2,1,32,1024]{3,2,1,0:T(8,128)(2,1)} %copy-done.34, ...), custom_call_target="tpu_custom_call" | custom-call | tf_op jit(solution)/shard_map/pallas_call | solution.py:535
  25.8 2.1 %collective-permute-start.4 = (bf16[1,128,1024]{2,1,0:T(8,128)(2,1)}, bf16[1,128,1024]{2,1,0:T(8,128)(2,1)S(1)}, u32[]{:S(2)}, u32[]{:S(2)}) collective-permute-start(bf16[1,128,1024]{2,1,0:T(8,128)(2,1)} %get-tuple-element.53), channel_id=1, source_target_pairs={{0,28},{4,0},{8,4},{12,8},{16,12},{20,16},{24,20},{28,24},{1,29},{... | collective-permute-start | bytes 786440 | tf_op jit(solution)/shard_map/ppermute | solution.py:491
  27.9 3.3 %collective-permute-start.11 = (bf16[2,1,32,1024]{3,2,1,0:T(8,128)(2,1)}, bf16[2,1,32,1024]{3,2,1,0:T(8,128)(2,1)S(1)}, u32[]{:S(2)}, u32[]{:S(2)}) collective-permute-start(bf16[2,1,32,1024]{3,2,1,0:T(8,128)(2,1)} %get-tuple-element.48.refs_5_), channel_id=1, source_target_pairs={{0,1},{1,2},{2,3},{3,0},{4,5},{5,6},{6,7},{7,4},{8,9},{9,10},{10,1... | collective-permute-start | bytes 393224 | tf_op jit(solution)/shard_map/ppermute | solution.py:509
  33.5 2.7 %shard_map.104 = (bf16[2,2,32,1024]{3,2,1,0:T(8,128)(2,1)}, bf16[2,2,32,1024]{3,2,1,0:T(8,128)(2,1)}, bf16[2,2,32,1024]{3,2,1,0:T(8,128)(2,1)}, bf16[2,2,32,1024]{3,2,1,0:T(8,128)(2,1)}) custom-call(s32[64]{0:T(128)} %plan.1, bf16[2,32,4096]{2,1,0:T(8,128)(2,1)} %copy-done.2, bf16[2,32,4096]{2,1,0:T(8,128)(2,1)} %copy-done.1, ...), custom_call_target="tpu_custom_call" | custom-call | tf_op jit(solution)/shard_map/pallas_call | solution.py:496
  36.3 3.8 %collective-permute-start.13 = (bf16[2,1,32,1024]{3,2,1,0:T(8,128)(2,1)S(1)}, bf16[2,1,32,1024]{3,2,1,0:T(8,128)(2,1)S(1)}, u32[]{:S(2)}, u32[]{:S(2)}) collective-permute-start(bf16[2,1,32,1024]{3,2,1,0:T(8,128)(2,1)S(1)} %copy-done.29), channel_id=1, source_target_pairs={{0,3},{1,0},{2,1},{3,2},{4,7},{5,4},{6,5},{7,6},{8,11},{9,8},{10,9... | collective-permute-start | bytes 393224 | tf_op jit(solution)/shard_map/ppermute | solution.py:509
  40.8 2.9 %edges.1 = (bf16[2,128,1024]{2,1,0:T(8,128)(2,1)}, bf16[2,128,512]{2,1,0:T(8,128)(2,1)}, bf16[2,128,512]{2,1,0:T(8,128)(2,1)}, bf16[2,128,768]{2,1,0:T(8,128)(2,1)}) custom-call(s32[64]{0:T(128)} %plan.1, bf16[1024,256]{1,0:T(8,128)(2,1)} %constant.15.clone.lay, bf16[2,1,128,1024]{3,2,1,0:T(8,128)(2,1)} %get-tuple-element.51.old, ...), custom_call_target="tpu_custom_call" | custom-call | tf_op jit(solution)/shard_map/edges/pallas_call | solution.py:552
  44.6 3.1 %collective-permute-done.12.refs_2_ = bf16[2,1,32,1024]{3,2,1,0:T(8,128)(2,1)S(1)} collective-permute-done((bf16[2,1,32,1024]{3,2,1,0:T(8,128)(2,1)}, bf16[2,1,32,1024]{3,2,1,0:T(8,128)(2,1)S(1)}, u32[]{:S(2)}, u32[]{:S(2)}) %collective-permute-start.12) | collective-permute-done | bytes 131104 | tf_op jit(solution)/shard_map/ppermute | solution.py:509
  47.8 1.7 %collective-permute-done.13.refs_3_ = bf16[2,1,32,1024]{3,2,1,0:T(8,128)(2,1)S(1)} collective-permute-done((bf16[2,1,32,1024]{3,2,1,0:T(8,128)(2,1)S(1)}, bf16[2,1,32,1024]{3,2,1,0:T(8,128)(2,1)S(1)}, u32[]{:S(2)}, u32[]{:S(2)}) %collective-permute-start.13) | collective-permute-done | bytes 131104 | tf_op jit(solution)/shard_map/ppermute | solution.py:509
  49.4 2.0 %collective-permute-start.10 = (bf16[2,128,768]{2,1,0:T(8,128)(2,1)}, bf16[2,128,768]{2,1,0:T(8,128)(2,1)S(1)}, u32[]{:S(2)}, u32[]{:S(2)}) collective-permute-start(bf16[2,128,768]{2,1,0:T(8,128)(2,1)} %get-tuple-element.62.refs_6_.mine), channel_id=1, source_target_pairs={{0,28},{4,0},{8,4},{12,8},{16,12},{20,16},{24,20},{28,24},{1,29},{... | collective-permute-start | bytes 1179656 | tf_op jit(solution)/shard_map/ppermute | solution.py:491
  51.5 2.3 %shard_map.105 = (bf16[2,1,128,1024]{3,2,1,0:T(8,128)(2,1)}, bf16[1,128,1024]{2,1,0:T(8,128)(2,1)}, bf16[1,128,1024]{2,1,0:T(8,128)(2,1)}) custom-call(s32[64]{0:T(128)} %plan.1, bf16[2,1,32,1024]{3,2,1,0:T(8,128)(2,1)} %get-tuple-element.47.refs_4_.refs_0_, bf16[2,1,32,1024]{3,2,1,0:T(8,128)(2,1)} %copy-done.30, bf16[2,1,32,1024]{3,2,1,0:T(8,128)(2,1)} %copy-done.31, ...), custom_call_target="tpu_custom_call" | custom-call | tf_op jit(solution)/shard_map/pallas_call | solution.py:535
  53.7 7.0 %collective-permute-done.17.refs_2_ = bf16[2,2,32,1024]{3,2,1,0:T(8,128)(2,1)S(1)} collective-permute-done((bf16[2,2,32,1024]{3,2,1,0:T(8,128)(2,1)}, bf16[2,2,32,1024]{3,2,1,0:T(8,128)(2,1)S(1)}, u32[]{:S(2)}, u32[]{:S(2)}) %collective-permute-start.17) | collective-permute-done | bytes 262176 | tf_op jit(solution)/shard_map/ppermute | solution.py:509
  60.7 1.6 %collective-permute-start.8 = (bf16[2,128,512]{2,1,0:T(8,128)(2,1)}, bf16[2,128,512]{2,1,0:T(8,128)(2,1)S(1)}, u32[]{:S(2)}, u32[]{:S(2)}) collective-permute-start(bf16[2,128,512]{2,1,0:T(8,128)(2,1)} %get-tuple-element.61.refs_5_), channel_id=1, source_target_pairs={{0,0},{1,2},{2,1},{3,3},{4,4},{5,6},{6,5},{7,7},{8,8},{9,10},{10,9... | collective-permute-start | bytes 786440 | tf_op jit(solution)/shard_map/ppermute | solution.py:517
  62.4 3.5 %collective-permute-done.7.a_in = bf16[2,128,512]{2,1,0:T(8,128)(2,1)S(1)} collective-permute-done((bf16[2,128,512]{2,1,0:T(8,128)(2,1)}, bf16[2,128,512]{2,1,0:T(8,128)(2,1)S(1)}, u32[]{:S(2)}, u32[]{:S(2)}) %collective-permute-start.7) | collective-permute-done | bytes 262176 | tf_op jit(solution)/shard_map/ppermute | solution.py:516
  65.8 2.4 %collective-permute-start.15 = (bf16[1,128,1024]{2,1,0:T(8,128)(2,1)}, bf16[1,128,1024]{2,1,0:T(8,128)(2,1)S(1)}, u32[]{:S(2)}, u32[]{:S(2)}) collective-permute-start(bf16[1,128,1024]{2,1,0:T(8,128)(2,1)} %get-tuple-element.65), channel_id=1, source_target_pairs={{0,28},{4,0},{8,4},{12,8},{16,12},{20,16},{24,20},{28,24},{1,29},{... | collective-permute-start | bytes 786440 | tf_op jit(solution)/shard_map/ppermute | solution.py:491
  73.5 8.7 %first.1 = (bf16[384,2048]{1,0:T(8,128)(2,1)}, bf16[2,128,1024]{2,1,0:T(8,128)(2,1)}, bf16[2,128,512]{2,1,0:T(8,128)(2,1)}, bf16[2,128,512]{2,1,0:T(8,128)(2,1)}...) custom-call(s32[64]{0:T(128)} %plan.1, ...), custom_call_target="tpu_custom_call" | custom-call | tf_op jit(solution)/shard_map/first/pallas_call | solution.py:563
  82.2 2.7 %collective-permute-start.22 = (bf16[2,128,768]{2,1,0:T(8,128)(2,1)}, bf16[2,128,768]{2,1,0:T(8,128)(2,1)S(1)}, u32[]{:S(2)}, u32[]{:S(2)}) collective-permute-start(bf16[2,128,768]{2,1,0:T(8,128)(2,1)} %get-tuple-element.69.mine), channel_id=1, source_target_pairs={{0,28},{4,0},{8,4},{12,8},{16,12},{20,16},{24,20},{28,24},{1,29},{... | collective-permute-start | bytes 1179656 | tf_op jit(solution)/shard_map/ppermute | solution.py:491
  85.0 1.9 %collective-permute-start.19 = (bf16[2,128,512]{2,1,0:T(8,128)(2,1)}, bf16[2,128,512]{2,1,0:T(8,128)(2,1)S(1)}, u32[]{:S(2)}, u32[]{:S(2)}) collective-permute-start(bf16[2,128,512]{2,1,0:T(8,128)(2,1)} %get-tuple-element.67), channel_id=1, source_target_pairs={{0,1},{1,0},{2,3},{3,2},{4,5},{5,4},{6,7},{7,6},{8,9},{9,8},{10,11... | collective-permute-start | bytes 786440 | tf_op jit(solution)/shard_map/ppermute | solution.py:516
  88.5 3.1 %collective-permute-start.26 = (bf16[2,32,1024]{2,1,0:T(8,128)(2,1)}, bf16[2,32,1024]{2,1,0:T(8,128)(2,1)S(1)}, u32[]{:S(2)}, u32[]{:S(2)}) collective-permute-start(bf16[2,32,1024]{2,1,0:T(8,128)(2,1)} %get-tuple-element.76), channel_id=1, source_target_pairs={{0,3},{1,0},{2,1},{3,2},{4,7},{5,4},{6,5},{7,6},{8,11},{9,8},{10,9... | collective-permute-start | bytes 393224 | tf_op jit(solution)/shard_map/ppermute | solution.py:509
  91.6 2.3 %collective-permute-done.19.a_in = bf16[2,128,512]{2,1,0:T(8,128)(2,1)S(1)} collective-permute-done((bf16[2,128,512]{2,1,0:T(8,128)(2,1)}, bf16[2,128,512]{2,1,0:T(8,128)(2,1)S(1)}, u32[]{:S(2)}, u32[]{:S(2)}) %collective-permute-start.19) | collective-permute-done | bytes 262176 | tf_op jit(solution)/shard_map/ppermute | solution.py:516
  93.9 4.1 %collective-permute-start.27 = (bf16[2,32,1024]{2,1,0:T(8,128)(2,1)}, bf16[2,32,1024]{2,1,0:T(8,128)(2,1)S(1)}, u32[]{:S(2)}, u32[]{:S(2)}) collective-permute-start(bf16[2,32,1024]{2,1,0:T(8,128)(2,1)} %get-tuple-element.77), channel_id=1, source_target_pairs={{0,2},{1,3},{2,0},{3,1},{4,6},{5,7},{6,4},{7,5},{8,10},{9,11},{10,... | collective-permute-start | bytes 393224 | tf_op jit(solution)/shard_map/ppermute | solution.py:509
  98.0 7.1 %collective-permute-start.28 = (bf16[2,32,1024]{2,1,0:T(8,128)(2,1)}, bf16[2,32,1024]{2,1,0:T(8,128)(2,1)S(1)}, u32[]{:S(2)}, u32[]{:S(2)}) collective-permute-start(bf16[2,32,1024]{2,1,0:T(8,128)(2,1)} %get-tuple-element.78), channel_id=1, source_target_pairs={{0,1},{1,2},{2,3},{3,0},{4,5},{5,6},{6,7},{7,4},{8,9},{9,10},{10,1... | collective-permute-start | bytes 393224 | tf_op jit(solution)/shard_map/ppermute | solution.py:509
  106.0 7.0 %second.1 = (bf16[2,32,1024]{2,1,0:T(8,128)(2,1)}, bf16[2,32,1024]{2,1,0:T(8,128)(2,1)}, bf16[2,32,1024]{2,1,0:T(8,128)(2,1)}, bf16[2,32,1024]{2,1,0:T(8,128)(2,1)}) custom-call(s32[64]{0:T(128)} %plan.1, bf16[256,1024]{1,0:T(8,128)(2,1)} %constant.16.clone.put, bf16[256,256]{1,0:T(8,128)(2,1)} %constant.17.clone.flat, bf16[512,640]{1,0:T(8,128)(2,1)} %bitcast.7, ...), custom_call_target="tpu_custom_call" | custom-call | tf_op jit(solution)/shard_map/second/pallas_call | solution.py:578
  113.0 3.8 %collective-permute-start.24 = (bf16[2,32,1024]{2,1,0:T(8,128)(2,1)}, bf16[2,32,1024]{2,1,0:T(8,128)(2,1)S(1)}, u32[]{:S(2)}, u32[]{:S(2)}) collective-permute-start(bf16[2,32,1024]{2,1,0:T(8,128)(2,1)} %get-tuple-element.73), channel_id=1, source_target_pairs={{0,2},{1,3},{2,0},{3,1},{4,6},{5,7},{6,4},{7,5},{8,10},{9,11},{10,... | collective-permute-start | bytes 393224 | tf_op jit(solution)/shard_map/ppermute | solution.py:509
  117.6 1.9 %shard_map.106.refs_4_ = bf16[2,2,32,4096]{3,2,1,0:T(8,128)(2,1)} custom-call(s32[64]{0:T(128)} %plan.1, bf16[2,32,1024]{2,1,0:T(8,128)(2,1)} %get-tuple-element.75.refs_0_, bf16[2,32,1024]{2,1,0:T(8,128)(2,1)} %copy-done.19, bf16[2,32,1024]{2,1,0:T(8,128)(2,1)} %copy-done.20, bf16[2,32,1024]{2,1,0:T(8,128)(2,1)} %copy-done.21), custom_call_target="tpu_custom_call" | custom-call | tf_op jit(solution)/shard_map/pallas_call | solution.py:588
  119.6 7.1 %collective-permute-done.24.refs_2_ = bf16[2,32,1024]{2,1,0:T(8,128)(2,1)S(1)} collective-permute-done((bf16[2,32,1024]{2,1,0:T(8,128)(2,1)}, bf16[2,32,1024]{2,1,0:T(8,128)(2,1)S(1)}, u32[]{:S(2)}, u32[]{:S(2)}) %collective-permute-start.24) | collective-permute-done | bytes 131104 | tf_op jit(solution)/shard_map/ppermute | solution.py:509
  127.4 1.9 %shard_map.107 = bf16[2,2,32,4096]{3,2,1,0:T(8,128)(2,1)} custom-call(s32[64]{0:T(128)} %plan.1, bf16[2,32,1024]{2,1,0:T(8,128)(2,1)} %get-tuple-element.71.refs_0_, bf16[2,32,1024]{2,1,0:T(8,128)(2,1)} %copy-done.22, bf16[2,32,1024]{2,1,0:T(8,128)(2,1)} %copy-done.23, bf16[2,32,1024]{2,1,0:T(8,128)(2,1)} %copy-done.24, ...), custom_call_target="tpu_custom_call", output_to_operand_aliasing={{}: (5, {})} | custom-call | tf_op jit(solution)/shard_map/pallas_call | solution.py:588
  (116 shorter events, 19.8 us)
Async XLA Ops:
  6.8 24.4 %collective-permute-start.6 = (bf16[2,32,4096]{2,1,0:T(8,128)(2,1)}, bf16[2,32,4096]{2,1,0:T(8,128)(2,1)S(1)}, u32[]{:S(2)}, u32[]{:S(2)}) collective-permute-start(bf16[2,32,4096]{2,1,0:T(8,128)(2,1)} %get-tuple-element.54), channel_id=1, source_target_pairs={{0,28},{4,0},{8,4},{12,8},{16,12},{20,16},{24,20},{28,24},{1,29},{... | collective-permute-start | bytes 1572872 | tf_op jit(solution)/shard_map/ppermute | solution.py:491
  10.4 22.3 %collective-permute-start.5 = (bf16[2,32,4096]{2,1,0:T(8,128)(2,1)}, bf16[2,32,4096]{2,1,0:T(8,128)(2,1)S(1)}, u32[]{:S(2)}, u32[]{:S(2)}) collective-permute-start(bf16[2,32,4096]{2,1,0:T(8,128)(2,1)} %get-tuple-element.46.refs_1_), channel_id=1, source_target_pairs={{0,4},{4,8},{8,12},{12,16},{16,20},{20,24},{24,28},{28,0},{1,5},{5... | collective-permute-start | bytes 1572872 | tf_op jit(solution)/shard_map/ppermute | solution.py:491
  10.5 8.3 %collective-permute-start = (bf16[2,1,32,1024]{3,2,1,0:T(8,128)(2,1)S(1)}, bf16[2,1,32,1024]{3,2,1,0:T(8,128)(2,1)S(1)}, u32[]{:S(2)}, u32[]{:S(2)}) collective-permute-start(bf16[2,1,32,1024]{3,2,1,0:T(8,128)(2,1)S(1)} %copy-done.28), channel_id=1, source_target_pairs={{0,1},{1,2},{2,3},{3,0},{4,5},{5,6},{6,7},{7,4},{8,9},{9,10},{10,1... | collective-permute-start | bytes 393224 | tf_op jit(solution)/shard_map/ppermute | solution.py:509
  12.0 10.9 %collective-permute-start.1 = (bf16[2,1,32,1024]{3,2,1,0:T(8,128)(2,1)S(1)}, bf16[2,1,32,1024]{3,2,1,0:T(8,128)(2,1)S(1)}, u32[]{:S(2)}, u32[]{:S(2)}) collective-permute-start(bf16[2,1,32,1024]{3,2,1,0:T(8,128)(2,1)S(1)} %copy-done.27), channel_id=1, source_target_pairs={{0,2},{1,3},{2,0},{3,1},{4,6},{5,7},{6,4},{7,5},{8,10},{9,11},{10,... | collective-permute-start | bytes 393224 | tf_op jit(solution)/shard_map/ppermute | solution.py:509
  14.6 8.3 %collective-permute-start.2 = (bf16[2,1,32,1024]{3,2,1,0:T(8,128)(2,1)S(1)}, bf16[2,1,32,1024]{3,2,1,0:T(8,128)(2,1)S(1)}, u32[]{:S(2)}, u32[]{:S(2)}) collective-permute-start(bf16[2,1,32,1024]{3,2,1,0:T(8,128)(2,1)S(1)} %copy-done.26), channel_id=1, source_target_pairs={{0,3},{1,0},{2,1},{3,2},{4,7},{5,4},{6,5},{7,6},{8,11},{9,8},{10,9... | collective-permute-start | bytes 393224 | tf_op jit(solution)/shard_map/ppermute | solution.py:509
  25.8 10.5 %collective-permute-start.4 = (bf16[1,128,1024]{2,1,0:T(8,128)(2,1)}, bf16[1,128,1024]{2,1,0:T(8,128)(2,1)S(1)}, u32[]{:S(2)}, u32[]{:S(2)}) collective-permute-start(bf16[1,128,1024]{2,1,0:T(8,128)(2,1)} %get-tuple-element.53), channel_id=1, source_target_pairs={{0,28},{4,0},{8,4},{12,8},{16,12},{20,16},{24,20},{28,24},{1,29},{... | collective-permute-start | bytes 786440 | tf_op jit(solution)/shard_map/ppermute | solution.py:491
  27.9 12.2 %collective-permute-start.3 = (bf16[1,128,1024]{2,1,0:T(8,128)(2,1)}, bf16[1,128,1024]{2,1,0:T(8,128)(2,1)S(1)}, u32[]{:S(2)}, u32[]{:S(2)}) collective-permute-start(bf16[1,128,1024]{2,1,0:T(8,128)(2,1)} %get-tuple-element.52.refs_2_), channel_id=1, source_target_pairs={{0,4},{4,8},{8,12},{12,16},{16,20},{20,24},{24,28},{28,0},{1,5},{5... | collective-permute-start | bytes 786440 | tf_op jit(solution)/shard_map/ppermute | solution.py:491
  27.9 15.8 %collective-permute-start.11 = (bf16[2,1,32,1024]{3,2,1,0:T(8,128)(2,1)}, bf16[2,1,32,1024]{3,2,1,0:T(8,128)(2,1)S(1)}, u32[]{:S(2)}, u32[]{:S(2)}) collective-permute-start(bf16[2,1,32,1024]{3,2,1,0:T(8,128)(2,1)} %get-tuple-element.48.refs_5_), channel_id=1, source_target_pairs={{0,1},{1,2},{2,3},{3,0},{4,5},{5,6},{6,7},{7,4},{8,9},{9,10},{10,1... | collective-permute-start | bytes 393224 | tf_op jit(solution)/shard_map/ppermute | solution.py:509
  31.2 16.5 %collective-permute-start.12 = (bf16[2,1,32,1024]{3,2,1,0:T(8,128)(2,1)}, bf16[2,1,32,1024]{3,2,1,0:T(8,128)(2,1)S(1)}, u32[]{:S(2)}, u32[]{:S(2)}) collective-permute-start(bf16[2,1,32,1024]{3,2,1,0:T(8,128)(2,1)} %get-tuple-element.49.refs_6_), channel_id=1, source_target_pairs={{0,2},{1,3},{2,0},{3,1},{4,6},{5,7},{6,4},{7,5},{8,10},{9,11},{10,... | collective-permute-start | bytes 393224 | tf_op jit(solution)/shard_map/ppermute | solution.py:509
  36.2 32.1 %copy-start.25 = (bf16[512,128]{1,0:T(8,128)(2,1)S(1)}, bf16[512,128]{1,0:T(8,128)(2,1)}, u32[]{:S(2)}) copy-start(bf16[512,128]{1,0:T(8,128)(2,1)} %param.16) | copy-start | bytes 393220
  36.2 15.3 %collective-permute-start.16 = (bf16[2,2,32,1024]{3,2,1,0:T(8,128)(2,1)}, bf16[2,2,32,1024]{3,2,1,0:T(8,128)(2,1)S(1)}, u32[]{:S(2)}, u32[]{:S(2)}) collective-permute-start(bf16[2,2,32,1024]{3,2,1,0:T(8,128)(2,1)} %get-tuple-element.56.refs_1_), channel_id=1, source_target_pairs={{0,1},{1,2},{2,3},{3,0},{4,5},{5,6},{6,7},{7,4},{8,9},{9,10},{10,1... | collective-permute-start | bytes 786440 | tf_op jit(solution)/shard_map/ppermute | solution.py:509
  36.3 13.1 %collective-permute-start.13 = (bf16[2,1,32,1024]{3,2,1,0:T(8,128)(2,1)S(1)}, bf16[2,1,32,1024]{3,2,1,0:T(8,128)(2,1)S(1)}, u32[]{:S(2)}, u32[]{:S(2)}) collective-permute-start(bf16[2,1,32,1024]{3,2,1,0:T(8,128)(2,1)S(1)} %copy-done.29), channel_id=1, source_target_pairs={{0,3},{1,0},{2,1},{3,2},{4,7},{5,4},{6,5},{7,6},{8,11},{9,8},{10,9... | collective-permute-start | bytes 393224 | tf_op jit(solution)/shard_map/ppermute | solution.py:509
  40.1 20.7 %collective-permute-start.17 = (bf16[2,2,32,1024]{3,2,1,0:T(8,128)(2,1)}, bf16[2,2,32,1024]{3,2,1,0:T(8,128)(2,1)S(1)}, u32[]{:S(2)}, u32[]{:S(2)}) collective-permute-start(bf16[2,2,32,1024]{3,2,1,0:T(8,128)(2,1)} %get-tuple-element.57.refs_2_), channel_id=1, source_target_pairs={{0,2},{1,3},{2,0},{3,1},{4,6},{5,7},{6,4},{7,5},{8,10},{9,11},{10,... | collective-permute-start | bytes 786440 | tf_op jit(solution)/shard_map/ppermute | solution.py:509
  40.8 28.2 %copy-start.36 = (f32[512]{0:T(512)S(1)}, f32[512]{0:T(512)}, u32[]{:S(2)}) copy-start(f32[512]{0:T(512)} %param.15) | copy-start | bytes 6148
  40.8 29.1 %copy-start = (bf16[640,512]{1,0:T(8,128)(2,1)S(1)}, bf16[640,512]{1,0:T(8,128)(2,1)}, u32[]{:S(2)}) copy-start(bf16[640,512]{1,0:T(8,128)(2,1)} %param.14) | copy-start | bytes 1966084
  43.7 18.6 %collective-permute-start.18 = (bf16[2,2,32,1024]{3,2,1,0:T(8,128)(2,1)S(1)}, bf16[2,2,32,1024]{3,2,1,0:T(8,128)(2,1)S(1)}, u32[]{:S(2)}, u32[]{:S(2)}) collective-permute-start(bf16[2,2,32,1024]{3,2,1,0:T(8,128)(2,1)S(1)} %copy-done.9), channel_id=1, source_target_pairs={{0,3},{1,0},{2,1},{3,2},{4,7},{5,4},{6,5},{7,6},{8,11},{9,8},{10,9... | collective-permute-start | bytes 786440 | tf_op jit(solution)/shard_map/ppermute | solution.py:509
  47.8 18.1 %collective-permute-start.7 = (bf16[2,128,512]{2,1,0:T(8,128)(2,1)}, bf16[2,128,512]{2,1,0:T(8,128)(2,1)S(1)}, u32[]{:S(2)}, u32[]{:S(2)}) collective-permute-start(bf16[2,128,512]{2,1,0:T(8,128)(2,1)} %get-tuple-element.60.refs_4_), channel_id=1, source_target_pairs={{0,1},{1,0},{2,3},{3,2},{4,5},{5,4},{6,7},{7,6},{8,9},{9,8},{10,11... | collective-permute-start | bytes 786440 | tf_op jit(solution)/shard_map/ppermute | solution.py:516
  49.4 23.0 %collective-permute-start.10 = (bf16[2,128,768]{2,1,0:T(8,128)(2,1)}, bf16[2,128,768]{2,1,0:T(8,128)(2,1)S(1)}, u32[]{:S(2)}, u32[]{:S(2)}) collective-permute-start(bf16[2,128,768]{2,1,0:T(8,128)(2,1)} %get-tuple-element.62.refs_6_.mine), channel_id=1, source_target_pairs={{0,28},{4,0},{8,4},{12,8},{16,12},{20,16},{24,20},{28,24},{1,29},{... | collective-permute-start | bytes 1179656 | tf_op jit(solution)/shard_map/ppermute | solution.py:491
  51.4 21.0 %collective-permute-start.9 = (bf16[2,128,768]{2,1,0:T(8,128)(2,1)}, bf16[2,128,768]{2,1,0:T(8,128)(2,1)S(1)}, u32[]{:S(2)}, u32[]{:S(2)}) collective-permute-start(bf16[2,128,768]{2,1,0:T(8,128)(2,1)} %get-tuple-element.62.refs_6_.mine), channel_id=1, source_target_pairs={{0,4},{4,8},{8,12},{12,16},{16,20},{20,24},{24,28},{28,0},{1,5},{5... | collective-permute-start | bytes 1179656 | tf_op jit(solution)/shard_map/ppermute | solution.py:491
  60.7 10.2 %collective-permute-start.8 = (bf16[2,128,512]{2,1,0:T(8,128)(2,1)}, bf16[2,128,512]{2,1,0:T(8,128)(2,1)S(1)}, u32[]{:S(2)}, u32[]{:S(2)}) collective-permute-start(bf16[2,128,512]{2,1,0:T(8,128)(2,1)} %get-tuple-element.61.refs_5_), channel_id=1, source_target_pairs={{0,0},{1,2},{2,1},{3,3},{4,4},{5,6},{6,5},{7,7},{8,8},{9,10},{10,9... | collective-permute-start | bytes 786440 | tf_op jit(solution)/shard_map/ppermute | solution.py:517
  62.4 8.6 %collective-permute-start.14 = (bf16[1,128,1024]{2,1,0:T(8,128)(2,1)}, bf16[1,128,1024]{2,1,0:T(8,128)(2,1)S(1)}, u32[]{:S(2)}, u32[]{:S(2)}) collective-permute-start(bf16[1,128,1024]{2,1,0:T(8,128)(2,1)} %get-tuple-element.64), channel_id=1, source_target_pairs={{0,4},{4,8},{8,12},{12,16},{16,20},{20,24},{24,28},{28,0},{1,5},{5... | collective-permute-start | bytes 786440 | tf_op jit(solution)/shard_map/ppermute | solution.py:491
  65.8 6.6 %collective-permute-start.15 = (bf16[1,128,1024]{2,1,0:T(8,128)(2,1)}, bf16[1,128,1024]{2,1,0:T(8,128)(2,1)S(1)}, u32[]{:S(2)}, u32[]{:S(2)}) collective-permute-start(bf16[1,128,1024]{2,1,0:T(8,128)(2,1)} %get-tuple-element.65), channel_id=1, source_target_pairs={{0,28},{4,0},{8,4},{12,8},{16,12},{20,16},{24,20},{28,24},{1,29},{... | collective-permute-start | bytes 786440 | tf_op jit(solution)/shard_map/ppermute | solution.py:491
  82.2 22.9 %collective-permute-start.22 = (bf16[2,128,768]{2,1,0:T(8,128)(2,1)}, bf16[2,128,768]{2,1,0:T(8,128)(2,1)S(1)}, u32[]{:S(2)}, u32[]{:S(2)}) collective-permute-start(bf16[2,128,768]{2,1,0:T(8,128)(2,1)} %get-tuple-element.69.mine), channel_id=1, source_target_pairs={{0,28},{4,0},{8,4},{12,8},{16,12},{20,16},{24,20},{28,24},{1,29},{... | collective-permute-start | bytes 1179656 | tf_op jit(solution)/shard_map/ppermute | solution.py:491
  85.0 20.1 %collective-permute-start.21 = (bf16[2,128,768]{2,1,0:T(8,128)(2,1)}, bf16[2,128,768]{2,1,0:T(8,128)(2,1)S(1)}, u32[]{:S(2)}, u32[]{:S(2)}) collective-permute-start(bf16[2,128,768]{2,1,0:T(8,128)(2,1)} %get-tuple-element.69.mine), channel_id=1, source_target_pairs={{0,4},{4,8},{8,12},{12,16},{16,20},{20,24},{24,28},{28,0},{1,5},{5... | collective-permute-start | bytes 1179656 | tf_op jit(solution)/shard_map/ppermute | solution.py:491
  85.0 8.9 %collective-permute-start.19 = (bf16[2,128,512]{2,1,0:T(8,128)(2,1)}, bf16[2,128,512]{2,1,0:T(8,128)(2,1)S(1)}, u32[]{:S(2)}, u32[]{:S(2)}) collective-permute-start(bf16[2,128,512]{2,1,0:T(8,128)(2,1)} %get-tuple-element.67), channel_id=1, source_target_pairs={{0,1},{1,0},{2,3},{3,2},{4,5},{5,4},{6,7},{7,6},{8,9},{9,8},{10,11... | collective-permute-start | bytes 786440 | tf_op jit(solution)/shard_map/ppermute | solution.py:516
  86.9 11.0 %collective-permute-start.20 = (bf16[2,128,512]{2,1,0:T(8,128)(2,1)}, bf16[2,128,512]{2,1,0:T(8,128)(2,1)S(1)}, u32[]{:S(2)}, u32[]{:S(2)}) collective-permute-start(bf16[2,128,512]{2,1,0:T(8,128)(2,1)} %get-tuple-element.68), channel_id=1, source_target_pairs={{0,0},{1,2},{2,1},{3,3},{4,4},{5,6},{6,5},{7,7},{8,8},{9,10},{10,9... | collective-permute-start | bytes 786440 | tf_op jit(solution)/shard_map/ppermute | solution.py:517
  88.5 28.3 %collective-permute-start.26 = (bf16[2,32,1024]{2,1,0:T(8,128)(2,1)}, bf16[2,32,1024]{2,1,0:T(8,128)(2,1)S(1)}, u32[]{:S(2)}, u32[]{:S(2)}) collective-permute-start(bf16[2,32,1024]{2,1,0:T(8,128)(2,1)} %get-tuple-element.76), channel_id=1, source_target_pairs={{0,3},{1,0},{2,1},{3,2},{4,7},{5,4},{6,5},{7,6},{8,11},{9,8},{10,9... | collective-permute-start | bytes 393224 | tf_op jit(solution)/shard_map/ppermute | solution.py:509
  93.9 23.0 %collective-permute-start.27 = (bf16[2,32,1024]{2,1,0:T(8,128)(2,1)}, bf16[2,32,1024]{2,1,0:T(8,128)(2,1)S(1)}, u32[]{:S(2)}, u32[]{:S(2)}) collective-permute-start(bf16[2,32,1024]{2,1,0:T(8,128)(2,1)} %get-tuple-element.77), channel_id=1, source_target_pairs={{0,2},{1,3},{2,0},{3,1},{4,6},{5,7},{6,4},{7,5},{8,10},{9,11},{10,... | collective-permute-start | bytes 393224 | tf_op jit(solution)/shard_map/ppermute | solution.py:509
  98.0 18.9 %collective-permute-start.28 = (bf16[2,32,1024]{2,1,0:T(8,128)(2,1)}, bf16[2,32,1024]{2,1,0:T(8,128)(2,1)S(1)}, u32[]{:S(2)}, u32[]{:S(2)}) collective-permute-start(bf16[2,32,1024]{2,1,0:T(8,128)(2,1)} %get-tuple-element.78), channel_id=1, source_target_pairs={{0,1},{1,2},{2,3},{3,0},{4,5},{5,6},{6,7},{7,4},{8,9},{9,10},{10,1... | collective-permute-start | bytes 393224 | tf_op jit(solution)/shard_map/ppermute | solution.py:509
  113.0 6.6 %collective-permute-start.23 = (bf16[2,32,1024]{2,1,0:T(8,128)(2,1)}, bf16[2,32,1024]{2,1,0:T(8,128)(2,1)S(1)}, u32[]{:S(2)}, u32[]{:S(2)}) collective-permute-start(bf16[2,32,1024]{2,1,0:T(8,128)(2,1)} %get-tuple-element.72), channel_id=1, source_target_pairs={{0,3},{1,0},{2,1},{3,2},{4,7},{5,4},{6,5},{7,6},{8,11},{9,8},{10,9... | collective-permute-start | bytes 393224 | tf_op jit(solution)/shard_map/ppermute | solution.py:509
  113.0 13.7 %collective-permute-start.24 = (bf16[2,32,1024]{2,1,0:T(8,128)(2,1)}, bf16[2,32,1024]{2,1,0:T(8,128)(2,1)S(1)}, u32[]{:S(2)}, u32[]{:S(2)}) collective-permute-start(bf16[2,32,1024]{2,1,0:T(8,128)(2,1)} %get-tuple-element.73), channel_id=1, source_target_pairs={{0,2},{1,3},{2,0},{3,1},{4,6},{5,7},{6,4},{7,5},{8,10},{9,11},{10,... | collective-permute-start | bytes 393224 | tf_op jit(solution)/shard_map/ppermute | solution.py:509
  116.8 9.9 %collective-permute-start.25 = (bf16[2,32,1024]{2,1,0:T(8,128)(2,1)}, bf16[2,32,1024]{2,1,0:T(8,128)(2,1)S(1)}, u32[]{:S(2)}, u32[]{:S(2)}) collective-permute-start(bf16[2,32,1024]{2,1,0:T(8,128)(2,1)} %get-tuple-element.74), channel_id=1, source_target_pairs={{0,1},{1,2},{2,3},{3,0},{4,5},{5,6},{6,7},{7,4},{8,9},{9,10},{10,1... | collective-permute-start | bytes 393224 | tf_op jit(solution)/shard_map/ppermute | solution.py:509
  (34 other events, 152.9 us)
where the time goes:
time: 130 us; the launch traced here: 129 us
  starting transfers between devices  51.3 us (39%)
  Pallas kernels  37.7 us (29%)
  waiting for transfers between devices  31.3 us (24%)
  local copies, waits for them, and re-layouts  8.15 us (6%)
    ppermute x15, starting transfers between devices, across_grp(): lax.ppermute(pieces[k], 'grp', [(i, (i + sign * k) % size) for i in range...  33.3 us
    ppermute x15, waiting for transfers between devices, across_grp(): lax.ppermute(pieces[k], 'grp', [(i, (i + sign * k) % size) for i in range...  24 us
    ppermute x5, starting transfers between devices, across_dom(): lax.ppermute(down, 'dom', down_ring)  12.9 us
    pallas_call x1, Pallas kernels, local_folded(): pl.pallas_call(functools.partial(first_kernel, size), out_shape=[shape(((...  8.73 us
    unnamed x76, local copies, waits for them, and re-layouts  7.3 us
    pallas_call x1, Pallas kernels, local_folded(): pl.pallas_call(functools.partial(second_kernel, size), out_shape=back_sha...  6.98 us
    ppermute x2, waiting for transfers between devices, exchange(): a_in = lax.ppermute(a_out, 'grp', pair_a)  5.75 us
    pallas_call x2, Pallas kernels, gather(): pl.pallas_call(functools.partial(gather_kernel, size), out_shape=[shape((...  4.44 us
  transfers between devices with their start and end apart: 29, of which 9 were waited for; matrix products, arithmetic and copies ran while one was open for 2% of the time, Pallas kernels for 16%

commit v1 on v0

--- a/solution.py
+++ b/solution.py
@@ -150,6 +150,7 @@
 HALF = 2 * PLANE
 FACE_LANES = 3 * PLANE
 PLAN_SIZE = 64
+SMALL, LARGE = 8, 16
 VMEM = pltpu.VMEM
 SMEM = pltpu.SMEM
 
@@ -173,6 +174,10 @@
                 if 0 <= y + dy < SIDE and 0 <= z + dz < SIDE:
                     flat[(y + dy) * SIDE + z + dz, y * SIDE + z] = 1
     return lay, put, flat
+
+
+def grant(mebibytes):
+    return pltpu.CompilerParams(vmem_limit_bytes=mebibytes * 2**20)
 
 
 def vmem_specs(count):
@@ -457,7 +462,8 @@
             grid=(1,),
             out_shape=[shape((per_dev, states, width, SLAB), bf16)] * size,
             in_specs=[smem] + [state_block(first + t) for t in range(states)] + [anywhere] * len(after),
-            out_specs=[pl.BlockSpec((per_dev, states, width, SLAB), lambda i: (0, 0, 0, 0))] * size,
+            out_specs=vmem_specs(size),
+            compiler_params=grant(SMALL),
         )(place, *([history] * states), *after)
 
     early = 1
@@ -468,6 +474,7 @@
         out_shape=shape((PLAN_SIZE,), jnp.int32),
         in_specs=[smem] * 4 + [anywhere] * size,
         out_specs=smem,
+        compiler_params=grant(SMALL),
         name="plan",
     )(place, face_patch.T, refined, dest_slot, *newest)
 
@@ -485,22 +492,23 @@
                 out_specs=[pl.BlockSpec((1, width, cells), lambda i, plan: (i, 0, 0))] * 2,
             ),
             out_shape=[shape((states, width, cells), bf16)] * 2,
+            compiler_params=grant(SMALL),
         )(plan, history, history)
 
     def across_dom(up, down):
         return lax.ppermute(up, "dom", up_ring), lax.ppermute(down, "dom", down_ring)
 
     def pack(first, states, below, above, *after):
-        whole = pl.BlockSpec((states, width, cells), lambda i: (0, 0, 0))
         block = (per_dev, states, width, SLAB)
         return pl.pallas_call(
             functools.partial(pack_kernel, size, states),
             grid=(1,),
             out_shape=[shape(block, bf16)] * size,
-            in_specs=[smem, whole, whole]
+            in_specs=[smem] + vmem_specs(2)
             + [state_block(first + t) for t in range(states)]
             + [anywhere] * len(after),
-            out_specs=[pl.BlockSpec(block, lambda i: (0, 0, 0, 0))] * size,
+            out_specs=vmem_specs(size),
+            compiler_params=grant(SMALL),
         )(plan, below, above, *([history] * states), *after)
 
     def across_grp(pieces, sign):
@@ -538,6 +546,7 @@
             + [shape((states, channels, SLAB), bf16)] * 2,
             in_specs=[smem] + vmem_specs(size) + [anywhere] * len(after),
             out_specs=vmem_specs(3),
+            compiler_params=grant(SMALL),
         )(plan, *pieces, *after)
 
     newest = across_grp(newest, 1)
@@ -554,6 +563,7 @@
         out_shape=[slab_shape] + edge_shapes,
         in_specs=[smem] + vmem_specs(4) + [anywhere] * size,
         out_specs=vmem_specs(4),
+        compiler_params=grant(SMALL),
         name="edges",
     )(plan, lay, old0, below0, above0, *packed)
     old1, up1, down1 = gather(middle, *edges)
@@ -566,6 +576,7 @@
         in_specs=[smem] + vmem_specs(15 + size),
         out_specs=vmem_specs(5 + size),
         scratch_shapes=[inputs],
+        compiler_params=grant(LARGE),
         name="first",
     )(
         plan, lay, put, flat, w_in_t, bias, w_out_t, slab0, *exchange(*edges),
@@ -581,6 +592,7 @@
         in_specs=[smem] + vmem_specs(12),
         out_specs=vmem_specs(size),
         scratch_shapes=[state, inputs],
+        compiler_params=grant(LARGE),
         name="second",
     )(plan, put, flat, w_in_t, bias, w_out_t, slab1, *parts, kept)
 
@@ -589,11 +601,10 @@
             functools.partial(finish_kernel, size),
             grid=(1,),
             out_shape=shape((per_dev, 2, width, cells), bf16),
-            in_specs=[smem]
-            + [pl.BlockSpec((per_dev, width, SLAB), lambda i: (0, 0, 0))] * size
-            + [anywhere] * len(before),
+            in_specs=[smem] + vmem_specs(size) + [anywhere] * len(before),
             out_specs=state_block(state),
             input_output_aliases={1 + size: 0} if before else {},
+            compiler_params=grant(SMALL),
         )(plan, *pieces, *before)
 
     out = finish(0, back1)

time: 130 us -> 125 us (0.962)
  Pallas kernels: 37.7 us -> 20.5 us
  starting transfers between devices: 51.3 us -> 58.9 us
  local copies, waits for them, and re-layouts: 8.15 us -> 11 us
  waiting for transfers between devices: 31.3 us -> 33.5 us
    ppermute x15, starting transfers between devices: 33.3 us -> 38.3 us  [across_grp(): lax.ppermute(pieces[k], 'grp', [(i, (i + sign * k) % size) for i in range...]
    ppermute x15, waiting for transfers between devices: 24 us -> 28.6 us  [across_grp(): lax.ppermute(pieces[k], 'grp', [(i, (i + sign * k) % size) for i in range...]
    ppermute x2, waiting for transfers between devices: 5.75 us -> 2 us  [exchange(): a_in = lax.ppermute(a_out, 'grp', pair_a)]
    unnamed x76 -> x42, local copies, waits for them, and re-layouts: 7.3 us -> 10.9 us
    pallas_call x1, Pallas kernels: 8.73 us -> 5.85 us  [local_folded(): pl.pallas_call(functools.partial(first_kernel, size), out_shape=[shape(((...]
    pallas_call x1, Pallas kernels: 6.98 us -> 4.25 us  [local_folded(): pl.pallas_call(functools.partial(second_kernel, size), out_shape=back_sha...]
    pallas_call x2, Pallas kernels: 3.82 us -> 1.17 us  [early_pack(): pl.pallas_call(functools.partial(early_pack_kernel, size, states), grid=(...]
    ppermute x5, waiting for transfers between devices: 0.01 us -> 2.5 us  [across_dom(): lax.ppermute(up, 'dom', up_ring)]
  transfers between devices with their start and end apart: 29 -> 29, of which waited for: 9 -> 11; matrix products, arithmetic and copies ran while one was open for 2% -> 1% of each run, Pallas kernels for 16% -> 9%
where the time goes in v1:
time: 125 us; the launch traced here: 124 us
  starting transfers between devices  58.9 us (47%)
  waiting for transfers between devices  33.5 us (27%)
  Pallas kernels  20.5 us (16%)
  local copies, waits for them, and re-layouts  11 us (9%)
    ppermute x15, starting transfers between devices, across_grp(): lax.ppermute(pieces[k], 'grp', [(i, (i + sign * k) % size) for i in range...  38.3 us
    ppermute x15, waiting for transfers between devices, across_grp(): lax.ppermute(pieces[k], 'grp', [(i, (i + sign * k) % size) for i in range...  28.6 us
    ppermute x5, starting transfers between devices, across_dom(): lax.ppermute(down, 'dom', down_ring)  12.9 us
    unnamed x42, local copies, waits for them, and re-layouts  10.9 us
    pallas_call x1, Pallas kernels, local_folded(): pl.pallas_call(functools.partial(first_kernel, size), out_shape=[shape(((...  5.85 us
    pallas_call x1, Pallas kernels, local_folded(): pl.pallas_call(functools.partial(second_kernel, size), out_shape=back_sha...  4.25 us
    ppermute x2, starting transfers between devices, exchange(): b_in = lax.ppermute(b_out, 'grp', pair_b)  4.24 us
    ppermute x2, starting transfers between devices, exchange(): a_in = lax.ppermute(a_out, 'grp', pair_a)  3.44 us
  transfers between devices with their start and end apart: 29, of which 11 were waited for; matrix products, arithmetic and copies ran while one was open for 1% of the time, Pallas kernels for 9%

profile of v1, /device:TPU:0, one launch (start us, length us, event | category | flops | bytes accessed | tf_op | source)
XLA Modules:
  0.0 124.1 jit_solution(17978414459883194962)
XLA Ops:
  0.1 1.6 %copy-done = bf16[2,4,32,4096]{3,2,1,0:T(8,128)(2,1)S(1)} copy-done((bf16[2,4,32,4096]{3,2,1,0:T(8,128)(2,1)S(1)}, bf16[2,4,32,4096]{3,2,1,0:T(8,128)(2,1)}, u32[]{:S(2)}) %copy-start) | copy-done | bytes 2097176
  4.3 3.4 %collective-permute-start.6 = (bf16[2,32,4096]{2,1,0:T(8,128)(2,1)S(1)}, bf16[2,32,4096]{2,1,0:T(8,128)(2,1)S(1)}, u32[]{:S(2)}, u32[]{:S(2)}) collective-permute-start(bf16[2,32,4096]{2,1,0:T(8,128)(2,1)S(1)} %get-tuple-element.54), channel_id=1, source_target_pairs={{0,28},{4,0},{8,4},{12,8},{16,12},{20,16},{24,20},{28,24},{1,29},{... | collective-permute-start | bytes 1572872 | tf_op jit(solution)/shard_map/ppermute | solution.py:499
  7.7 1.6 %collective-permute-start = (bf16[2,1,32,1024]{3,2,1,0:T(8,128)(2,1)S(1)}, bf16[2,1,32,1024]{3,2,1,0:T(8,128)(2,1)S(1)}, u32[]{:S(2)}, u32[]{:S(2)}) collective-permute-start(bf16[2,1,32,1024]{3,2,1,0:T(8,128)(2,1)S(1)} %get-tuple-element.43.refs_1_), channel_id=1, source_target_pairs={{0,1},{1,2},{2,3},{3,0},{4,5},{5,6},{6,7},{7,4},{8,9},{9,10},{10,1... | collective-permute-start | bytes 393224 | tf_op jit(solution)/shard_map/ppermute | solution.py:517
  9.3 2.6 %collective-permute-start.1 = (bf16[2,1,32,1024]{3,2,1,0:T(8,128)(2,1)S(1)}, bf16[2,1,32,1024]{3,2,1,0:T(8,128)(2,1)S(1)}, u32[]{:S(2)}, u32[]{:S(2)}) collective-permute-start(bf16[2,1,32,1024]{3,2,1,0:T(8,128)(2,1)S(1)} %get-tuple-element.44.refs_2_), channel_id=1, source_target_pairs={{0,2},{1,3},{2,0},{3,1},{4,6},{5,7},{6,4},{7,5},{8,10},{9,11},{10,... | collective-permute-start | bytes 393224 | tf_op jit(solution)/shard_map/ppermute | solution.py:517
  13.8 2.2 %collective-permute-done.refs_1_ = bf16[2,1,32,1024]{3,2,1,0:T(8,128)(2,1)S(1)} collective-permute-done((bf16[2,1,32,1024]{3,2,1,0:T(8,128)(2,1)S(1)}, bf16[2,1,32,1024]{3,2,1,0:T(8,128)(2,1)S(1)}, u32[]{:S(2)}, u32[]{:S(2)}) %collective-permute-start) | collective-permute-done | bytes 131104 | tf_op jit(solution)/shard_map/ppermute | solution.py:517
  16.0 4.5 %collective-permute-done.1.refs_2_ = bf16[2,1,32,1024]{3,2,1,0:T(8,128)(2,1)S(1)} collective-permute-done((bf16[2,1,32,1024]{3,2,1,0:T(8,128)(2,1)S(1)}, bf16[2,1,32,1024]{3,2,1,0:T(8,128)(2,1)S(1)}, u32[]{:S(2)}, u32[]{:S(2)}) %collective-permute-start.1) | collective-permute-done | bytes 131104 | tf_op jit(solution)/shard_map/ppermute | solution.py:517
  21.1 1.8 %collective-permute-start.4 = (bf16[1,128,1024]{2,1,0:T(8,128)(2,1)S(1)}, bf16[1,128,1024]{2,1,0:T(8,128)(2,1)S(1)}, u32[]{:S(2)}, u32[]{:S(2)}) collective-permute-start(bf16[1,128,1024]{2,1,0:T(8,128)(2,1)S(1)} %get-tuple-element.53), channel_id=1, source_target_pairs={{0,28},{4,0},{8,4},{12,8},{16,12},{20,16},{24,20},{28,24},{1,29},{... | collective-permute-start | bytes 786440 | tf_op jit(solution)/shard_map/ppermute | solution.py:499
  23.0 3.4 %collective-permute-start.11 = (bf16[2,1,32,1024]{3,2,1,0:T(8,128)(2,1)S(1)}, bf16[2,1,32,1024]{3,2,1,0:T(8,128)(2,1)S(1)}, u32[]{:S(2)}, u32[]{:S(2)}) collective-permute-start(bf16[2,1,32,1024]{3,2,1,0:T(8,128)(2,1)S(1)} %get-tuple-element.48.refs_5_), channel_id=1, source_target_pairs={{0,1},{1,2},{2,3},{3,0},{4,5},{5,6},{6,7},{7,4},{8,9},{9,10},{10,1... | collective-permute-start | bytes 393224 | tf_op jit(solution)/shard_map/ppermute | solution.py:517
  26.3 1.4 %collective-permute-start.12 = (bf16[2,1,32,1024]{3,2,1,0:T(8,128)(2,1)S(1)}, bf16[2,1,32,1024]{3,2,1,0:T(8,128)(2,1)S(1)}, u32[]{:S(2)}, u32[]{:S(2)}) collective-permute-start(bf16[2,1,32,1024]{3,2,1,0:T(8,128)(2,1)S(1)} %get-tuple-element.49.refs_6_), channel_id=1, source_target_pairs={{0,2},{1,3},{2,0},{3,1},{4,6},{5,7},{6,4},{7,5},{8,10},{9,11},{10,... | collective-permute-start | bytes 393224 | tf_op jit(solution)/shard_map/ppermute | solution.py:517
  28.8 3.5 %collective-permute-start.13 = (bf16[2,1,32,1024]{3,2,1,0:T(8,128)(2,1)S(1)}, bf16[2,1,32,1024]{3,2,1,0:T(8,128)(2,1)S(1)}, u32[]{:S(2)}, u32[]{:S(2)}) collective-permute-start(bf16[2,1,32,1024]{3,2,1,0:T(8,128)(2,1)S(1)} %get-tuple-element.50.refs_7_), channel_id=1, source_target_pairs={{0,3},{1,0},{2,1},{3,2},{4,7},{5,4},{6,5},{7,6},{8,11},{9,8},{10,9... | collective-permute-start | bytes 393224 | tf_op jit(solution)/shard_map/ppermute | solution.py:517
  33.7 1.7 %edges.1 = (bf16[2,128,1024]{2,1,0:T(8,128)(2,1)S(1)}, bf16[2,128,512]{2,1,0:T(8,128)(2,1)S(1)}, bf16[2,128,512]{2,1,0:T(8,128)(2,1)}, bf16[2,128,768]{2,1,0:T(8,128)(2,1)S(1)}) custom-call(s32[64]{0:T(128)S(1)} %plan.1, bf16[1024,256]{1,0:T(8,128)(2,1)S(1)} %copy-done.2, bf16[2,1,128,1024]{3,2,1,0:T(8,128)(2,1)S(1)} %get-tuple-element.51.old, ...), custom_call_target="tpu_custom_call" | custom-call | tf_op jit(solution)/shard_map/edges/pallas_call | solution.py:561
  35.4 3.0 %collective-permute-start.18 = (bf16[2,2,32,1024]{3,2,1,0:T(8,128)(2,1)S(1)}, bf16[2,2,32,1024]{3,2,1,0:T(8,128)(2,1)S(1)}, u32[]{:S(2)}, u32[]{:S(2)}) collective-permute-start(bf16[2,2,32,1024]{3,2,1,0:T(8,128)(2,1)S(1)} %get-tuple-element.58.refs_3_), channel_id=1, source_target_pairs={{0,3},{1,0},{2,1},{3,2},{4,7},{5,4},{6,5},{7,6},{8,11},{9,8},{10,9... | collective-permute-start | bytes 786440 | tf_op jit(solution)/shard_map/ppermute | solution.py:517
  38.4 4.1 %collective-permute-done.12.refs_2_ = bf16[2,1,32,1024]{3,2,1,0:T(8,128)(2,1)S(1)} collective-permute-done((bf16[2,1,32,1024]{3,2,1,0:T(8,128)(2,1)S(1)}, bf16[2,1,32,1024]{3,2,1,0:T(8,128)(2,1)S(1)}, u32[]{:S(2)}, u32[]{:S(2)}) %collective-permute-start.12) | collective-permute-done | bytes 131104 | tf_op jit(solution)/shard_map/ppermute | solution.py:517
  42.5 1.5 %collective-permute-done.13.refs_3_ = bf16[2,1,32,1024]{3,2,1,0:T(8,128)(2,1)S(1)} collective-permute-done((bf16[2,1,32,1024]{3,2,1,0:T(8,128)(2,1)S(1)}, bf16[2,1,32,1024]{3,2,1,0:T(8,128)(2,1)S(1)}, u32[]{:S(2)}, u32[]{:S(2)}) %collective-permute-start.13) | collective-permute-done | bytes 131104 | tf_op jit(solution)/shard_map/ppermute | solution.py:517
  44.0 2.1 %collective-permute-start.10 = (bf16[2,128,768]{2,1,0:T(8,128)(2,1)S(1)}, bf16[2,128,768]{2,1,0:T(8,128)(2,1)}, u32[]{:S(2)}, u32[]{:S(2)}) collective-permute-start(bf16[2,128,768]{2,1,0:T(8,128)(2,1)S(1)} %get-tuple-element.62.refs_6_.mine), channel_id=1, source_target_pairs={{0,28},{4,0},{8,4},{12,8},{16,12},{20,16},{24,20},{28,24},{1,29},{... | collective-permute-start | bytes 1179656 | tf_op jit(solution)/shard_map/ppermute | solution.py:499
  46.2 1.4 %shard_map.105 = (bf16[2,1,128,1024]{3,2,1,0:T(8,128)(2,1)S(1)}, bf16[1,128,1024]{2,1,0:T(8,128)(2,1)}, bf16[1,128,1024]{2,1,0:T(8,128)(2,1)}) custom-call(s32[64]{0:T(128)S(1)} %plan.1, bf16[2,1,32,1024]{3,2,1,0:T(8,128)(2,1)S(1)} %get-tuple-element.47.refs_4_.refs_0_, bf16[2,1,32,1024]{3,2,1,0:T(8,128)(2,1)S(1)} %collective-permute-done.11.refs_1_, ...), custom_call_target="tpu_custom_call" | custom-call | tf_op jit(solution)/shard_map/pallas_call | solution.py:543
  48.4 7.2 %collective-permute-done.17.refs_2_ = bf16[2,2,32,1024]{3,2,1,0:T(8,128)(2,1)S(1)} collective-permute-done((bf16[2,2,32,1024]{3,2,1,0:T(8,128)(2,1)S(1)}, bf16[2,2,32,1024]{3,2,1,0:T(8,128)(2,1)S(1)}, u32[]{:S(2)}, u32[]{:S(2)}) %collective-permute-start.17) | collective-permute-done | bytes 262176 | tf_op jit(solution)/shard_map/ppermute | solution.py:517
  56.3 3.6 %collective-permute-start.8 = (bf16[2,128,512]{2,1,0:T(8,128)(2,1)}, bf16[2,128,512]{2,1,0:T(8,128)(2,1)}, u32[]{:S(2)}, u32[]{:S(2)}) collective-permute-start(bf16[2,128,512]{2,1,0:T(8,128)(2,1)} %get-tuple-element.61.refs_5_), channel_id=1, source_target_pairs={{0,0},{1,2},{2,1},{3,3},{4,4},{5,6},{6,5},{7,7},{8,8},{9,10},{10,9... | collective-permute-start | bytes 786440 | tf_op jit(solution)/shard_map/ppermute | solution.py:525
  61.3 2.6 %collective-permute-start.15 = (bf16[1,128,1024]{2,1,0:T(8,128)(2,1)}, bf16[1,128,1024]{2,1,0:T(8,128)(2,1)}, u32[]{:S(2)}, u32[]{:S(2)}) collective-permute-start(bf16[1,128,1024]{2,1,0:T(8,128)(2,1)} %get-tuple-element.65), channel_id=1, source_target_pairs={{0,28},{4,0},{8,4},{12,8},{16,12},{20,16},{24,20},{28,24},{1,29},{... | collective-permute-start | bytes 786440 | tf_op jit(solution)/shard_map/ppermute | solution.py:499
  64.2 1.4 %copy.14 = bf16[640,512]{0,1:T(8,128)(2,1)S(1)} copy(bf16[640,512]{1,0:T(8,128)(2,1)} %param.14) | data formatting | bytes 1310720 | tf_op args[4]
  65.6 2.5 %collective-permute-done.14.old_below = bf16[1,128,1024]{2,1,0:T(8,128)(2,1)} collective-permute-done((bf16[1,128,1024]{2,1,0:T(8,128)(2,1)}, bf16[1,128,1024]{2,1,0:T(8,128)(2,1)}, u32[]{:S(2)}, u32[]{:S(2)}) %collective-permute-start.14) | collective-permute-done | bytes 262176 | tf_op jit(solution)/shard_map/ppermute | solution.py:499
  73.1 5.9 %first.1 = (bf16[384,2048]{1,0:T(8,128)(2,1)S(1)}, bf16[2,128,1024]{2,1,0:T(8,128)(2,1)S(1)}, bf16[2,128,512]{2,1,0:T(8,128)(2,1)S(1)}, bf16[2,128,512]{2,1,0:T(...) custom-call(s32[64]{0:T(128)S(1)} %plan.1, ...), custom_call_target="tpu_custom_call" | custom-call | tf_op jit(solution)/shard_map/first/pallas_call | solution.py:573
  78.9 2.9 %collective-permute-start.22 = (bf16[2,128,768]{2,1,0:T(8,128)(2,1)S(1)}, bf16[2,128,768]{2,1,0:T(8,128)(2,1)S(1)}, u32[]{:S(2)}, u32[]{:S(2)}) collective-permute-start(bf16[2,128,768]{2,1,0:T(8,128)(2,1)S(1)} %get-tuple-element.69.mine), channel_id=1, source_target_pairs={{0,28},{4,0},{8,4},{12,8},{16,12},{20,16},{24,20},{28,24},{1,29},{... | collective-permute-start | bytes 1179656 | tf_op jit(solution)/shard_map/ppermute | solution.py:499
  81.8 3.4 %collective-permute-start.19 = (bf16[2,128,512]{2,1,0:T(8,128)(2,1)S(1)}, bf16[2,128,512]{2,1,0:T(8,128)(2,1)S(1)}, u32[]{:S(2)}, u32[]{:S(2)}) collective-permute-start(bf16[2,128,512]{2,1,0:T(8,128)(2,1)S(1)} %get-tuple-element.67), channel_id=1, source_target_pairs={{0,1},{1,0},{2,3},{3,2},{4,5},{5,4},{6,7},{7,6},{8,9},{9,8},{10,11... | collective-permute-start | bytes 786440 | tf_op jit(solution)/shard_map/ppermute | solution.py:524
  85.9 4.1 %collective-permute-start.26 = (bf16[2,32,1024]{2,1,0:T(8,128)(2,1)S(1)}, bf16[2,32,1024]{2,1,0:T(8,128)(2,1)S(1)}, u32[]{:S(2)}, u32[]{:S(2)}) collective-permute-start(bf16[2,32,1024]{2,1,0:T(8,128)(2,1)S(1)} %get-tuple-element.76), channel_id=1, source_target_pairs={{0,3},{1,0},{2,1},{3,2},{4,7},{5,4},{6,5},{7,6},{8,11},{9,8},{10,9... | collective-permute-start | bytes 393224 | tf_op jit(solution)/shard_map/ppermute | solution.py:517
  90.0 2.0 %collective-permute-done.19.a_in = bf16[2,128,512]{2,1,0:T(8,128)(2,1)S(1)} collective-permute-done((bf16[2,128,512]{2,1,0:T(8,128)(2,1)S(1)}, bf16[2,128,512]{2,1,0:T(8,128)(2,1)S(1)}, u32[]{:S(2)}, u32[]{:S(2)}) %collective-permute-start.19) | collective-permute-done | bytes 262176 | tf_op jit(solution)/shard_map/ppermute | solution.py:524
  92.0 6.5 %collective-permute-start.27 = (bf16[2,32,1024]{2,1,0:T(8,128)(2,1)S(1)}, bf16[2,32,1024]{2,1,0:T(8,128)(2,1)S(1)}, u32[]{:S(2)}, u32[]{:S(2)}) collective-permute-start(bf16[2,32,1024]{2,1,0:T(8,128)(2,1)S(1)} %get-tuple-element.77), channel_id=1, source_target_pairs={{0,2},{1,3},{2,0},{3,1},{4,6},{5,7},{6,4},{7,5},{8,10},{9,11},{10,... | collective-permute-start | bytes 393224 | tf_op jit(solution)/shard_map/ppermute | solution.py:517
  98.5 5.4 %collective-permute-start.28 = (bf16[2,32,1024]{2,1,0:T(8,128)(2,1)S(1)}, bf16[2,32,1024]{2,1,0:T(8,128)(2,1)S(1)}, u32[]{:S(2)}, u32[]{:S(2)}) collective-permute-start(bf16[2,32,1024]{2,1,0:T(8,128)(2,1)S(1)} %get-tuple-element.78), channel_id=1, source_target_pairs={{0,1},{1,2},{2,3},{3,0},{4,5},{5,6},{6,7},{7,4},{8,9},{9,10},{10,1... | collective-permute-start | bytes 393224 | tf_op jit(solution)/shard_map/ppermute | solution.py:517
  104.0 4.3 %second.1 = (bf16[2,32,1024]{2,1,0:T(8,128)(2,1)S(1)}, bf16[2,32,1024]{2,1,0:T(8,128)(2,1)S(1)}, bf16[2,32,1024]{2,1,0:T(8,128)(2,1)S(1)}, bf16[2,32,1024]{2,1,0:T(8,128)(2,1)S(1)}) custom-call(s32[64]{0:T(128)S(1)} %plan.1, bf16[256,1024]{1,0:T(8,128)(2,1)S(1)} %copy-done.3, bf16[256,256]{1,0:T(8,128)(2,1)S(1)} %copy-done.6, bf16[512,640]{1,0:T(8,128)(2,1)S(1)} %bitcast.7, ...), custom_call_target="tpu_custom_call" | custom-call | tf_op jit(solution)/shard_map/second/pallas_call | solution.py:589
  108.3 3.9 %collective-permute-start.24 = (bf16[2,32,1024]{2,1,0:T(8,128)(2,1)S(1)}, bf16[2,32,1024]{2,1,0:T(8,128)(2,1)S(1)}, u32[]{:S(2)}, u32[]{:S(2)}) collective-permute-start(bf16[2,32,1024]{2,1,0:T(8,128)(2,1)S(1)} %get-tuple-element.73), channel_id=1, source_target_pairs={{0,2},{1,3},{2,0},{3,1},{4,6},{5,7},{6,4},{7,5},{8,10},{9,11},{10,... | collective-permute-start | bytes 393224 | tf_op jit(solution)/shard_map/ppermute | solution.py:517
  112.2 1.4 %shard_map.106.refs_4_ = bf16[2,2,32,4096]{3,2,1,0:T(8,128)(2,1)} custom-call(s32[64]{0:T(128)S(1)} %plan.1, bf16[2,32,1024]{2,1,0:T(8,128)(2,1)S(1)} %get-tuple-element.75.refs_0_, bf16[2,32,1024]{2,1,0:T(8,128)(2,1)S(1)} %collective-permute-done.26.refs_1_, bf16[2,32,1024]{2,1,0:T(8,128)(2,1)S(1)} %collective-permute-done.27.refs_2_, ...), custom_call_target="tpu_custom_call" | custom-call | tf_op jit(solution)/shard_map/pallas_call | solution.py:600
  113.7 9.1 %collective-permute-done.24.refs_2_ = bf16[2,32,1024]{2,1,0:T(8,128)(2,1)S(1)} collective-permute-done((bf16[2,32,1024]{2,1,0:T(8,128)(2,1)S(1)}, bf16[2,32,1024]{2,1,0:T(8,128)(2,1)S(1)}, u32[]{:S(2)}, u32[]{:S(2)}) %collective-permute-start.24) | collective-permute-done | bytes 131104 | tf_op jit(solution)/shard_map/ppermute | solution.py:517
  (82 shorter events, 17.9 us)
Async XLA Ops:
  4.3 22.0 %collective-permute-start.6 = (bf16[2,32,4096]{2,1,0:T(8,128)(2,1)S(1)}, bf16[2,32,4096]{2,1,0:T(8,128)(2,1)S(1)}, u32[]{:S(2)}, u32[]{:S(2)}) collective-permute-start(bf16[2,32,4096]{2,1,0:T(8,128)(2,1)S(1)} %get-tuple-element.54), channel_id=1, source_target_pairs={{0,28},{4,0},{8,4},{12,8},{16,12},{20,16},{24,20},{28,24},{1,29},{... | collective-permute-start | bytes 1572872 | tf_op jit(solution)/shard_map/ppermute | solution.py:499
  7.7 20.0 %collective-permute-start.5 = (bf16[2,32,4096]{2,1,0:T(8,128)(2,1)S(1)}, bf16[2,32,4096]{2,1,0:T(8,128)(2,1)S(1)}, u32[]{:S(2)}, u32[]{:S(2)}) collective-permute-start(bf16[2,32,4096]{2,1,0:T(8,128)(2,1)S(1)} %get-tuple-element.46.refs_1_), channel_id=1, source_target_pairs={{0,4},{4,8},{8,12},{12,16},{16,20},{20,24},{24,28},{28,0},{1,5},{5... | collective-permute-start | bytes 1572872 | tf_op jit(solution)/shard_map/ppermute | solution.py:499
  7.7 8.3 %collective-permute-start = (bf16[2,1,32,1024]{3,2,1,0:T(8,128)(2,1)S(1)}, bf16[2,1,32,1024]{3,2,1,0:T(8,128)(2,1)S(1)}, u32[]{:S(2)}, u32[]{:S(2)}) collective-permute-start(bf16[2,1,32,1024]{3,2,1,0:T(8,128)(2,1)S(1)} %get-tuple-element.43.refs_1_), channel_id=1, source_target_pairs={{0,1},{1,2},{2,3},{3,0},{4,5},{5,6},{6,7},{7,4},{8,9},{9,10},{10,1... | collective-permute-start | bytes 393224 | tf_op jit(solution)/shard_map/ppermute | solution.py:517
  9.3 11.2 %collective-permute-start.1 = (bf16[2,1,32,1024]{3,2,1,0:T(8,128)(2,1)S(1)}, bf16[2,1,32,1024]{3,2,1,0:T(8,128)(2,1)S(1)}, u32[]{:S(2)}, u32[]{:S(2)}) collective-permute-start(bf16[2,1,32,1024]{3,2,1,0:T(8,128)(2,1)S(1)} %get-tuple-element.44.refs_2_), channel_id=1, source_target_pairs={{0,2},{1,3},{2,0},{3,1},{4,6},{5,7},{6,4},{7,5},{8,10},{9,11},{10,... | collective-permute-start | bytes 393224 | tf_op jit(solution)/shard_map/ppermute | solution.py:517
  11.9 8.6 %collective-permute-start.2 = (bf16[2,1,32,1024]{3,2,1,0:T(8,128)(2,1)S(1)}, bf16[2,1,32,1024]{3,2,1,0:T(8,128)(2,1)S(1)}, u32[]{:S(2)}, u32[]{:S(2)}) collective-permute-start(bf16[2,1,32,1024]{3,2,1,0:T(8,128)(2,1)S(1)} %get-tuple-element.45.refs_3_), channel_id=1, source_target_pairs={{0,3},{1,0},{2,1},{3,2},{4,7},{5,4},{6,5},{7,6},{8,11},{9,8},{10,9... | collective-permute-start | bytes 393224 | tf_op jit(solution)/shard_map/ppermute | solution.py:517
  21.1 7.7 %collective-permute-start.4 = (bf16[1,128,1024]{2,1,0:T(8,128)(2,1)S(1)}, bf16[1,128,1024]{2,1,0:T(8,128)(2,1)S(1)}, u32[]{:S(2)}, u32[]{:S(2)}) collective-permute-start(bf16[1,128,1024]{2,1,0:T(8,128)(2,1)S(1)} %get-tuple-element.53), channel_id=1, source_target_pairs={{0,28},{4,0},{8,4},{12,8},{16,12},{20,16},{24,20},{28,24},{1,29},{... | collective-permute-start | bytes 786440 | tf_op jit(solution)/shard_map/ppermute | solution.py:499
  23.0 9.4 %collective-permute-start.3 = (bf16[1,128,1024]{2,1,0:T(8,128)(2,1)S(1)}, bf16[1,128,1024]{2,1,0:T(8,128)(2,1)S(1)}, u32[]{:S(2)}, u32[]{:S(2)}) collective-permute-start(bf16[1,128,1024]{2,1,0:T(8,128)(2,1)S(1)} %get-tuple-element.52.refs_2_), channel_id=1, source_target_pairs={{0,4},{4,8},{8,12},{12,16},{16,20},{20,24},{24,28},{28,0},{1,5},{5... | collective-permute-start | bytes 786440 | tf_op jit(solution)/shard_map/ppermute | solution.py:499
  23.0 12.5 %collective-permute-start.11 = (bf16[2,1,32,1024]{3,2,1,0:T(8,128)(2,1)S(1)}, bf16[2,1,32,1024]{3,2,1,0:T(8,128)(2,1)S(1)}, u32[]{:S(2)}, u32[]{:S(2)}) collective-permute-start(bf16[2,1,32,1024]{3,2,1,0:T(8,128)(2,1)S(1)} %get-tuple-element.48.refs_5_), channel_id=1, source_target_pairs={{0,1},{1,2},{2,3},{3,0},{4,5},{5,6},{6,7},{7,4},{8,9},{9,10},{10,1... | collective-permute-start | bytes 393224 | tf_op jit(solution)/shard_map/ppermute | solution.py:517
  26.3 16.2 %collective-permute-start.12 = (bf16[2,1,32,1024]{3,2,1,0:T(8,128)(2,1)S(1)}, bf16[2,1,32,1024]{3,2,1,0:T(8,128)(2,1)S(1)}, u32[]{:S(2)}, u32[]{:S(2)}) collective-permute-start(bf16[2,1,32,1024]{3,2,1,0:T(8,128)(2,1)S(1)} %get-tuple-element.49.refs_6_), channel_id=1, source_target_pairs={{0,2},{1,3},{2,0},{3,1},{4,6},{5,7},{6,4},{7,5},{8,10},{9,11},{10,... | collective-permute-start | bytes 393224 | tf_op jit(solution)/shard_map/ppermute | solution.py:517
  28.5 35.5 %copy-start.18 = (bf16[512,128]{1,0:T(8,128)(2,1)S(1)}, bf16[512,128]{1,0:T(8,128)(2,1)}, u32[]{:S(2)}) copy-start(bf16[512,128]{1,0:T(8,128)(2,1)} %param.16) | copy-start | bytes 393220
  28.5 17.7 %collective-permute-start.16 = (bf16[2,2,32,1024]{3,2,1,0:T(8,128)(2,1)S(1)}, bf16[2,2,32,1024]{3,2,1,0:T(8,128)(2,1)S(1)}, u32[]{:S(2)}, u32[]{:S(2)}) collective-permute-start(bf16[2,2,32,1024]{3,2,1,0:T(8,128)(2,1)S(1)} %get-tuple-element.56.refs_1_), channel_id=1, source_target_pairs={{0,1},{1,2},{2,3},{3,0},{4,5},{5,6},{6,7},{7,4},{8,9},{9,10},{10,1... | collective-permute-start | bytes 786440 | tf_op jit(solution)/shard_map/ppermute | solution.py:517
  28.8 15.2 %collective-permute-start.13 = (bf16[2,1,32,1024]{3,2,1,0:T(8,128)(2,1)S(1)}, bf16[2,1,32,1024]{3,2,1,0:T(8,128)(2,1)S(1)}, u32[]{:S(2)}, u32[]{:S(2)}) collective-permute-start(bf16[2,1,32,1024]{3,2,1,0:T(8,128)(2,1)S(1)} %get-tuple-element.50.refs_7_), channel_id=1, source_target_pairs={{0,3},{1,0},{2,1},{3,2},{4,7},{5,4},{6,5},{7,6},{8,11},{9,8},{10,9... | collective-permute-start | bytes 393224 | tf_op jit(solution)/shard_map/ppermute | solution.py:517
  32.4 23.2 %collective-permute-start.17 = (bf16[2,2,32,1024]{3,2,1,0:T(8,128)(2,1)S(1)}, bf16[2,2,32,1024]{3,2,1,0:T(8,128)(2,1)S(1)}, u32[]{:S(2)}, u32[]{:S(2)}) collective-permute-start(bf16[2,2,32,1024]{3,2,1,0:T(8,128)(2,1)S(1)} %get-tuple-element.57.refs_2_), channel_id=1, source_target_pairs={{0,2},{1,3},{2,0},{3,1},{4,6},{5,7},{6,4},{7,5},{8,10},{9,11},{10,... | collective-permute-start | bytes 786440 | tf_op jit(solution)/shard_map/ppermute | solution.py:517
  35.4 32.8 %copy-start.3 = (bf16[256,1024]{1,0:T(8,128)(2,1)S(1)}, bf16[256,1024]{1,0:T(8,128)(2,1)}, u32[]{:S(2)}) copy-start(bf16[256,1024]{1,0:T(8,128)(2,1)} %constant.16.clone.put) | copy-start | bytes 1572868
  35.4 32.8 %copy-start.6 = (bf16[256,256]{1,0:T(8,128)(2,1)S(1)}, bf16[256,256]{1,0:T(8,128)(2,1)}, u32[]{:S(2)}) copy-start(bf16[256,256]{1,0:T(8,128)(2,1)} %constant.17.clone.flat) | copy-start | bytes 393220
  35.4 24.5 %collective-permute-start.18 = (bf16[2,2,32,1024]{3,2,1,0:T(8,128)(2,1)S(1)}, bf16[2,2,32,1024]{3,2,1,0:T(8,128)(2,1)S(1)}, u32[]{:S(2)}, u32[]{:S(2)}) collective-permute-start(bf16[2,2,32,1024]{3,2,1,0:T(8,128)(2,1)S(1)} %get-tuple-element.58.refs_3_), channel_id=1, source_target_pairs={{0,3},{1,0},{2,1},{3,2},{4,7},{5,4},{6,5},{7,6},{8,11},{9,8},{10,9... | collective-permute-start | bytes 786440 | tf_op jit(solution)/shard_map/ppermute | solution.py:517
  42.5 18.1 %collective-permute-start.7 = (bf16[2,128,512]{2,1,0:T(8,128)(2,1)S(1)}, bf16[2,128,512]{2,1,0:T(8,128)(2,1)S(1)}, u32[]{:S(2)}, u32[]{:S(2)}) collective-permute-start(bf16[2,128,512]{2,1,0:T(8,128)(2,1)S(1)} %get-tuple-element.60.refs_4_), channel_id=1, source_target_pairs={{0,1},{1,0},{2,3},{3,2},{4,5},{5,4},{6,7},{7,6},{8,9},{9,8},{10,11... | collective-permute-start | bytes 786440 | tf_op jit(solution)/shard_map/ppermute | solution.py:524
  44.0 24.2 %collective-permute-start.10 = (bf16[2,128,768]{2,1,0:T(8,128)(2,1)S(1)}, bf16[2,128,768]{2,1,0:T(8,128)(2,1)}, u32[]{:S(2)}, u32[]{:S(2)}) collective-permute-start(bf16[2,128,768]{2,1,0:T(8,128)(2,1)S(1)} %get-tuple-element.62.refs_6_.mine), channel_id=1, source_target_pairs={{0,28},{4,0},{8,4},{12,8},{16,12},{20,16},{24,20},{28,24},{1,29},{... | collective-permute-start | bytes 1179656 | tf_op jit(solution)/shard_map/ppermute | solution.py:499
  46.1 22.1 %collective-permute-start.9 = (bf16[2,128,768]{2,1,0:T(8,128)(2,1)S(1)}, bf16[2,128,768]{2,1,0:T(8,128)(2,1)}, u32[]{:S(2)}, u32[]{:S(2)}) collective-permute-start(bf16[2,128,768]{2,1,0:T(8,128)(2,1)S(1)} %get-tuple-element.62.refs_6_.mine), channel_id=1, source_target_pairs={{0,4},{4,8},{8,12},{12,16},{16,20},{20,24},{24,28},{28,0},{1,5},{5... | collective-permute-start | bytes 1179656 | tf_op jit(solution)/shard_map/ppermute | solution.py:499
  56.3 9.3 %collective-permute-start.8 = (bf16[2,128,512]{2,1,0:T(8,128)(2,1)}, bf16[2,128,512]{2,1,0:T(8,128)(2,1)}, u32[]{:S(2)}, u32[]{:S(2)}) collective-permute-start(bf16[2,128,512]{2,1,0:T(8,128)(2,1)} %get-tuple-element.61.refs_5_), channel_id=1, source_target_pairs={{0,0},{1,2},{2,1},{3,3},{4,4},{5,6},{6,5},{7,7},{8,8},{9,10},{10,9... | collective-permute-start | bytes 786440 | tf_op jit(solution)/shard_map/ppermute | solution.py:525
  60.6 7.5 %collective-permute-start.14 = (bf16[1,128,1024]{2,1,0:T(8,128)(2,1)}, bf16[1,128,1024]{2,1,0:T(8,128)(2,1)}, u32[]{:S(2)}, u32[]{:S(2)}) collective-permute-start(bf16[1,128,1024]{2,1,0:T(8,128)(2,1)} %get-tuple-element.64), channel_id=1, source_target_pairs={{0,4},{4,8},{8,12},{12,16},{16,20},{20,24},{24,28},{28,0},{1,5},{5... | collective-permute-start | bytes 786440 | tf_op jit(solution)/shard_map/ppermute | solution.py:499
  61.3 6.9 %collective-permute-start.15 = (bf16[1,128,1024]{2,1,0:T(8,128)(2,1)}, bf16[1,128,1024]{2,1,0:T(8,128)(2,1)}, u32[]{:S(2)}, u32[]{:S(2)}) collective-permute-start(bf16[1,128,1024]{2,1,0:T(8,128)(2,1)} %get-tuple-element.65), channel_id=1, source_target_pairs={{0,28},{4,0},{8,4},{12,8},{16,12},{20,16},{24,20},{28,24},{1,29},{... | collective-permute-start | bytes 786440 | tf_op jit(solution)/shard_map/ppermute | solution.py:499
  78.9 25.0 %collective-permute-start.22 = (bf16[2,128,768]{2,1,0:T(8,128)(2,1)S(1)}, bf16[2,128,768]{2,1,0:T(8,128)(2,1)S(1)}, u32[]{:S(2)}, u32[]{:S(2)}) collective-permute-start(bf16[2,128,768]{2,1,0:T(8,128)(2,1)S(1)} %get-tuple-element.69.mine), channel_id=1, source_target_pairs={{0,28},{4,0},{8,4},{12,8},{16,12},{20,16},{24,20},{28,24},{1,29},{... | collective-permute-start | bytes 1179656 | tf_op jit(solution)/shard_map/ppermute | solution.py:499
  81.8 22.2 %collective-permute-start.21 = (bf16[2,128,768]{2,1,0:T(8,128)(2,1)S(1)}, bf16[2,128,768]{2,1,0:T(8,128)(2,1)S(1)}, u32[]{:S(2)}, u32[]{:S(2)}) collective-permute-start(bf16[2,128,768]{2,1,0:T(8,128)(2,1)S(1)} %get-tuple-element.69.mine), channel_id=1, source_target_pairs={{0,4},{4,8},{8,12},{12,16},{16,20},{20,24},{24,28},{28,0},{1,5},{5... | collective-permute-start | bytes 1179656 | tf_op jit(solution)/shard_map/ppermute | solution.py:499
  81.8 10.2 %collective-permute-start.19 = (bf16[2,128,512]{2,1,0:T(8,128)(2,1)S(1)}, bf16[2,128,512]{2,1,0:T(8,128)(2,1)S(1)}, u32[]{:S(2)}, u32[]{:S(2)}) collective-permute-start(bf16[2,128,512]{2,1,0:T(8,128)(2,1)S(1)} %get-tuple-element.67), channel_id=1, source_target_pairs={{0,1},{1,0},{2,3},{3,2},{4,5},{5,4},{6,7},{7,6},{8,9},{9,8},{10,11... | collective-permute-start | bytes 786440 | tf_op jit(solution)/shard_map/ppermute | solution.py:524
  85.2 13.3 %collective-permute-start.20 = (bf16[2,128,512]{2,1,0:T(8,128)(2,1)S(1)}, bf16[2,128,512]{2,1,0:T(8,128)(2,1)S(1)}, u32[]{:S(2)}, u32[]{:S(2)}) collective-permute-start(bf16[2,128,512]{2,1,0:T(8,128)(2,1)S(1)} %get-tuple-element.68), channel_id=1, source_target_pairs={{0,0},{1,2},{2,1},{3,3},{4,4},{5,6},{6,5},{7,7},{8,8},{9,10},{10,9... | collective-permute-start | bytes 786440 | tf_op jit(solution)/shard_map/ppermute | solution.py:525
  85.9 26.3 %collective-permute-start.26 = (bf16[2,32,1024]{2,1,0:T(8,128)(2,1)S(1)}, bf16[2,32,1024]{2,1,0:T(8,128)(2,1)S(1)}, u32[]{:S(2)}, u32[]{:S(2)}) collective-permute-start(bf16[2,32,1024]{2,1,0:T(8,128)(2,1)S(1)} %get-tuple-element.76), channel_id=1, source_target_pairs={{0,3},{1,0},{2,1},{3,2},{4,7},{5,4},{6,5},{7,6},{8,11},{9,8},{10,9... | collective-permute-start | bytes 393224 | tf_op jit(solution)/shard_map/ppermute | solution.py:517
  92.0 20.2 %collective-permute-start.27 = (bf16[2,32,1024]{2,1,0:T(8,128)(2,1)S(1)}, bf16[2,32,1024]{2,1,0:T(8,128)(2,1)S(1)}, u32[]{:S(2)}, u32[]{:S(2)}) collective-permute-start(bf16[2,32,1024]{2,1,0:T(8,128)(2,1)S(1)} %get-tuple-element.77), channel_id=1, source_target_pairs={{0,2},{1,3},{2,0},{3,1},{4,6},{5,7},{6,4},{7,5},{8,10},{9,11},{10,... | collective-permute-start | bytes 393224 | tf_op jit(solution)/shard_map/ppermute | solution.py:517
  98.5 13.7 %collective-permute-start.28 = (bf16[2,32,1024]{2,1,0:T(8,128)(2,1)S(1)}, bf16[2,32,1024]{2,1,0:T(8,128)(2,1)S(1)}, u32[]{:S(2)}, u32[]{:S(2)}) collective-permute-start(bf16[2,32,1024]{2,1,0:T(8,128)(2,1)S(1)} %get-tuple-element.78), channel_id=1, source_target_pairs={{0,1},{1,2},{2,3},{3,0},{4,5},{5,6},{6,7},{7,4},{8,9},{9,10},{10,1... | collective-permute-start | bytes 393224 | tf_op jit(solution)/shard_map/ppermute | solution.py:517
  108.2 5.5 %collective-permute-start.23 = (bf16[2,32,1024]{2,1,0:T(8,128)(2,1)S(1)}, bf16[2,32,1024]{2,1,0:T(8,128)(2,1)S(1)}, u32[]{:S(2)}, u32[]{:S(2)}) collective-permute-start(bf16[2,32,1024]{2,1,0:T(8,128)(2,1)S(1)} %get-tuple-element.72), channel_id=1, source_target_pairs={{0,3},{1,0},{2,1},{3,2},{4,7},{5,4},{6,5},{7,6},{8,11},{9,8},{10,9... | collective-permute-start | bytes 393224 | tf_op jit(solution)/shard_map/ppermute | solution.py:517
  108.3 14.5 %collective-permute-start.24 = (bf16[2,32,1024]{2,1,0:T(8,128)(2,1)S(1)}, bf16[2,32,1024]{2,1,0:T(8,128)(2,1)S(1)}, u32[]{:S(2)}, u32[]{:S(2)}) collective-permute-start(bf16[2,32,1024]{2,1,0:T(8,128)(2,1)S(1)} %get-tuple-element.73), channel_id=1, source_target_pairs={{0,2},{1,3},{2,0},{3,1},{4,6},{5,7},{6,4},{7,5},{8,10},{9,11},{10,... | collective-permute-start | bytes 393224 | tf_op jit(solution)/shard_map/ppermute | solution.py:517
  112.2 10.5 %collective-permute-start.25 = (bf16[2,32,1024]{2,1,0:T(8,128)(2,1)S(1)}, bf16[2,32,1024]{2,1,0:T(8,128)(2,1)S(1)}, u32[]{:S(2)}, u32[]{:S(2)}) collective-permute-start(bf16[2,32,1024]{2,1,0:T(8,128)(2,1)S(1)} %get-tuple-element.74), channel_id=1, source_target_pairs={{0,1},{1,2},{2,3},{3,0},{4,5},{5,6},{6,7},{7,4},{8,9},{9,10},{10,1... | collective-permute-start | bytes 393224 | tf_op jit(solution)/shard_map/ppermute | solution.py:517
  (17 other events, 74.4 us)

commit v2 on v1

--- a/solution.py
+++ b/solution.py
@@ -259,15 +259,16 @@
 
 
 def pack_kernel(size, states, plan, below, above, *refs):
-    outs = refs[-size:]
-    for t in range(states):
-        for j in range(refs[t].shape[0]):
+    per_dev = refs[0].shape[0]
+    outs = refs[-size * per_dev :]
+    for j in range(per_dev):
+        for t in range(states):
 
             def store(source):
                 for k in range(1, size + 1):
                     k = k % size
                     for here, there in slab_lanes(lax.rem(plan[1] + k, size), size):
-                        outs[k][j, t, :, here] = source[0, :, there]
+                        outs[j * size + k][t, :, here] = source[0, :, there]
 
             settle(plan, j, refs[t], below.at[pl.ds(t, 1)], above.at[pl.ds(t, 1)], store)
 
@@ -318,94 +319,105 @@
 
 
 def laplacian(plan, slab, a_in, b_in, mine, below, above, put, flat, spread, first_row):
-    f32 = jnp.float32
+    f32, bf16 = jnp.float32, jnp.bfloat16
     grp = plan[1]
     per_dev, channels = slab.shape[0], slab.shape[1]
-    even = lax.rem(grp, 2) == 0
-    lowest, highest = grp == 0, grp == 3
+    odd = lax.rem(grp, 2)
+    lowest, highest = (grp == 0).astype(jnp.int32), (grp == 3).astype(jnp.int32)
+
+    def weight(chosen):
+        return jnp.full((16, PLANE), chosen, jnp.int32).astype(f32).astype(bf16)
+
+    def scaled(value, chosen):
+        rows = value.shape[0]
+        return (value.reshape(rows // 16, 16, PLANE) * chosen[None]).reshape(rows, PLANE)
+
+    inner_a, inner_b, inner_own = weight(1 - odd), weight(odd - highest), weight(highest)
+    outer_a, outer_b = weight(odd), weight(1 - odd - lowest)
     cands = [ref.at[s] for ref in (below, mine, above) for s in range(per_dev)]
-    face_of_lane = lax.broadcasted_iota(jnp.int32, (channels, PLANE), 1) // 64
+    face_of_lane = lax.broadcasted_iota(jnp.int32, (16, PLANE), 1) // 64
+    low, high = slice(0, PLANE), slice(PLANE, HALF)
     for j in range(per_dev):
         layer = [slab[j, :, i * PLANE : (i + 1) * PLANE] for i in range(4)]
-        wide = [x.astype(f32) for x in layer]
-        a, b = a_in[j].astype(f32), b_in[j].astype(f32)
-        inner = jnp.where(even, a, b)
-        outer = jnp.where(even, b, a)
-        inner0 = jnp.where(highest, wide[2], inner[:, :PLANE])
-        inner1 = jnp.where(highest, wide[1], inner[:, PLANE:])
+        a, b = a_in[j], b_in[j]
+        inner0 = scaled(a[:, low], inner_a) + scaled(b[:, low], inner_b) + scaled(layer[2], inner_own)
+        inner1 = scaled(a[:, high], inner_a) + scaled(b[:, high], inner_b) + scaled(layer[1], inner_own)
+        outer0 = scaled(a[:, low], outer_a) + scaled(b[:, low], outer_b)
+        outer1 = scaled(a[:, high], outer_a) + scaled(b[:, high], outer_b)
         code = [plan[8 + 6 * j + f] for f in range(6)]
         lane_code = jnp.where(
             face_of_lane < 2,
             jnp.where(face_of_lane == 0, code[2], code[3]),
             jnp.where(face_of_lane == 2, code[4], code[5]),
         )
-        face0 = jnp.zeros((channels, PLANE), f32)
-        face1 = jnp.zeros((channels, PLANE), f32)
-        rest = jnp.zeros((channels, PLANE), f32)
+        rest = jnp.zeros((channels, PLANE), bf16)
         for c, cand in enumerate(cands):
-            face0 = jnp.where(code[0] == c, cand[:, HALF:FACE_LANES].astype(f32), face0)
-            face1 = jnp.where(code[1] == c, cand[:, PLANE:HALF].astype(f32), face1)
-            rest = jnp.where(lane_code == c, cand[:, 0:PLANE].astype(f32), rest)
-        outer0 = jnp.where(lowest, face0, outer[:, :PLANE])
-        outer1 = jnp.where(lowest, face1, outer[:, PLANE:])
-        placed = jnp.dot(rest.astype(jnp.bfloat16), put[...], preferred_element_type=f32)
-        sides = (
-            (outer0, wide[1]),
-            (wide[0], inner0),
-            (inner1, wide[3]),
-            (wide[2], outer1),
-        )
+            outer0 = outer0 + scaled(cand[:, HALF:FACE_LANES], weight(jnp.where(code[0] == c, lowest, 0)))
+            outer1 = outer1 + scaled(cand[:, PLANE:HALF], weight(jnp.where(code[1] == c, lowest, 0)))
+            rest = rest + scaled(cand[:, low], jnp.where(lane_code == c, 1.0, 0.0).astype(bf16))
+        placed = jnp.dot(rest, put[...], preferred_element_type=f32)
+        sides = ((outer0, layer[1]), (layer[0], inner0), (inner1, layer[3]), (layer[2], outer1))
         for i in range(4):
             total = jnp.dot(layer[i], flat[...], preferred_element_type=f32)
-            total = total + placed[:, i * PLANE : (i + 1) * PLANE] + sides[i][0] + sides[i][1]
+            total = total + placed[:, i * PLANE : (i + 1) * PLANE]
+            total = total + sides[i][0].astype(f32) + sides[i][1].astype(f32)
             spread[first_row : first_row + channels, j * SLAB + i * PLANE : j * SLAB + (i + 1) * PLANE] = (
-                total.astype(jnp.bfloat16)
+                total.astype(bf16)
             )
 
 
 TILE = 512
 
 
-def network(plan, inputs, slab, w_in, bias, w_out, state):
-    per_dev = slab.shape[0]
-    per_slab = SLAB // TILE
-    steps = [1.0 - 0.5 * plan[6 + j].astype(jnp.float32) for j in range(per_dev)]
-    for j in range(per_dev):
-        for n in range(per_slab):
-            lanes = slice(j * SLAB + n * TILE, j * SLAB + (n + 1) * TILE)
-            pre = jnp.dot(w_in[...], inputs[:, lanes], preferred_element_type=jnp.float32) + bias[...]
-            half = 0.5 * pre
-            hidden = (half + half * jnp.tanh(half)).astype(jnp.bfloat16)
-            update = jnp.dot(w_out[...], hidden, preferred_element_type=jnp.float32)
-            update = update.astype(jnp.bfloat16).astype(jnp.float32)
-            here = slice(n * TILE, (n + 1) * TILE)
-            state[j, :, here] = (slab[j, :, here].astype(jnp.float32) + steps[j] * update).astype(
-                jnp.bfloat16
-            )
-
-
-def emit_back(plan, state, backs):
+def network(plan, j, inputs, slab, w_in, bias, w_out, state):
+    step = 1.0 - 0.5 * plan[6 + j].astype(jnp.float32)
+    for n in range(SLAB // TILE):
+        lanes = slice(j * SLAB + n * TILE, j * SLAB + (n + 1) * TILE)
+        shift = jnp.concatenate([bias[...]] * (TILE // bias.shape[1]), 1)
+        pre = jnp.dot(w_in[...], inputs[:, lanes], preferred_element_type=jnp.float32) + shift
+        half = 0.5 * pre
+        hidden = (half + half * jnp.tanh(half)).astype(jnp.bfloat16)
+        update = jnp.dot(w_out[...], hidden, preferred_element_type=jnp.float32)
+        update = update.astype(jnp.bfloat16).astype(jnp.float32)
+        here = slice(n * TILE, (n + 1) * TILE)
+        state[j, :, here] = (slab[j, :, here].astype(jnp.float32) + step * update).astype(jnp.bfloat16)
+
+
+def weights_kernel(w_in, bias, w_out, w_first, w_second, w_out_t, bias_t):
+    channels = w_out.shape[1]
+    turned = w_in[...].astype(jnp.float32).T.astype(jnp.bfloat16)
+    older = (HIST - 1) * channels
+    w_first[...] = turned
+    w_second[:, 0:older] = turned[:, channels : HIST * channels]
+    w_second[:, older : HIST * channels] = turned[:, 0:channels]
+    w_second[:, HIST * channels :] = turned[:, HIST * channels :]
+    w_out_t[...] = w_out[...].astype(jnp.float32).T.astype(jnp.bfloat16)
+    for r in range(bias.shape[0]):
+        bias_t[r * 128 : (r + 1) * 128, :] = jnp.broadcast_to(bias[r : r + 1, :], (128, 128)).T
+
+
+def emit_back(plan, state, j, backs):
     grp, size = plan[1], len(backs)
-    width = backs[0].shape[1]
+    width = backs[0].shape[0]
     for k in range(size):
-        rows = pl.ds(pl.multiple_of(lax.rem(grp - k + size, size) * width, width), width)
-        for j in range(state.shape[0]):
-            backs[k][j] = state[j, rows, :]
-
-
-def first_kernel(size, plan, lay, put, flat, w_in, bias, w_out, slab, a_in, b_in, mine, below, above, old, old_below, old_above, *refs):
-    pieces = refs[:size]
-    kept, state, a_out, b_out, f_out = refs[size : size + 5]
-    backs = refs[size + 5 : 2 * size + 5]
-    inputs = refs[2 * size + 5]
+        backs[k][...] = state[j, channel_rows(grp, k, size, width), :]
+
+
+def fill_late(plan, j, pieces, inputs, first):
+    size, width = len(pieces), pieces[0].shape[1]
+    channels = size * width
+    for k in range(size):
+        for t in range(pieces[k].shape[0]):
+            rows = channel_rows(plan[1], k, size, width, (first + t) * channels)
+            inputs[rows, j * SLAB : (j + 1) * SLAB] = pieces[k][t]
+
+
+def first_kernel(size, plan, put, flat, w_in, bias, w_out, slab, a_in, b_in, mine, below, above, old, old_below, old_above, *refs):
+    pieces, (inputs, state), backs = refs[:size], refs[size : size + 2], refs[size + 2 :]
     per_dev, channels = slab.shape[0], slab.shape[1]
-    width, early = pieces[0].shape[2], old.shape[1]
+    early = old.shape[1]
     for j in range(per_dev):
         lanes = slice(j * SLAB, (j + 1) * SLAB)
-        for k in range(size):
-            for t in range(pieces[k].shape[1]):
-                rows = channel_rows(plan[1], k, size, width, (1 + early + t) * channels)
-                inputs[rows, lanes] = pieces[k][j, t]
         inputs[0:channels, lanes] = slab[j]
 
         def store(source):
@@ -413,23 +425,39 @@
                 inputs[(1 + t) * channels : (2 + t) * channels, lanes] = source[t]
 
         settle(plan, j, old, old_below, old_above, store)
+    fill_late(plan, 0, pieces, inputs, 1 + early)
     laplacian(plan, slab, a_in, b_in, mine, below, above, put, flat, inputs, HIST * channels)
-    network(plan, inputs, slab, w_in, bias, w_out, state)
+    network(plan, 0, inputs, slab, w_in, bias, w_out, state)
+    emit_back(plan, state, 0, backs)
+
+
+def rest_kernel(size, early, plan, lay, w_in, bias, w_out, slab, ready, passed, *refs):
+    pieces = refs[:size]
+    inputs, state, a_out, b_out, f_out = refs[size : size + 5]
+    backs = refs[size + 5 :]
+    per_dev = slab.shape[0]
+    for j in range(1, per_dev):
+        fill_late(plan, j, pieces[(j - 1) * size : j * size], inputs, 1 + early)
+    state[0] = ready[0]
+    for j in range(1, per_dev):
+        network(plan, j, inputs, slab, w_in, bias, w_out, state)
+        emit_back(plan, state, j, backs[(j - 1) * size : j * size])
     emit_edges(plan, state, lay, a_out, b_out, f_out)
-    emit_back(plan, state, backs)
-    kept[...] = inputs[0 : (HIST - 1) * channels, :]
-
-
-def second_kernel(size, plan, put, flat, w_in, bias, w_out, slab, a_in, b_in, mine, below, above, kept, *refs):
+
+
+def second_kernel(size, plan, put, flat, w_in, bias, w_out, slab, a_in, b_in, mine, below, above, passed, *refs):
     backs = refs[:size]
-    state, inputs = refs[size : size + 2]
+    inputs, state = refs[size:]
     per_dev, channels = slab.shape[0], slab.shape[1]
-    inputs[channels : HIST * channels, :] = kept[...]
     for j in range(per_dev):
-        inputs[0:channels, j * SLAB : (j + 1) * SLAB] = slab[j]
+        inputs[(HIST - 1) * channels : HIST * channels, j * SLAB : (j + 1) * SLAB] = slab[j]
     laplacian(plan, slab, a_in, b_in, mine, below, above, put, flat, inputs, HIST * channels)
-    network(plan, inputs, slab, w_in, bias, w_out, state)
-    emit_back(plan, state, backs)
+    for j in range(per_dev):
+        network(plan, j, inputs, slab, w_in, bias, w_out, state)
+    for k in range(size):
+        rows = channel_rows(plan[1], k, size, backs[k].shape[1])
+        for j in range(per_dev):
+            backs[k][j] = state[j, rows, :]
 
 
 def finish_kernel(size, plan, *refs):
@@ -437,7 +465,7 @@
     for k in range(size):
         for here, there in slab_lanes(lax.rem(plan[1] + k, size), size):
             for j in range(out.shape[0]):
-                out[j, 0, :, there] = refs[k][j, :, here]
+                out[j, 0, :, there] = refs[k][j, :, here] if len(refs[k].shape) == 3 else refs[j * size + k][:, here]
 
 
 def local_folded(history, face_patch, refined, dest_slot, w_in, in_bias, w_out):
@@ -445,6 +473,7 @@
     per_dev, hist, width, cells = history.shape
     size = lax.axis_size("grp")
     channels = width * size
+    hidden = w_in.shape[1]
     doms = lax.axis_size("dom")
     smem = pl.BlockSpec(memory_space=SMEM)
     anywhere = pl.BlockSpec(memory_space=pl.ANY)
@@ -499,15 +528,15 @@
         return lax.ppermute(up, "dom", up_ring), lax.ppermute(down, "dom", down_ring)
 
     def pack(first, states, below, above, *after):
-        block = (per_dev, states, width, SLAB)
+        block = (states, width, SLAB)
         return pl.pallas_call(
             functools.partial(pack_kernel, size, states),
             grid=(1,),
-            out_shape=[shape(block, bf16)] * size,
+            out_shape=[shape(block, bf16)] * (size * per_dev),
             in_specs=[smem] + vmem_specs(2)
             + [state_block(first + t) for t in range(states)]
             + [anywhere] * len(after),
-            out_specs=vmem_specs(size),
+            out_specs=vmem_specs(size * per_dev),
             compiler_params=grant(SMALL),
         )(plan, below, above, *([history] * states), *after)
 
@@ -527,8 +556,15 @@
         return a_in, b_in, f_out, below, above
 
     lay, put, flat = (jnp.asarray(table, bf16) for table in face_tables())
-    w_in_t, w_out_t = w_in.T, w_out.T
-    bias = in_bias[:, None]
+    w_first, w_second, w_out_t, bias = pl.pallas_call(
+        weights_kernel,
+        out_shape=[shape((hidden, (hist + 1) * channels), bf16)] * 2
+        + [shape((channels, hidden), bf16), shape((hidden, 128), jnp.float32)],
+        in_specs=vmem_specs(3),
+        out_specs=vmem_specs(4),
+        compiler_params=grant(SMALL),
+        name="weights",
+    )(w_in, in_bias.reshape(-1, 128), w_out)
 
     slab_shape = shape((per_dev, channels, SLAB), bf16)
     edge_shapes = [
@@ -536,7 +572,7 @@
         shape((per_dev, channels, HALF), bf16),
         shape((per_dev, channels, FACE_LANES), bf16),
     ]
-    back_shapes = [shape((per_dev, width, SLAB), bf16)] * size
+    back_shape = shape((width, SLAB), bf16)
 
     def gather(pieces, *after):
         states = pieces[0].shape[1]
@@ -557,11 +593,12 @@
     middle = across_grp(middle, 1)
     below0, above0 = across_dom(up0, down0)
     packed = pack(1 + early, late, below, above, up0)
-    oldest = across_grp(packed, 1)
+    late0 = across_grp(packed[:size], 1)
+    late1 = across_grp(packed[size:], 1)
     slab0, *edges = pl.pallas_call(
         edge_kernel,
         out_shape=[slab_shape] + edge_shapes,
-        in_specs=[smem] + vmem_specs(4) + [anywhere] * size,
+        in_specs=[smem] + vmem_specs(4) + [anywhere] * len(packed),
         out_specs=vmem_specs(4),
         compiler_params=grant(SMALL),
         name="edges",
@@ -569,45 +606,53 @@
     old1, up1, down1 = gather(middle, *edges)
     below1, above1 = across_dom(up1, down1)
 
-    inputs = pltpu.VMEM(((hist + 1) * channels, per_dev * SLAB), bf16)
-    kept, slab1, *rest = pl.pallas_call(
+    inputs = shape(((hist + 1) * channels, per_dev * SLAB), bf16)
+    stacked, ready, *back0 = pl.pallas_call(
         functools.partial(first_kernel, size),
-        out_shape=[shape(((hist - 1) * channels, per_dev * SLAB), bf16), slab_shape] + edge_shapes + back_shapes,
-        in_specs=[smem] + vmem_specs(15 + size),
-        out_specs=vmem_specs(5 + size),
-        scratch_shapes=[inputs],
+        out_shape=[inputs, shape((1, channels, SLAB), bf16)] + [back_shape] * size,
+        in_specs=[smem] + vmem_specs(14 + size),
+        out_specs=vmem_specs(2 + size),
         compiler_params=grant(LARGE),
         name="first",
     )(
-        plan, lay, put, flat, w_in_t, bias, w_out_t, slab0, *exchange(*edges),
-        old1, below1, above1, *oldest,
+        plan, put, flat, w_first, bias, w_out_t, slab0, *exchange(*edges),
+        old1, below1, above1, *late0,
     )
-
+    back0 = across_grp(back0, -1)
+    stacked, slab1, *rest = pl.pallas_call(
+        functools.partial(rest_kernel, size, early),
+        out_shape=[inputs, slab_shape] + edge_shapes + [back_shape] * (size * (per_dev - 1)),
+        in_specs=[smem] + vmem_specs(7 + size * (per_dev - 1)),
+        out_specs=vmem_specs(5 + size * (per_dev - 1)),
+        input_output_aliases={7: 0},
+        compiler_params=grant(LARGE),
+        name="rest",
+    )(plan, lay, w_first, bias, w_out_t, slab0, ready, stacked, *late1)
     parts = exchange(*rest[:3])
     back1 = across_grp(rest[3:], -1)
-    state = pltpu.VMEM((per_dev, channels, SLAB), bf16)
-    back2 = pl.pallas_call(
+    *back2, stacked = pl.pallas_call(
         functools.partial(second_kernel, size),
-        out_shape=back_shapes,
+        out_shape=[shape((per_dev, width, SLAB), bf16)] * size + [inputs],
         in_specs=[smem] + vmem_specs(12),
-        out_specs=vmem_specs(size),
-        scratch_shapes=[state, inputs],
+        out_specs=vmem_specs(size + 1),
+        scratch_shapes=[pltpu.VMEM((per_dev, channels, SLAB), bf16)],
+        input_output_aliases={12: size},
         compiler_params=grant(LARGE),
         name="second",
-    )(plan, put, flat, w_in_t, bias, w_out_t, slab1, *parts, kept)
+    )(plan, put, flat, w_second, bias, w_out_t, slab1, *parts, stacked)
 
     def finish(state, pieces, *before):
         return pl.pallas_call(
             functools.partial(finish_kernel, size),
             grid=(1,),
             out_shape=shape((per_dev, 2, width, cells), bf16),
-            in_specs=[smem] + vmem_specs(size) + [anywhere] * len(before),
+            in_specs=[smem] + vmem_specs(len(pieces)) + [anywhere] * len(before),
             out_specs=state_block(state),
-            input_output_aliases={1 + size: 0} if before else {},
+            input_output_aliases={1 + len(pieces): 0} if before else {},
             compiler_params=grant(SMALL),
         )(plan, *pieces, *before)
 
-    out = finish(0, back1)
+    out = finish(0, back0 + back1)
     back2 = across_grp(back2, -1)
     return finish(1, back2, out)
 

time: 125 us -> 123 us (0.984)
  local copies, waits for them, and re-layouts: 11 us -> 3.66 us
  starting transfers between devices: 58.9 us -> 62.5 us
  waiting for transfers between devices: 33.5 us -> 35.7 us
  Pallas kernels: 20.5 us -> 19 us
    unnamed x42 -> x22, local copies, waits for them, and re-layouts: 10.9 us -> 3.66 us
    ppermute x15 -> x21, starting transfers between devices: 38.3 us -> 45.3 us  [across_grp(): lax.ppermute(pieces[k], 'grp', [(i, (i + sign * k) % size) for i in range...]
    ppermute x5, waiting for transfers between devices: 2.5 us -> 5.69 us  [across_dom(): lax.ppermute(up, 'dom', up_ring)]
    ppermute x5, starting transfers between devices: 12.9 us -> 9.82 us  [across_dom(): lax.ppermute(down, 'dom', down_ring)]
    ppermute x2, starting transfers between devices: 4.24 us -> 1.34 us  [exchange(): b_in = lax.ppermute(b_out, 'grp', pair_b)]
    ppermute x2, starting transfers between devices: 3.44 us -> 5.93 us  [exchange(): a_in = lax.ppermute(a_out, 'grp', pair_a)]
    ppermute x15 -> x21, waiting for transfers between devices: 28.6 us -> 26.6 us  [across_grp(): lax.ppermute(pieces[k], 'grp', [(i, (i + sign * k) % size) for i in range...]
    pallas_call x2 -> x4, Pallas kernels: 10.1 us -> 9.93 us  [the longest x1 4.06 us: local_folded(): pl.pallas_call(functools.partial(second_kernel, size), out_shape=[shape((...]
  transfers between devices with their start and end apart: 29 -> 35, of which waited for: 11 -> 9; matrix products, arithmetic and copies ran while one was open for 1% -> 0% of each run, Pallas kernels for 9% -> 10%
where the time goes in v2:
time: 123 us; the launch traced here: 121 us
  starting transfers between devices  62.5 us (51%)
  waiting for transfers between devices  35.7 us (29%)
  Pallas kernels  19 us (15%)
  local copies, waits for them, and re-layouts  3.66 us (3%)
    ppermute x21, starting transfers between devices, across_grp(): lax.ppermute(pieces[k], 'grp', [(i, (i + sign * k) % size) for i in range...  45.3 us
    ppermute x21, waiting for transfers between devices, across_grp(): lax.ppermute(pieces[k], 'grp', [(i, (i + sign * k) % size) for i in range...  26.6 us
    ppermute x5, starting transfers between devices, across_dom(): lax.ppermute(down, 'dom', down_ring)  9.82 us
    ppermute x2, starting transfers between devices, exchange(): a_in = lax.ppermute(a_out, 'grp', pair_a)  5.93 us
    ppermute x5, waiting for transfers between devices, across_dom(): lax.ppermute(up, 'dom', up_ring)  5.69 us
    pallas_call x1, Pallas kernels, local_folded(): pl.pallas_call(functools.partial(second_kernel, size), out_shape=[shape((...  4.06 us
    unnamed x22, local copies, waits for them, and re-layouts  3.66 us
    ppermute x2, waiting for transfers between devices, exchange(): a_in = lax.ppermute(a_out, 'grp', pair_a)  3.08 us
  transfers between devices with their start and end apart: 35, of which 9 were waited for; matrix products, arithmetic and copies ran while one was open for 0% of the time, Pallas kernels for 10%

profile of v2, /device:TPU:0, one launch (start us, length us, event | category | flops | bytes accessed | tf_op | source)
XLA Modules:
  0.0 121.2 jit_solution(2500907340330174289)
XLA Ops:
  0.1 1.6 %copy-done = bf16[2,4,32,4096]{3,2,1,0:T(8,128)(2,1)S(1)} copy-done((bf16[2,4,32,4096]{3,2,1,0:T(8,128)(2,1)S(1)}, bf16[2,4,32,4096]{3,2,1,0:T(8,128)(2,1)}, u32[]{:S(2)}) %copy-start) | copy-done | bytes 2097176
  6.3 3.4 %collective-permute-start.6 = (bf16[2,32,4096]{2,1,0:T(8,128)(2,1)S(1)}, bf16[2,32,4096]{2,1,0:T(8,128)(2,1)S(1)}, u32[]{:S(2)}, u32[]{:S(2)}) collective-permute-start(bf16[2,32,4096]{2,1,0:T(8,128)(2,1)S(1)} %get-tuple-element.72), channel_id=1, source_target_pairs={{0,28},{4,0},{8,4},{12,8},{16,12},{20,16},{24,20},{28,24},{1,29},{... | collective-permute-start | bytes 1572872 | tf_op jit(solution)/shard_map/ppermute | solution.py:528
  9.7 1.6 %collective-permute-start = (bf16[2,1,32,1024]{3,2,1,0:T(8,128)(2,1)S(1)}, bf16[2,1,32,1024]{3,2,1,0:T(8,128)(2,1)S(1)}, u32[]{:S(2)}, u32[]{:S(2)}) collective-permute-start(bf16[2,1,32,1024]{3,2,1,0:T(8,128)(2,1)S(1)} %get-tuple-element.57.refs_1_), channel_id=1, source_target_pairs={{0,1},{1,2},{2,3},{3,0},{4,5},{5,6},{6,7},{7,4},{8,9},{9,10},{10,1... | collective-permute-start | bytes 393224 | tf_op jit(solution)/shard_map/ppermute | solution.py:546
  11.3 2.6 %collective-permute-start.1 = (bf16[2,1,32,1024]{3,2,1,0:T(8,128)(2,1)S(1)}, bf16[2,1,32,1024]{3,2,1,0:T(8,128)(2,1)S(1)}, u32[]{:S(2)}, u32[]{:S(2)}) collective-permute-start(bf16[2,1,32,1024]{3,2,1,0:T(8,128)(2,1)S(1)} %get-tuple-element.58.refs_2_), channel_id=1, source_target_pairs={{0,2},{1,3},{2,0},{3,1},{4,6},{5,7},{6,4},{7,5},{8,10},{9,11},{10,... | collective-permute-start | bytes 393224 | tf_op jit(solution)/shard_map/ppermute | solution.py:546
  15.8 2.2 %collective-permute-done.refs_1_ = bf16[2,1,32,1024]{3,2,1,0:T(8,128)(2,1)S(1)} collective-permute-done((bf16[2,1,32,1024]{3,2,1,0:T(8,128)(2,1)S(1)}, bf16[2,1,32,1024]{3,2,1,0:T(8,128)(2,1)S(1)}, u32[]{:S(2)}, u32[]{:S(2)}) %collective-permute-start) | collective-permute-done | bytes 131104 | tf_op jit(solution)/shard_map/ppermute | solution.py:546
  18.0 4.5 %collective-permute-done.1.refs_2_ = bf16[2,1,32,1024]{3,2,1,0:T(8,128)(2,1)S(1)} collective-permute-done((bf16[2,1,32,1024]{3,2,1,0:T(8,128)(2,1)S(1)}, bf16[2,1,32,1024]{3,2,1,0:T(8,128)(2,1)S(1)}, u32[]{:S(2)}, u32[]{:S(2)}) %collective-permute-start.1) | collective-permute-done | bytes 131104 | tf_op jit(solution)/shard_map/ppermute | solution.py:546
  23.1 1.8 %collective-permute-start.4 = (bf16[1,128,1024]{2,1,0:T(8,128)(2,1)S(1)}, bf16[1,128,1024]{2,1,0:T(8,128)(2,1)S(1)}, u32[]{:S(2)}, u32[]{:S(2)}) collective-permute-start(bf16[1,128,1024]{2,1,0:T(8,128)(2,1)S(1)} %get-tuple-element.71), channel_id=1, source_target_pairs={{0,28},{4,0},{8,4},{12,8},{16,12},{20,16},{24,20},{28,24},{1,29},{... | collective-permute-start | bytes 786440 | tf_op jit(solution)/shard_map/ppermute | solution.py:528
  24.9 3.4 %collective-permute-start.11 = (bf16[2,1,32,1024]{3,2,1,0:T(8,128)(2,1)S(1)}, bf16[2,1,32,1024]{3,2,1,0:T(8,128)(2,1)S(1)}, u32[]{:S(2)}, u32[]{:S(2)}) collective-permute-start(bf16[2,1,32,1024]{3,2,1,0:T(8,128)(2,1)S(1)} %get-tuple-element.66.refs_5_), channel_id=1, source_target_pairs={{0,1},{1,2},{2,3},{3,0},{4,5},{5,6},{6,7},{7,4},{8,9},{9,10},{10,1... | collective-permute-start | bytes 393224 | tf_op jit(solution)/shard_map/ppermute | solution.py:546
  28.3 1.4 %collective-permute-start.12 = (bf16[2,1,32,1024]{3,2,1,0:T(8,128)(2,1)S(1)}, bf16[2,1,32,1024]{3,2,1,0:T(8,128)(2,1)S(1)}, u32[]{:S(2)}, u32[]{:S(2)}) collective-permute-start(bf16[2,1,32,1024]{3,2,1,0:T(8,128)(2,1)S(1)} %get-tuple-element.67.refs_6_), channel_id=1, source_target_pairs={{0,2},{1,3},{2,0},{3,1},{4,6},{5,7},{6,4},{7,5},{8,10},{9,11},{10,... | collective-permute-start | bytes 393224 | tf_op jit(solution)/shard_map/ppermute | solution.py:546
  30.8 2.0 %collective-permute-done.3.below = bf16[1,128,1024]{2,1,0:T(8,128)(2,1)S(1)} collective-permute-done((bf16[1,128,1024]{2,1,0:T(8,128)(2,1)S(1)}, bf16[1,128,1024]{2,1,0:T(8,128)(2,1)S(1)}, u32[]{:S(2)}, u32[]{:S(2)}) %collective-permute-start.3) | collective-permute-done | bytes 262176 | tf_op jit(solution)/shard_map/ppermute | solution.py:528
  34.1 3.4 %collective-permute-start.7 = (bf16[2,128,512]{2,1,0:T(8,128)(2,1)S(1)}, bf16[2,128,512]{2,1,0:T(8,128)(2,1)S(1)}, u32[]{:S(2)}, u32[]{:S(2)}) collective-permute-start(bf16[2,128,512]{2,1,0:T(8,128)(2,1)S(1)} %get-tuple-element.82.refs_4_), channel_id=1, source_target_pairs={{0,1},{1,0},{2,3},{3,2},{4,5},{5,4},{6,7},{7,6},{8,9},{9,8},{10,11... | collective-permute-start | bytes 786440 | tf_op jit(solution)/shard_map/ppermute | solution.py:553
  39.5 1.5 %collective-permute-start.17 = (bf16[2,32,1024]{2,1,0:T(8,128)(2,1)S(1)}, bf16[2,32,1024]{2,1,0:T(8,128)(2,1)S(1)}, u32[]{:S(2)}, u32[]{:S(2)}) collective-permute-start(bf16[2,32,1024]{2,1,0:T(8,128)(2,1)S(1)} %get-tuple-element.75.refs_2_), channel_id=1, source_target_pairs={{0,2},{1,3},{2,0},{3,1},{4,6},{5,7},{6,4},{7,5},{8,10},{9,11},{10,... | collective-permute-start | bytes 393224 | tf_op jit(solution)/shard_map/ppermute | solution.py:546
  42.4 10.7 %collective-permute-done.13.refs_3_ = bf16[2,1,32,1024]{3,2,1,0:T(8,128)(2,1)S(1)} collective-permute-done((bf16[2,1,32,1024]{3,2,1,0:T(8,128)(2,1)S(1)}, bf16[2,1,32,1024]{3,2,1,0:T(8,128)(2,1)S(1)}, u32[]{:S(2)}, u32[]{:S(2)}) %collective-permute-start.13) | collective-permute-done | bytes 131104 | tf_op jit(solution)/shard_map/ppermute | solution.py:546
  55.1 2.7 %collective-permute-start.15 = (bf16[1,128,1024]{2,1,0:T(8,128)(2,1)S(1)}, bf16[1,128,1024]{2,1,0:T(8,128)(2,1)S(1)}, u32[]{:S(2)}, u32[]{:S(2)}) collective-permute-start(bf16[1,128,1024]{2,1,0:T(8,128)(2,1)S(1)} %get-tuple-element.87), channel_id=1, source_target_pairs={{0,28},{4,0},{8,4},{12,8},{16,12},{20,16},{24,20},{28,24},{1,29},{... | collective-permute-start | bytes 786440 | tf_op jit(solution)/shard_map/ppermute | solution.py:528
  57.8 8.9 %collective-permute-start.19 = (bf16[2,32,1024]{2,1,0:T(8,128)(2,1)S(1)}, bf16[2,32,1024]{2,1,0:T(8,128)(2,1)S(1)}, u32[]{:S(2)}, u32[]{:S(2)}) collective-permute-start(bf16[2,32,1024]{2,1,0:T(8,128)(2,1)S(1)} %get-tuple-element.78.refs_5_), channel_id=1, source_target_pairs={{0,1},{1,2},{2,3},{3,0},{4,5},{5,6},{6,7},{7,4},{8,9},{9,10},{10,1... | collective-permute-start | bytes 393224 | tf_op jit(solution)/shard_map/ppermute | solution.py:546
  66.7 3.6 %collective-permute-done.14.old_below = bf16[1,128,1024]{2,1,0:T(8,128)(2,1)S(1)} collective-permute-done((bf16[1,128,1024]{2,1,0:T(8,128)(2,1)S(1)}, bf16[1,128,1024]{2,1,0:T(8,128)(2,1)S(1)}, u32[]{:S(2)}, u32[]{:S(2)}) %collective-permute-start.14) | collective-permute-done | bytes 262176 | tf_op jit(solution)/shard_map/ppermute | solution.py:528
  70.4 1.9 %collective-permute-start.21 = (bf16[2,32,1024]{2,1,0:T(8,128)(2,1)S(1)}, bf16[2,32,1024]{2,1,0:T(8,128)(2,1)S(1)}, u32[]{:S(2)}, u32[]{:S(2)}) collective-permute-start(bf16[2,32,1024]{2,1,0:T(8,128)(2,1)S(1)} %get-tuple-element.80.refs_7_), channel_id=1, source_target_pairs={{0,3},{1,0},{2,1},{3,2},{4,7},{5,4},{6,5},{7,6},{8,11},{9,8},{10,9... | collective-permute-start | bytes 393224 | tf_op jit(solution)/shard_map/ppermute | solution.py:546
  72.7 2.7 %first.1 = (bf16[640,2048]{1,0:T(8,128)(2,1)S(1)}, bf16[1,128,1024]{2,1,0:T(8,128)(2,1)S(1)}, bf16[32,1024]{1,0:T(8,128)(2,1)S(1)}, bf16[32,1024]{1,0:T(8,128)(2...) custom-call(s32[64]{0:T(128)S(1)} %plan.1, bf16[256,1024]{1,0:T(8,128)(2,1)S(1)} %copy-done.3, ...), custom_call_target="tpu_custom_call" | custom-call | tf_op jit(solution)/shard_map/first/pallas_call | solution.py:610
  75.4 1.6 %collective-permute-done.20.refs_2_ = bf16[2,32,1024]{2,1,0:T(8,128)(2,1)S(1)} collective-permute-done((bf16[2,32,1024]{2,1,0:T(8,128)(2,1)S(1)}, bf16[2,32,1024]{2,1,0:T(8,128)(2,1)S(1)}, u32[]{:S(2)}, u32[]{:S(2)}) %collective-permute-start.20) | collective-permute-done | bytes 131104 | tf_op jit(solution)/shard_map/ppermute | solution.py:546
  77.0 2.8 %rest.1 = (bf16[640,2048]{1,0:T(8,128)(2,1)S(1)}, bf16[2,128,1024]{2,1,0:T(8,128)(2,1)S(1)}, bf16[2,128,512]{2,1,0:T(8,128)(2,1)S(1)}, bf16[2,128,512]{2,1,0:T(8...) custom-call(s32[64]{0:T(128)S(1)} %plan.1, ...), custom_call_target="tpu_custom_call", output_to_operand_aliasing={{0}: (7, {})} | custom-call | tf_op jit(solution)/shard_map/rest/pallas_call | solution.py:622
  81.1 2.5 %collective-permute-start.22 = (bf16[2,128,512]{2,1,0:T(8,128)(2,1)S(1)}, bf16[2,128,512]{2,1,0:T(8,128)(2,1)S(1)}, u32[]{:S(2)}, u32[]{:S(2)}) collective-permute-start(bf16[2,128,512]{2,1,0:T(8,128)(2,1)S(1)} %get-tuple-element.91), channel_id=1, source_target_pairs={{0,1},{1,0},{2,3},{3,2},{4,5},{5,4},{6,7},{7,6},{8,9},{9,8},{10,11... | collective-permute-start | bytes 786440 | tf_op jit(solution)/shard_map/ppermute | solution.py:553
  84.2 2.9 %collective-permute-start.32 = (bf16[32,1024]{1,0:T(8,128)(2,1)S(1)}, bf16[32,1024]{1,0:T(8,128)(2,1)S(1)}, u32[]{:S(2)}, u32[]{:S(2)}) collective-permute-start(bf16[32,1024]{1,0:T(8,128)(2,1)S(1)} %get-tuple-element.104), channel_id=1, source_target_pairs={{0,3},{1,0},{2,1},{3,2},{4,7},{5,4},{6,5},{7,6},{8,11},{9,8},{10,9... | collective-permute-start | bytes 196616 | tf_op jit(solution)/shard_map/ppermute | solution.py:546
  87.1 3.1 %collective-permute-done.22.a_in = bf16[2,128,512]{2,1,0:T(8,128)(2,1)S(1)} collective-permute-done((bf16[2,128,512]{2,1,0:T(8,128)(2,1)S(1)}, bf16[2,128,512]{2,1,0:T(8,128)(2,1)S(1)}, u32[]{:S(2)}, u32[]{:S(2)}) %collective-permute-start.22) | collective-permute-done | bytes 262176 | tf_op jit(solution)/shard_map/ppermute | solution.py:553
  90.2 2.5 %collective-permute-start.33 = (bf16[32,1024]{1,0:T(8,128)(2,1)S(1)}, bf16[32,1024]{1,0:T(8,128)(2,1)S(1)}, u32[]{:S(2)}, u32[]{:S(2)}) collective-permute-start(bf16[32,1024]{1,0:T(8,128)(2,1)S(1)} %get-tuple-element.105), channel_id=1, source_target_pairs={{0,2},{1,3},{2,0},{3,1},{4,6},{5,7},{6,4},{7,5},{8,10},{9,11},{10,... | collective-permute-start | bytes 196616 | tf_op jit(solution)/shard_map/ppermute | solution.py:546
  92.7 5.3 %collective-permute-start.34 = (bf16[32,1024]{1,0:T(8,128)(2,1)S(1)}, bf16[32,1024]{1,0:T(8,128)(2,1)S(1)}, u32[]{:S(2)}, u32[]{:S(2)}) collective-permute-start(bf16[32,1024]{1,0:T(8,128)(2,1)S(1)} %get-tuple-element.106), channel_id=1, source_target_pairs={{0,1},{1,2},{2,3},{3,0},{4,5},{5,6},{6,7},{7,4},{8,9},{9,10},{10,1... | collective-permute-start | bytes 196616 | tf_op jit(solution)/shard_map/ppermute | solution.py:546
  98.0 4.1 %second.1 = (bf16[2,32,1024]{2,1,0:T(8,128)(2,1)S(1)}, bf16[2,32,1024]{2,1,0:T(8,128)(2,1)S(1)}, bf16[2,32,1024]{2,1,0:T(8,128)(2,1)S(1)}, bf16[2,32,1024]{2,1,0:T(8,128)(2,1)S(1)}, bf16[640,2048]{1,0:T(8,128)(2,1)S(1)}) custom-call(s32[64]{0:T(128)S(1)} %plan.1, bf16[256,1024]{1,0:T(8,128)(2,1)S(1)} %copy-done.3, ...), custom_call_target="tpu_custom_call", output_to_operand_aliasing={{4}: (12, {})} | custom-call | tf_op jit(solution)/shard_map/second/pallas_call | solution.py:633
  102.0 3.6 %collective-permute-start.26 = (bf16[2,32,1024]{2,1,0:T(8,128)(2,1)S(1)}, bf16[2,32,1024]{2,1,0:T(8,128)(2,1)S(1)}, u32[]{:S(2)}, u32[]{:S(2)}) collective-permute-start(bf16[2,32,1024]{2,1,0:T(8,128)(2,1)S(1)} %get-tuple-element.96), channel_id=1, source_target_pairs={{0,3},{1,0},{2,1},{3,2},{4,7},{5,4},{6,5},{7,6},{8,11},{9,8},{10,9... | collective-permute-start | bytes 393224 | tf_op jit(solution)/shard_map/ppermute | solution.py:546
  106.3 1.9 %collective-permute-start.28 = (bf16[2,32,1024]{2,1,0:T(8,128)(2,1)S(1)}, bf16[2,32,1024]{2,1,0:T(8,128)(2,1)S(1)}, u32[]{:S(2)}, u32[]{:S(2)}) collective-permute-start(bf16[2,32,1024]{2,1,0:T(8,128)(2,1)S(1)} %get-tuple-element.98), channel_id=1, source_target_pairs={{0,1},{1,2},{2,3},{3,0},{4,5},{5,6},{6,7},{7,4},{8,9},{9,10},{10,1... | collective-permute-start | bytes 393224 | tf_op jit(solution)/shard_map/ppermute | solution.py:546
  108.6 2.0 %collective-permute-start.31 = (bf16[32,1024]{1,0:T(8,128)(2,1)S(1)}, bf16[32,1024]{1,0:T(8,128)(2,1)S(1)}, u32[]{:S(2)}, u32[]{:S(2)}) collective-permute-start(bf16[32,1024]{1,0:T(8,128)(2,1)S(1)} %get-tuple-element.102), channel_id=1, source_target_pairs={{0,1},{1,2},{2,3},{3,0},{4,5},{5,6},{6,7},{7,4},{8,9},{9,10},{10,1... | collective-permute-start | bytes 196616 | tf_op jit(solution)/shard_map/ppermute | solution.py:546
  110.7 7.7 %collective-permute-done.30.refs_2_ = bf16[32,1024]{1,0:T(8,128)(2,1)S(1)} collective-permute-done((bf16[32,1024]{1,0:T(8,128)(2,1)S(1)}, bf16[32,1024]{1,0:T(8,128)(2,1)S(1)}, u32[]{:S(2)}, u32[]{:S(2)}) %collective-permute-start.30) | collective-permute-done | bytes 65568 | tf_op jit(solution)/shard_map/ppermute | solution.py:546
  118.4 1.4 %shard_map.106.refs_4_ = bf16[2,2,32,4096]{3,2,1,0:T(8,128)(2,1)} custom-call(s32[64]{0:T(128)S(1)} %plan.1, bf16[32,1024]{1,0:T(8,128)(2,1)S(1)} %get-tuple-element.99.refs_0_, bf16[32,1024]{1,0:T(8,128)(2,1)S(1)} %collective-permute-done.29.refs_1_, bf16[32,1024]{1,0:T(8,128)(2,1)S(1)} %collective-permute-done.30.refs_2_, ...), custom_call_target="tpu_custom_call" | custom-call | tf_op jit(solution)/shard_map/pallas_call | solution.py:645
  119.8 1.4 %shard_map.107 = bf16[2,2,32,4096]{3,2,1,0:T(8,128)(2,1)} custom-call(s32[64]{0:T(128)S(1)} %plan.1, bf16[2,32,1024]{2,1,0:T(8,128)(2,1)S(1)} %get-tuple-element.95.refs_0_, bf16[2,32,1024]{2,1,0:T(8,128)(2,1)S(1)} %collective-permute-done.26.refs_1_, bf16[2,32,1024]{2,1,0:T(8,128)(2,1)S(1)} %collective-permute-done.27.refs_2_, ...), custom_call_target="tpu_custom_call", output_to_operand_aliasing={{}: (5, {})} | custom-call | tf_op jit(solution)/shard_map/pallas_call | solution.py:645
  (75 shorter events, 18.2 us)
Async XLA Ops:
  6.3 22.0 %collective-permute-start.6 = (bf16[2,32,4096]{2,1,0:T(8,128)(2,1)S(1)}, bf16[2,32,4096]{2,1,0:T(8,128)(2,1)S(1)}, u32[]{:S(2)}, u32[]{:S(2)}) collective-permute-start(bf16[2,32,4096]{2,1,0:T(8,128)(2,1)S(1)} %get-tuple-element.72), channel_id=1, source_target_pairs={{0,28},{4,0},{8,4},{12,8},{16,12},{20,16},{24,20},{28,24},{1,29},{... | collective-permute-start | bytes 1572872 | tf_op jit(solution)/shard_map/ppermute | solution.py:528
  9.7 20.0 %collective-permute-start.5 = (bf16[2,32,4096]{2,1,0:T(8,128)(2,1)S(1)}, bf16[2,32,4096]{2,1,0:T(8,128)(2,1)S(1)}, u32[]{:S(2)}, u32[]{:S(2)}) collective-permute-start(bf16[2,32,4096]{2,1,0:T(8,128)(2,1)S(1)} %get-tuple-element.64.refs_1_), channel_id=1, source_target_pairs={{0,4},{4,8},{8,12},{12,16},{16,20},{20,24},{24,28},{28,0},{1,5},{5... | collective-permute-start | bytes 1572872 | tf_op jit(solution)/shard_map/ppermute | solution.py:528
  9.7 8.3 %collective-permute-start = (bf16[2,1,32,1024]{3,2,1,0:T(8,128)(2,1)S(1)}, bf16[2,1,32,1024]{3,2,1,0:T(8,128)(2,1)S(1)}, u32[]{:S(2)}, u32[]{:S(2)}) collective-permute-start(bf16[2,1,32,1024]{3,2,1,0:T(8,128)(2,1)S(1)} %get-tuple-element.57.refs_1_), channel_id=1, source_target_pairs={{0,1},{1,2},{2,3},{3,0},{4,5},{5,6},{6,7},{7,4},{8,9},{9,10},{10,1... | collective-permute-start | bytes 393224 | tf_op jit(solution)/shard_map/ppermute | solution.py:546
  11.3 11.2 %collective-permute-start.1 = (bf16[2,1,32,1024]{3,2,1,0:T(8,128)(2,1)S(1)}, bf16[2,1,32,1024]{3,2,1,0:T(8,128)(2,1)S(1)}, u32[]{:S(2)}, u32[]{:S(2)}) collective-permute-start(bf16[2,1,32,1024]{3,2,1,0:T(8,128)(2,1)S(1)} %get-tuple-element.58.refs_2_), channel_id=1, source_target_pairs={{0,2},{1,3},{2,0},{3,1},{4,6},{5,7},{6,4},{7,5},{8,10},{9,11},{10,... | collective-permute-start | bytes 393224 | tf_op jit(solution)/shard_map/ppermute | solution.py:546
  13.9 8.6 %collective-permute-start.2 = (bf16[2,1,32,1024]{3,2,1,0:T(8,128)(2,1)S(1)}, bf16[2,1,32,1024]{3,2,1,0:T(8,128)(2,1)S(1)}, u32[]{:S(2)}, u32[]{:S(2)}) collective-permute-start(bf16[2,1,32,1024]{3,2,1,0:T(8,128)(2,1)S(1)} %get-tuple-element.59.refs_3_), channel_id=1, source_target_pairs={{0,3},{1,0},{2,1},{3,2},{4,7},{5,4},{6,5},{7,6},{8,11},{9,8},{10,9... | collective-permute-start | bytes 393224 | tf_op jit(solution)/shard_map/ppermute | solution.py:546
  23.1 7.7 %collective-permute-start.4 = (bf16[1,128,1024]{2,1,0:T(8,128)(2,1)S(1)}, bf16[1,128,1024]{2,1,0:T(8,128)(2,1)S(1)}, u32[]{:S(2)}, u32[]{:S(2)}) collective-permute-start(bf16[1,128,1024]{2,1,0:T(8,128)(2,1)S(1)} %get-tuple-element.71), channel_id=1, source_target_pairs={{0,28},{4,0},{8,4},{12,8},{16,12},{20,16},{24,20},{28,24},{1,29},{... | collective-permute-start | bytes 786440 | tf_op jit(solution)/shard_map/ppermute | solution.py:528
  24.9 7.9 %collective-permute-start.3 = (bf16[1,128,1024]{2,1,0:T(8,128)(2,1)S(1)}, bf16[1,128,1024]{2,1,0:T(8,128)(2,1)S(1)}, u32[]{:S(2)}, u32[]{:S(2)}) collective-permute-start(bf16[1,128,1024]{2,1,0:T(8,128)(2,1)S(1)} %get-tuple-element.70.refs_2_), channel_id=1, source_target_pairs={{0,4},{4,8},{8,12},{12,16},{16,20},{20,24},{24,28},{28,0},{1,5},{5... | collective-permute-start | bytes 786440 | tf_op jit(solution)/shard_map/ppermute | solution.py:528
  24.9 14.6 %collective-permute-start.11 = (bf16[2,1,32,1024]{3,2,1,0:T(8,128)(2,1)S(1)}, bf16[2,1,32,1024]{3,2,1,0:T(8,128)(2,1)S(1)}, u32[]{:S(2)}, u32[]{:S(2)}) collective-permute-start(bf16[2,1,32,1024]{3,2,1,0:T(8,128)(2,1)S(1)} %get-tuple-element.66.refs_5_), channel_id=1, source_target_pairs={{0,1},{1,2},{2,3},{3,0},{4,5},{5,6},{6,7},{7,4},{8,9},{9,10},{10,1... | collective-permute-start | bytes 393224 | tf_op jit(solution)/shard_map/ppermute | solution.py:546
  28.3 12.7 %collective-permute-start.12 = (bf16[2,1,32,1024]{3,2,1,0:T(8,128)(2,1)S(1)}, bf16[2,1,32,1024]{3,2,1,0:T(8,128)(2,1)S(1)}, u32[]{:S(2)}, u32[]{:S(2)}) collective-permute-start(bf16[2,1,32,1024]{3,2,1,0:T(8,128)(2,1)S(1)} %get-tuple-element.67.refs_6_), channel_id=1, source_target_pairs={{0,2},{1,3},{2,0},{3,1},{4,6},{5,7},{6,4},{7,5},{8,10},{9,11},{10,... | collective-permute-start | bytes 393224 | tf_op jit(solution)/shard_map/ppermute | solution.py:546
  34.1 21.0 %collective-permute-start.7 = (bf16[2,128,512]{2,1,0:T(8,128)(2,1)S(1)}, bf16[2,128,512]{2,1,0:T(8,128)(2,1)S(1)}, u32[]{:S(2)}, u32[]{:S(2)}) collective-permute-start(bf16[2,128,512]{2,1,0:T(8,128)(2,1)S(1)} %get-tuple-element.82.refs_4_), channel_id=1, source_target_pairs={{0,1},{1,0},{2,3},{3,2},{4,5},{5,4},{6,7},{7,6},{8,9},{9,8},{10,11... | collective-permute-start | bytes 786440 | tf_op jit(solution)/shard_map/ppermute | solution.py:553
  37.5 15.6 %collective-permute-start.13 = (bf16[2,1,32,1024]{3,2,1,0:T(8,128)(2,1)S(1)}, bf16[2,1,32,1024]{3,2,1,0:T(8,128)(2,1)S(1)}, u32[]{:S(2)}, u32[]{:S(2)}) collective-permute-start(bf16[2,1,32,1024]{3,2,1,0:T(8,128)(2,1)S(1)} %get-tuple-element.68.refs_7_), channel_id=1, source_target_pairs={{0,3},{1,0},{2,1},{3,2},{4,7},{5,4},{6,5},{7,6},{8,11},{9,8},{10,9... | collective-permute-start | bytes 393224 | tf_op jit(solution)/shard_map/ppermute | solution.py:546
  38.5 15.1 %collective-permute-start.16 = (bf16[2,32,1024]{2,1,0:T(8,128)(2,1)S(1)}, bf16[2,32,1024]{2,1,0:T(8,128)(2,1)S(1)}, u32[]{:S(2)}, u32[]{:S(2)}) collective-permute-start(bf16[2,32,1024]{2,1,0:T(8,128)(2,1)S(1)} %get-tuple-element.74.refs_1_), channel_id=1, source_target_pairs={{0,1},{1,2},{2,3},{3,0},{4,5},{5,6},{6,7},{7,4},{8,9},{9,10},{10,1... | collective-permute-start | bytes 393224 | tf_op jit(solution)/shard_map/ppermute | solution.py:546
  39.5 14.7 %collective-permute-start.17 = (bf16[2,32,1024]{2,1,0:T(8,128)(2,1)S(1)}, bf16[2,32,1024]{2,1,0:T(8,128)(2,1)S(1)}, u32[]{:S(2)}, u32[]{:S(2)}) collective-permute-start(bf16[2,32,1024]{2,1,0:T(8,128)(2,1)S(1)} %get-tuple-element.75.refs_2_), channel_id=1, source_target_pairs={{0,2},{1,3},{2,0},{3,1},{4,6},{5,7},{6,4},{7,5},{8,10},{9,11},{10,... | collective-permute-start | bytes 393224 | tf_op jit(solution)/shard_map/ppermute | solution.py:546
  41.1 13.9 %collective-permute-start.18 = (bf16[2,32,1024]{2,1,0:T(8,128)(2,1)S(1)}, bf16[2,32,1024]{2,1,0:T(8,128)(2,1)S(1)}, u32[]{:S(2)}, u32[]{:S(2)}) collective-permute-start(bf16[2,32,1024]{2,1,0:T(8,128)(2,1)S(1)} %get-tuple-element.76.refs_3_), channel_id=1, source_target_pairs={{0,3},{1,0},{2,1},{3,2},{4,7},{5,4},{6,5},{7,6},{8,11},{9,8},{10,9... | collective-permute-start | bytes 393224 | tf_op jit(solution)/shard_map/ppermute | solution.py:546
  53.1 19.5 %collective-permute-start.10 = (bf16[2,128,768]{2,1,0:T(8,128)(2,1)S(1)}, bf16[2,128,768]{2,1,0:T(8,128)(2,1)S(1)}, u32[]{:S(2)}, u32[]{:S(2)}) collective-permute-start(bf16[2,128,768]{2,1,0:T(8,128)(2,1)S(1)} %get-tuple-element.84.refs_6_.mine), channel_id=1, source_target_pairs={{0,28},{4,0},{8,4},{12,8},{16,12},{20,16},{24,20},{28,24},{1,29},{... | collective-permute-start | bytes 1179656 | tf_op jit(solution)/shard_map/ppermute | solution.py:528
  53.7 19.0 %collective-permute-start.9 = (bf16[2,128,768]{2,1,0:T(8,128)(2,1)S(1)}, bf16[2,128,768]{2,1,0:T(8,128)(2,1)S(1)}, u32[]{:S(2)}, u32[]{:S(2)}) collective-permute-start(bf16[2,128,768]{2,1,0:T(8,128)(2,1)S(1)} %get-tuple-element.84.refs_6_.mine), channel_id=1, source_target_pairs={{0,4},{4,8},{8,12},{12,16},{16,20},{20,24},{24,28},{28,0},{1,5},{5... | collective-permute-start | bytes 1179656 | tf_op jit(solution)/shard_map/ppermute | solution.py:528
  55.0 15.4 %collective-permute-start.14 = (bf16[1,128,1024]{2,1,0:T(8,128)(2,1)S(1)}, bf16[1,128,1024]{2,1,0:T(8,128)(2,1)S(1)}, u32[]{:S(2)}, u32[]{:S(2)}) collective-permute-start(bf16[1,128,1024]{2,1,0:T(8,128)(2,1)S(1)} %get-tuple-element.86), channel_id=1, source_target_pairs={{0,4},{4,8},{8,12},{12,16},{16,20},{20,24},{24,28},{28,0},{1,5},{5... | collective-permute-start | bytes 786440 | tf_op jit(solution)/shard_map/ppermute | solution.py:528
  55.1 15.3 %collective-permute-start.15 = (bf16[1,128,1024]{2,1,0:T(8,128)(2,1)S(1)}, bf16[1,128,1024]{2,1,0:T(8,128)(2,1)S(1)}, u32[]{:S(2)}, u32[]{:S(2)}) collective-permute-start(bf16[1,128,1024]{2,1,0:T(8,128)(2,1)S(1)} %get-tuple-element.87), channel_id=1, source_target_pairs={{0,28},{4,0},{8,4},{12,8},{16,12},{20,16},{24,20},{28,24},{1,29},{... | collective-permute-start | bytes 786440 | tf_op jit(solution)/shard_map/ppermute | solution.py:528
  57.8 17.6 %collective-permute-start.19 = (bf16[2,32,1024]{2,1,0:T(8,128)(2,1)S(1)}, bf16[2,32,1024]{2,1,0:T(8,128)(2,1)S(1)}, u32[]{:S(2)}, u32[]{:S(2)}) collective-permute-start(bf16[2,32,1024]{2,1,0:T(8,128)(2,1)S(1)} %get-tuple-element.78.refs_5_), channel_id=1, source_target_pairs={{0,1},{1,2},{2,3},{3,0},{4,5},{5,6},{6,7},{7,4},{8,9},{9,10},{10,1... | collective-permute-start | bytes 393224 | tf_op jit(solution)/shard_map/ppermute | solution.py:546
  79.8 18.2 %collective-permute-start.25 = (bf16[2,128,768]{2,1,0:T(8,128)(2,1)S(1)}, bf16[2,128,768]{2,1,0:T(8,128)(2,1)S(1)}, u32[]{:S(2)}, u32[]{:S(2)}) collective-permute-start(bf16[2,128,768]{2,1,0:T(8,128)(2,1)S(1)} %get-tuple-element.93.mine), channel_id=1, source_target_pairs={{0,28},{4,0},{8,4},{12,8},{16,12},{20,16},{24,20},{28,24},{1,29},{... | collective-permute-start | bytes 1179656 | tf_op jit(solution)/shard_map/ppermute | solution.py:528
  81.1 16.9 %collective-permute-start.24 = (bf16[2,128,768]{2,1,0:T(8,128)(2,1)S(1)}, bf16[2,128,768]{2,1,0:T(8,128)(2,1)S(1)}, u32[]{:S(2)}, u32[]{:S(2)}) collective-permute-start(bf16[2,128,768]{2,1,0:T(8,128)(2,1)S(1)} %get-tuple-element.93.mine), channel_id=1, source_target_pairs={{0,4},{4,8},{8,12},{12,16},{16,20},{20,24},{24,28},{28,0},{1,5},{5... | collective-permute-start | bytes 1179656 | tf_op jit(solution)/shard_map/ppermute | solution.py:528
  81.1 9.1 %collective-permute-start.22 = (bf16[2,128,512]{2,1,0:T(8,128)(2,1)S(1)}, bf16[2,128,512]{2,1,0:T(8,128)(2,1)S(1)}, u32[]{:S(2)}, u32[]{:S(2)}) collective-permute-start(bf16[2,128,512]{2,1,0:T(8,128)(2,1)S(1)} %get-tuple-element.91), channel_id=1, source_target_pairs={{0,1},{1,0},{2,3},{3,2},{4,5},{5,4},{6,7},{7,6},{8,9},{9,8},{10,11... | collective-permute-start | bytes 786440 | tf_op jit(solution)/shard_map/ppermute | solution.py:553
  83.6 9.1 %collective-permute-start.23 = (bf16[2,128,512]{2,1,0:T(8,128)(2,1)S(1)}, bf16[2,128,512]{2,1,0:T(8,128)(2,1)S(1)}, u32[]{:S(2)}, u32[]{:S(2)}) collective-permute-start(bf16[2,128,512]{2,1,0:T(8,128)(2,1)S(1)} %get-tuple-element.92), channel_id=1, source_target_pairs={{0,0},{1,2},{2,1},{3,3},{4,4},{5,6},{6,5},{7,7},{8,8},{9,10},{10,9... | collective-permute-start | bytes 786440 | tf_op jit(solution)/shard_map/ppermute | solution.py:554
  84.2 21.4 %collective-permute-start.32 = (bf16[32,1024]{1,0:T(8,128)(2,1)S(1)}, bf16[32,1024]{1,0:T(8,128)(2,1)S(1)}, u32[]{:S(2)}, u32[]{:S(2)}) collective-permute-start(bf16[32,1024]{1,0:T(8,128)(2,1)S(1)} %get-tuple-element.104), channel_id=1, source_target_pairs={{0,3},{1,0},{2,1},{3,2},{4,7},{5,4},{6,5},{7,6},{8,11},{9,8},{10,9... | collective-permute-start | bytes 196616 | tf_op jit(solution)/shard_map/ppermute | solution.py:546
  90.2 16.1 %collective-permute-start.33 = (bf16[32,1024]{1,0:T(8,128)(2,1)S(1)}, bf16[32,1024]{1,0:T(8,128)(2,1)S(1)}, u32[]{:S(2)}, u32[]{:S(2)}) collective-permute-start(bf16[32,1024]{1,0:T(8,128)(2,1)S(1)} %get-tuple-element.105), channel_id=1, source_target_pairs={{0,2},{1,3},{2,0},{3,1},{4,6},{5,7},{6,4},{7,5},{8,10},{9,11},{10,... | collective-permute-start | bytes 196616 | tf_op jit(solution)/shard_map/ppermute | solution.py:546
  92.7 15.5 %collective-permute-start.34 = (bf16[32,1024]{1,0:T(8,128)(2,1)S(1)}, bf16[32,1024]{1,0:T(8,128)(2,1)S(1)}, u32[]{:S(2)}, u32[]{:S(2)}) collective-permute-start(bf16[32,1024]{1,0:T(8,128)(2,1)S(1)} %get-tuple-element.106), channel_id=1, source_target_pairs={{0,1},{1,2},{2,3},{3,0},{4,5},{5,6},{6,7},{7,4},{8,9},{9,10},{10,1... | collective-permute-start | bytes 196616 | tf_op jit(solution)/shard_map/ppermute | solution.py:546
  98.0 10.7 %collective-permute-start.29 = (bf16[32,1024]{1,0:T(8,128)(2,1)S(1)}, bf16[32,1024]{1,0:T(8,128)(2,1)S(1)}, u32[]{:S(2)}, u32[]{:S(2)}) collective-permute-start(bf16[32,1024]{1,0:T(8,128)(2,1)S(1)} %get-tuple-element.100), channel_id=1, source_target_pairs={{0,3},{1,0},{2,1},{3,2},{4,7},{5,4},{6,5},{7,6},{8,11},{9,8},{10,9... | collective-permute-start | bytes 196616 | tf_op jit(solution)/shard_map/ppermute | solution.py:546
  102.0 17.7 %collective-permute-start.26 = (bf16[2,32,1024]{2,1,0:T(8,128)(2,1)S(1)}, bf16[2,32,1024]{2,1,0:T(8,128)(2,1)S(1)}, u32[]{:S(2)}, u32[]{:S(2)}) collective-permute-start(bf16[2,32,1024]{2,1,0:T(8,128)(2,1)S(1)} %get-tuple-element.96), channel_id=1, source_target_pairs={{0,3},{1,0},{2,1},{3,2},{4,7},{5,4},{6,5},{7,6},{8,11},{9,8},{10,9... | collective-permute-start | bytes 393224 | tf_op jit(solution)/shard_map/ppermute | solution.py:546
  105.6 14.1 %collective-permute-start.27 = (bf16[2,32,1024]{2,1,0:T(8,128)(2,1)S(1)}, bf16[2,32,1024]{2,1,0:T(8,128)(2,1)S(1)}, u32[]{:S(2)}, u32[]{:S(2)}) collective-permute-start(bf16[2,32,1024]{2,1,0:T(8,128)(2,1)S(1)} %get-tuple-element.97), channel_id=1, source_target_pairs={{0,2},{1,3},{2,0},{3,1},{4,6},{5,7},{6,4},{7,5},{8,10},{9,11},{10,... | collective-permute-start | bytes 393224 | tf_op jit(solution)/shard_map/ppermute | solution.py:546
  106.3 13.5 %collective-permute-start.28 = (bf16[2,32,1024]{2,1,0:T(8,128)(2,1)S(1)}, bf16[2,32,1024]{2,1,0:T(8,128)(2,1)S(1)}, u32[]{:S(2)}, u32[]{:S(2)}) collective-permute-start(bf16[2,32,1024]{2,1,0:T(8,128)(2,1)S(1)} %get-tuple-element.98), channel_id=1, source_target_pairs={{0,1},{1,2},{2,3},{3,0},{4,5},{5,6},{6,7},{7,4},{8,9},{9,10},{10,1... | collective-permute-start | bytes 393224 | tf_op jit(solution)/shard_map/ppermute | solution.py:546
  108.2 10.2 %collective-permute-start.30 = (bf16[32,1024]{1,0:T(8,128)(2,1)S(1)}, bf16[32,1024]{1,0:T(8,128)(2,1)S(1)}, u32[]{:S(2)}, u32[]{:S(2)}) collective-permute-start(bf16[32,1024]{1,0:T(8,128)(2,1)S(1)} %get-tuple-element.101), channel_id=1, source_target_pairs={{0,2},{1,3},{2,0},{3,1},{4,6},{5,7},{6,4},{7,5},{8,10},{9,11},{10,... | collective-permute-start | bytes 196616 | tf_op jit(solution)/shard_map/ppermute | solution.py:546
  108.6 9.8 %collective-permute-start.31 = (bf16[32,1024]{1,0:T(8,128)(2,1)S(1)}, bf16[32,1024]{1,0:T(8,128)(2,1)S(1)}, u32[]{:S(2)}, u32[]{:S(2)}) collective-permute-start(bf16[32,1024]{1,0:T(8,128)(2,1)S(1)} %get-tuple-element.102), channel_id=1, source_target_pairs={{0,1},{1,2},{2,3},{3,0},{4,5},{5,6},{6,7},{7,4},{8,9},{9,10},{10,1... | collective-permute-start | bytes 196616 | tf_op jit(solution)/shard_map/ppermute | solution.py:546
  (14 other events, 241.9 us)

commit v3 on v2

--- a/solution.py
+++ b/solution.py
@@ -366,7 +366,7 @@
             )
 
 
-TILE = 512
+TILE = 1024
 
 
 def network(plan, j, inputs, slab, w_in, bias, w_out, state):
@@ -547,11 +547,15 @@
         return moved
 
     pair_a = [(i, i ^ 1) for i in range(size)]
-    pair_b = [(i, i if i in (0, size - 1) else ((i + 1) ^ 1) - 1) for i in range(size)]
+    pair_b = []
+    for d in range(doms):
+        for i in range(size):
+            target = (d ^ 1, i) if i in (0, size - 1) else (d, ((i + 1) ^ 1) - 1)
+            pair_b.append((d * size + i, target[0] * size + target[1]))
 
     def exchange(a_out, b_out, f_out):
+        b_in = lax.ppermute(b_out, ("dom", "grp"), pair_b)
         a_in = lax.ppermute(a_out, "grp", pair_a)
-        b_in = lax.ppermute(b_out, "grp", pair_b)
         below, above = across_dom(f_out, f_out)
         return a_in, b_in, f_out, below, above
 
@@ -659,7 +663,7 @@
 
 def solution(mesh):
     placed = (P("dom", None, "grp", None), P(), P(), P(), P(), P(), P())
-    folded = mesh.shape["grp"] == 4
+    folded = mesh.shape["grp"] == 4 and mesh.shape["dom"] % 2 == 0
 
     def body(*arrays):
         return (local_folded if folded else local_general)(*arrays)

time: 123 us -> 118 us (0.959); the launches traced: 121 us -> 118 us
  starting transfers between devices: 62.5 us -> 51.5 us
  waiting for transfers between devices: 35.7 us -> 44 us
    ppermute x21, starting transfers between devices: 45.3 us -> 36.7 us  [across_grp(): lax.ppermute(pieces[k], 'grp', [(i, (i + sign * k) % size) for i in range...]
    ppermute x21, waiting for transfers between devices: 26.6 us -> 30.2 us  [across_grp(): lax.ppermute(pieces[k], 'grp', [(i, (i + sign * k) % size) for i in range...]
    ppermute x2, waiting for transfers between devices: 3.08 us -> 5.89 us  [exchange(): a_in = lax.ppermute(a_out, 'grp', pair_a)]
    ppermute x5, waiting for transfers between devices: 5.69 us -> 7.52 us  [across_dom(): lax.ppermute(up, 'dom', up_ring)]
    ppermute x2, starting transfers between devices: 5.93 us -> 4.27 us  [exchange(): a_in = lax.ppermute(a_out, 'grp', pair_a)]
  transfers between devices with their start and end apart: 35 -> 35, of which waited for: 9 -> 10; matrix products, arithmetic and copies ran while one was open for 0% -> 0% of each run, Pallas kernels for 10% -> 10%
where the time goes in v3:
time: 118 us
  starting transfers between devices  51.5 us (44%)
  waiting for transfers between devices  44 us (37%)
  Pallas kernels  18.4 us (16%)
  local copies, waits for them, and re-layouts  3.66 us (3%)
    ppermute x21, starting transfers between devices, across_grp(): lax.ppermute(pieces[k], 'grp', [(i, (i + sign * k) % size) for i in range...  36.7 us
    ppermute x21, waiting for transfers between devices, across_grp(): lax.ppermute(pieces[k], 'grp', [(i, (i + sign * k) % size) for i in range...  30.2 us
    ppermute x5, starting transfers between devices, across_dom(): lax.ppermute(down, 'dom', down_ring)  9.9 us
    ppermute x5, waiting for transfers between devices, across_dom(): lax.ppermute(up, 'dom', up_ring)  7.52 us
    ppermute x2, waiting for transfers between devices, exchange(): a_in = lax.ppermute(a_out, 'grp', pair_a)  5.89 us
    ppermute x2, starting transfers between devices, exchange(): a_in = lax.ppermute(a_out, 'grp', pair_a)  4.27 us
    pallas_call x1, Pallas kernels, local_folded(): pl.pallas_call(functools.partial(second_kernel, size), out_shape=[shape((...  3.8 us
    unnamed x22, local copies, waits for them, and re-layouts  3.66 us
  transfers between devices with their start and end apart: 35, of which 10 were waited for; matrix products, arithmetic and copies ran while one was open for 0% of the time, Pallas kernels for 10%

profile of v3, /device:TPU:0, one launch (start us, length us, event | category | flops | bytes accessed | tf_op | source)
XLA Modules:
  0.0 117.8 jit_solution(2388187085142656836)
XLA Ops:
  0.1 1.6 %copy-done = bf16[2,4,32,4096]{3,2,1,0:T(8,128)(2,1)S(1)} copy-done((bf16[2,4,32,4096]{3,2,1,0:T(8,128)(2,1)S(1)}, bf16[2,4,32,4096]{3,2,1,0:T(8,128)(2,1)}, u32[]{:S(2)}) %copy-start) | copy-done | bytes 2097176
  4.3 1.3 %plan.1 = s32[64]{0:T(128)S(1)} custom-call(s32[2]{0:T(128)S(1)} %pad_add_fusion.place, s32[6,16]{1,0:T(8,128)S(1)} %bitcast.4, s32[16]{0:T(128)S(1)} %copy-done.9, s32[16]{0:T(128)S(1)} %copy-done.10, bf16[2,1,32,1024]{3,2,1,0:T(8,128)(2,1)S(1)} %get-tuple-element.56.refs_0_, bf16[2,1,32,1024]{3,2,1,0:T(8,128)(2,1)S(1)} %get-tuple-element.57.refs_1_, ...), custom_call_target="tpu_custom_call" | custom-call | tf_op jit(solution)/shard_map/plan/pallas_call | solution.py:501
  6.3 3.4 %collective-permute-start.6 = (bf16[2,32,4096]{2,1,0:T(8,128)(2,1)S(1)}, bf16[2,32,4096]{2,1,0:T(8,128)(2,1)S(1)}, u32[]{:S(2)}, u32[]{:S(2)}) collective-permute-start(bf16[2,32,4096]{2,1,0:T(8,128)(2,1)S(1)} %get-tuple-element.72), channel_id=1, source_target_pairs={{0,28},{4,0},{8,4},{12,8},{16,12},{20,16},{24,20},{28,24},{1,29},{... | collective-permute-start | bytes 1572872 | tf_op jit(solution)/shard_map/ppermute | solution.py:528
  9.7 1.6 %collective-permute-start = (bf16[2,1,32,1024]{3,2,1,0:T(8,128)(2,1)S(1)}, bf16[2,1,32,1024]{3,2,1,0:T(8,128)(2,1)S(1)}, u32[]{:S(2)}, u32[]{:S(2)}) collective-permute-start(bf16[2,1,32,1024]{3,2,1,0:T(8,128)(2,1)S(1)} %get-tuple-element.57.refs_1_), channel_id=1, source_target_pairs={{0,1},{1,2},{2,3},{3,0},{4,5},{5,6},{6,7},{7,4},{8,9},{9,10},{10,1... | collective-permute-start | bytes 393224 | tf_op jit(solution)/shard_map/ppermute | solution.py:546
  11.3 2.6 %collective-permute-start.1 = (bf16[2,1,32,1024]{3,2,1,0:T(8,128)(2,1)S(1)}, bf16[2,1,32,1024]{3,2,1,0:T(8,128)(2,1)S(1)}, u32[]{:S(2)}, u32[]{:S(2)}) collective-permute-start(bf16[2,1,32,1024]{3,2,1,0:T(8,128)(2,1)S(1)} %get-tuple-element.58.refs_2_), channel_id=1, source_target_pairs={{0,2},{1,3},{2,0},{3,1},{4,6},{5,7},{6,4},{7,5},{8,10},{9,11},{10,... | collective-permute-start | bytes 393224 | tf_op jit(solution)/shard_map/ppermute | solution.py:546
  13.9 1.3 %collective-permute-start.2 = (bf16[2,1,32,1024]{3,2,1,0:T(8,128)(2,1)S(1)}, bf16[2,1,32,1024]{3,2,1,0:T(8,128)(2,1)S(1)}, u32[]{:S(2)}, u32[]{:S(2)}) collective-permute-start(bf16[2,1,32,1024]{3,2,1,0:T(8,128)(2,1)S(1)} %get-tuple-element.59.refs_3_), channel_id=1, source_target_pairs={{0,3},{1,0},{2,1},{3,2},{4,7},{5,4},{6,5},{7,6},{8,11},{9,8},{10,9... | collective-permute-start | bytes 393224 | tf_op jit(solution)/shard_map/ppermute | solution.py:546
  15.8 2.2 %collective-permute-done.refs_1_ = bf16[2,1,32,1024]{3,2,1,0:T(8,128)(2,1)S(1)} collective-permute-done((bf16[2,1,32,1024]{3,2,1,0:T(8,128)(2,1)S(1)}, bf16[2,1,32,1024]{3,2,1,0:T(8,128)(2,1)S(1)}, u32[]{:S(2)}, u32[]{:S(2)}) %collective-permute-start) | collective-permute-done | bytes 131104 | tf_op jit(solution)/shard_map/ppermute | solution.py:546
  18.0 4.5 %collective-permute-done.1.refs_2_ = bf16[2,1,32,1024]{3,2,1,0:T(8,128)(2,1)S(1)} collective-permute-done((bf16[2,1,32,1024]{3,2,1,0:T(8,128)(2,1)S(1)}, bf16[2,1,32,1024]{3,2,1,0:T(8,128)(2,1)S(1)}, u32[]{:S(2)}, u32[]{:S(2)}) %collective-permute-start.1) | collective-permute-done | bytes 131104 | tf_op jit(solution)/shard_map/ppermute | solution.py:546
  23.1 1.8 %collective-permute-start.4 = (bf16[1,128,1024]{2,1,0:T(8,128)(2,1)S(1)}, bf16[1,128,1024]{2,1,0:T(8,128)(2,1)S(1)}, u32[]{:S(2)}, u32[]{:S(2)}) collective-permute-start(bf16[1,128,1024]{2,1,0:T(8,128)(2,1)S(1)} %get-tuple-element.71), channel_id=1, source_target_pairs={{0,28},{4,0},{8,4},{12,8},{16,12},{20,16},{24,20},{28,24},{1,29},{... | collective-permute-start | bytes 786440 | tf_op jit(solution)/shard_map/ppermute | solution.py:528
  24.9 3.4 %collective-permute-start.11 = (bf16[2,1,32,1024]{3,2,1,0:T(8,128)(2,1)S(1)}, bf16[2,1,32,1024]{3,2,1,0:T(8,128)(2,1)S(1)}, u32[]{:S(2)}, u32[]{:S(2)}) collective-permute-start(bf16[2,1,32,1024]{3,2,1,0:T(8,128)(2,1)S(1)} %get-tuple-element.66.refs_5_), channel_id=1, source_target_pairs={{0,1},{1,2},{2,3},{3,0},{4,5},{5,6},{6,7},{7,4},{8,9},{9,10},{10,1... | collective-permute-start | bytes 393224 | tf_op jit(solution)/shard_map/ppermute | solution.py:546
  28.3 1.4 %collective-permute-start.12 = (bf16[2,1,32,1024]{3,2,1,0:T(8,128)(2,1)S(1)}, bf16[2,1,32,1024]{3,2,1,0:T(8,128)(2,1)S(1)}, u32[]{:S(2)}, u32[]{:S(2)}) collective-permute-start(bf16[2,1,32,1024]{3,2,1,0:T(8,128)(2,1)S(1)} %get-tuple-element.67.refs_6_), channel_id=1, source_target_pairs={{0,2},{1,3},{2,0},{3,1},{4,6},{5,7},{6,4},{7,5},{8,10},{9,11},{10,... | collective-permute-start | bytes 393224 | tf_op jit(solution)/shard_map/ppermute | solution.py:546
  30.8 2.0 %collective-permute-done.3.below = bf16[1,128,1024]{2,1,0:T(8,128)(2,1)S(1)} collective-permute-done((bf16[1,128,1024]{2,1,0:T(8,128)(2,1)S(1)}, bf16[1,128,1024]{2,1,0:T(8,128)(2,1)S(1)}, u32[]{:S(2)}, u32[]{:S(2)}) %collective-permute-start.3) | collective-permute-done | bytes 262176 | tf_op jit(solution)/shard_map/ppermute | solution.py:528
  34.1 3.4 %collective-permute-start.7 = (bf16[2,128,512]{2,1,0:T(8,128)(2,1)S(1)}, bf16[2,128,512]{2,1,0:T(8,128)(2,1)S(1)}, u32[]{:S(2)}, u32[]{:S(2)}) collective-permute-start(bf16[2,128,512]{2,1,0:T(8,128)(2,1)S(1)} %get-tuple-element.82.refs_4_), channel_id=1, source_target_pairs={{0,1},{1,0},{2,3},{3,2},{4,5},{5,4},{6,7},{7,6},{8,9},{9,8},{10,11... | collective-permute-start | bytes 786440 | tf_op jit(solution)/shard_map/ppermute | solution.py:558
  39.5 1.5 %collective-permute-start.17 = (bf16[2,32,1024]{2,1,0:T(8,128)(2,1)S(1)}, bf16[2,32,1024]{2,1,0:T(8,128)(2,1)S(1)}, u32[]{:S(2)}, u32[]{:S(2)}) collective-permute-start(bf16[2,32,1024]{2,1,0:T(8,128)(2,1)S(1)} %get-tuple-element.75.refs_2_), channel_id=1, source_target_pairs={{0,2},{1,3},{2,0},{3,1},{4,6},{5,7},{6,4},{7,5},{8,10},{9,11},{10,... | collective-permute-start | bytes 393224 | tf_op jit(solution)/shard_map/ppermute | solution.py:546
  41.1 1.4 %collective-permute-start.18 = (bf16[2,32,1024]{2,1,0:T(8,128)(2,1)S(1)}, bf16[2,32,1024]{2,1,0:T(8,128)(2,1)S(1)}, u32[]{:S(2)}, u32[]{:S(2)}) collective-permute-start(bf16[2,32,1024]{2,1,0:T(8,128)(2,1)S(1)} %get-tuple-element.76.refs_3_), channel_id=1, source_target_pairs={{0,3},{1,0},{2,1},{3,2},{4,7},{5,4},{6,5},{7,6},{8,11},{9,8},{10,9... | collective-permute-start | bytes 393224 | tf_op jit(solution)/shard_map/ppermute | solution.py:546
  42.4 10.7 %collective-permute-done.13.refs_3_ = bf16[2,1,32,1024]{3,2,1,0:T(8,128)(2,1)S(1)} collective-permute-done((bf16[2,1,32,1024]{3,2,1,0:T(8,128)(2,1)S(1)}, bf16[2,1,32,1024]{3,2,1,0:T(8,128)(2,1)S(1)}, u32[]{:S(2)}, u32[]{:S(2)}) %collective-permute-start.13) | collective-permute-done | bytes 131104 | tf_op jit(solution)/shard_map/ppermute | solution.py:546
  54.9 2.4 %collective-permute-start.15 = (bf16[1,128,1024]{2,1,0:T(8,128)(2,1)S(1)}, bf16[1,128,1024]{2,1,0:T(8,128)(2,1)S(1)}, u32[]{:S(2)}, u32[]{:S(2)}) collective-permute-start(bf16[1,128,1024]{2,1,0:T(8,128)(2,1)S(1)} %get-tuple-element.87), channel_id=1, source_target_pairs={{0,28},{4,0},{8,4},{12,8},{16,12},{20,16},{24,20},{28,24},{1,29},{... | collective-permute-start | bytes 786440 | tf_op jit(solution)/shard_map/ppermute | solution.py:528
  57.2 7.6 %collective-permute-start.19 = (bf16[2,32,1024]{2,1,0:T(8,128)(2,1)S(1)}, bf16[2,32,1024]{2,1,0:T(8,128)(2,1)S(1)}, u32[]{:S(2)}, u32[]{:S(2)}) collective-permute-start(bf16[2,32,1024]{2,1,0:T(8,128)(2,1)S(1)} %get-tuple-element.78.refs_5_), channel_id=1, source_target_pairs={{0,1},{1,2},{2,3},{3,0},{4,5},{5,6},{6,7},{7,4},{8,9},{9,10},{10,1... | collective-permute-start | bytes 393224 | tf_op jit(solution)/shard_map/ppermute | solution.py:546
  64.9 5.5 %collective-permute-done.14.old_below = bf16[1,128,1024]{2,1,0:T(8,128)(2,1)S(1)} collective-permute-done((bf16[1,128,1024]{2,1,0:T(8,128)(2,1)S(1)}, bf16[1,128,1024]{2,1,0:T(8,128)(2,1)S(1)}, u32[]{:S(2)}, u32[]{:S(2)}) %collective-permute-start.14) | collective-permute-done | bytes 262176 | tf_op jit(solution)/shard_map/ppermute | solution.py:528
  70.4 1.9 %collective-permute-start.21 = (bf16[2,32,1024]{2,1,0:T(8,128)(2,1)S(1)}, bf16[2,32,1024]{2,1,0:T(8,128)(2,1)S(1)}, u32[]{:S(2)}, u32[]{:S(2)}) collective-permute-start(bf16[2,32,1024]{2,1,0:T(8,128)(2,1)S(1)} %get-tuple-element.80.refs_7_), channel_id=1, source_target_pairs={{0,3},{1,0},{2,1},{3,2},{4,7},{5,4},{6,5},{7,6},{8,11},{9,8},{10,9... | collective-permute-start | bytes 393224 | tf_op jit(solution)/shard_map/ppermute | solution.py:546
  72.7 2.6 %first.1 = (bf16[640,2048]{1,0:T(8,128)(2,1)S(1)}, bf16[1,128,1024]{2,1,0:T(8,128)(2,1)S(1)}, bf16[32,1024]{1,0:T(8,128)(2,1)S(1)}, bf16[32,1024]{1,0:T(8,128)(2...) custom-call(s32[64]{0:T(128)S(1)} %plan.1, bf16[256,1024]{1,0:T(8,128)(2,1)S(1)} %copy-done.3, ...), custom_call_target="tpu_custom_call" | custom-call | tf_op jit(solution)/shard_map/first/pallas_call | solution.py:614
  75.3 1.7 %collective-permute-done.20.refs_2_ = bf16[2,32,1024]{2,1,0:T(8,128)(2,1)S(1)} collective-permute-done((bf16[2,32,1024]{2,1,0:T(8,128)(2,1)S(1)}, bf16[2,32,1024]{2,1,0:T(8,128)(2,1)S(1)}, u32[]{:S(2)}, u32[]{:S(2)}) %collective-permute-start.20) | collective-permute-done | bytes 131104 | tf_op jit(solution)/shard_map/ppermute | solution.py:546
  77.0 2.6 %rest.1 = (bf16[640,2048]{1,0:T(8,128)(2,1)S(1)}, bf16[2,128,1024]{2,1,0:T(8,128)(2,1)S(1)}, bf16[2,128,512]{2,1,0:T(8,128)(2,1)S(1)}, bf16[2,128,512]{2,1,0:T(8...) custom-call(s32[64]{0:T(128)S(1)} %plan.1, ...), custom_call_target="tpu_custom_call", output_to_operand_aliasing={{0}: (7, {})} | custom-call | tf_op jit(solution)/shard_map/rest/pallas_call | solution.py:626
  79.6 1.7 %collective-permute-start.25 = (bf16[2,128,768]{2,1,0:T(8,128)(2,1)S(1)}, bf16[2,128,768]{2,1,0:T(8,128)(2,1)S(1)}, u32[]{:S(2)}, u32[]{:S(2)}) collective-permute-start(bf16[2,128,768]{2,1,0:T(8,128)(2,1)S(1)} %get-tuple-element.93.mine), channel_id=1, source_target_pairs={{0,28},{4,0},{8,4},{12,8},{16,12},{20,16},{24,20},{28,24},{1,29},{... | collective-permute-start | bytes 1179656 | tf_op jit(solution)/shard_map/ppermute | solution.py:528
  82.4 1.6 %collective-permute-start.32 = (bf16[32,1024]{1,0:T(8,128)(2,1)S(1)}, bf16[32,1024]{1,0:T(8,128)(2,1)S(1)}, u32[]{:S(2)}, u32[]{:S(2)}) collective-permute-start(bf16[32,1024]{1,0:T(8,128)(2,1)S(1)} %get-tuple-element.104), channel_id=1, source_target_pairs={{0,3},{1,0},{2,1},{3,2},{4,7},{5,4},{6,5},{7,6},{8,11},{9,8},{10,9... | collective-permute-start | bytes 196616 | tf_op jit(solution)/shard_map/ppermute | solution.py:546
  83.9 5.9 %collective-permute-done.22.a_in = bf16[2,128,512]{2,1,0:T(8,128)(2,1)S(1)} collective-permute-done((bf16[2,128,512]{2,1,0:T(8,128)(2,1)S(1)}, bf16[2,128,512]{2,1,0:T(8,128)(2,1)S(1)}, u32[]{:S(2)}, u32[]{:S(2)}) %collective-permute-start.22) | collective-permute-done | bytes 262176 | tf_op jit(solution)/shard_map/ppermute | solution.py:558
  92.1 2.8 %collective-permute-start.29 = (bf16[32,1024]{1,0:T(8,128)(2,1)S(1)}, bf16[32,1024]{1,0:T(8,128)(2,1)S(1)}, u32[]{:S(2)}, u32[]{:S(2)}) collective-permute-start(bf16[32,1024]{1,0:T(8,128)(2,1)S(1)} %get-tuple-element.100), channel_id=1, source_target_pairs={{0,3},{1,0},{2,1},{3,2},{4,7},{5,4},{6,5},{7,6},{8,11},{9,8},{10,9... | collective-permute-start | bytes 196616 | tf_op jit(solution)/shard_map/ppermute | solution.py:546
  94.9 3.8 %second.1 = (bf16[2,32,1024]{2,1,0:T(8,128)(2,1)S(1)}, bf16[2,32,1024]{2,1,0:T(8,128)(2,1)S(1)}, bf16[2,32,1024]{2,1,0:T(8,128)(2,1)S(1)}, bf16[2,32,1024]{2,1,0:T(8,128)(2,1)S(1)}, bf16[640,2048]{1,0:T(8,128)(2,1)S(1)}) custom-call(s32[64]{0:T(128)S(1)} %plan.1, bf16[256,1024]{1,0:T(8,128)(2,1)S(1)} %copy-done.3, ...), custom_call_target="tpu_custom_call", output_to_operand_aliasing={{4}: (12, {})} | custom-call | tf_op jit(solution)/shard_map/second/pallas_call | solution.py:637
  100.9 2.9 %collective-permute-start.30 = (bf16[32,1024]{1,0:T(8,128)(2,1)S(1)}, bf16[32,1024]{1,0:T(8,128)(2,1)S(1)}, u32[]{:S(2)}, u32[]{:S(2)}) collective-permute-start(bf16[32,1024]{1,0:T(8,128)(2,1)S(1)} %get-tuple-element.101), channel_id=1, source_target_pairs={{0,2},{1,3},{2,0},{3,1},{4,6},{5,7},{6,4},{7,5},{8,10},{9,11},{10,... | collective-permute-start | bytes 196616 | tf_op jit(solution)/shard_map/ppermute | solution.py:546
  104.1 10.9 %collective-permute-done.30.refs_2_ = bf16[32,1024]{1,0:T(8,128)(2,1)S(1)} collective-permute-done((bf16[32,1024]{1,0:T(8,128)(2,1)S(1)}, bf16[32,1024]{1,0:T(8,128)(2,1)S(1)}, u32[]{:S(2)}, u32[]{:S(2)}) %collective-permute-start.30) | collective-permute-done | bytes 65568 | tf_op jit(solution)/shard_map/ppermute | solution.py:546
  115.0 1.4 %shard_map.106.refs_4_ = bf16[2,2,32,4096]{3,2,1,0:T(8,128)(2,1)} custom-call(s32[64]{0:T(128)S(1)} %plan.1, bf16[32,1024]{1,0:T(8,128)(2,1)S(1)} %get-tuple-element.99.refs_0_, bf16[32,1024]{1,0:T(8,128)(2,1)S(1)} %collective-permute-done.29.refs_1_, bf16[32,1024]{1,0:T(8,128)(2,1)S(1)} %collective-permute-done.30.refs_2_, ...), custom_call_target="tpu_custom_call" | custom-call | tf_op jit(solution)/shard_map/pallas_call | solution.py:649
  116.4 1.4 %shard_map.107 = bf16[2,2,32,4096]{3,2,1,0:T(8,128)(2,1)} custom-call(s32[64]{0:T(128)S(1)} %plan.1, bf16[2,32,1024]{2,1,0:T(8,128)(2,1)S(1)} %get-tuple-element.95.refs_0_, bf16[2,32,1024]{2,1,0:T(8,128)(2,1)S(1)} %collective-permute-done.26.refs_1_, bf16[2,32,1024]{2,1,0:T(8,128)(2,1)S(1)} %collective-permute-done.27.refs_2_, ...), custom_call_target="tpu_custom_call", output_to_operand_aliasing={{}: (5, {})} | custom-call | tf_op jit(solution)/shard_map/pallas_call | solution.py:649
  (75 shorter events, 16.8 us)
Async XLA Ops:
  6.3 22.0 %collective-permute-start.6 = (bf16[2,32,4096]{2,1,0:T(8,128)(2,1)S(1)}, bf16[2,32,4096]{2,1,0:T(8,128)(2,1)S(1)}, u32[]{:S(2)}, u32[]{:S(2)}) collective-permute-start(bf16[2,32,4096]{2,1,0:T(8,128)(2,1)S(1)} %get-tuple-element.72), channel_id=1, source_target_pairs={{0,28},{4,0},{8,4},{12,8},{16,12},{20,16},{24,20},{28,24},{1,29},{... | collective-permute-start | bytes 1572872 | tf_op jit(solution)/shard_map/ppermute | solution.py:528
  9.7 20.0 %collective-permute-start.5 = (bf16[2,32,4096]{2,1,0:T(8,128)(2,1)S(1)}, bf16[2,32,4096]{2,1,0:T(8,128)(2,1)S(1)}, u32[]{:S(2)}, u32[]{:S(2)}) collective-permute-start(bf16[2,32,4096]{2,1,0:T(8,128)(2,1)S(1)} %get-tuple-element.64.refs_1_), channel_id=1, source_target_pairs={{0,4},{4,8},{8,12},{12,16},{16,20},{20,24},{24,28},{28,0},{1,5},{5... | collective-permute-start | bytes 1572872 | tf_op jit(solution)/shard_map/ppermute | solution.py:528
  9.7 8.3 %collective-permute-start = (bf16[2,1,32,1024]{3,2,1,0:T(8,128)(2,1)S(1)}, bf16[2,1,32,1024]{3,2,1,0:T(8,128)(2,1)S(1)}, u32[]{:S(2)}, u32[]{:S(2)}) collective-permute-start(bf16[2,1,32,1024]{3,2,1,0:T(8,128)(2,1)S(1)} %get-tuple-element.57.refs_1_), channel_id=1, source_target_pairs={{0,1},{1,2},{2,3},{3,0},{4,5},{5,6},{6,7},{7,4},{8,9},{9,10},{10,1... | collective-permute-start | bytes 393224 | tf_op jit(solution)/shard_map/ppermute | solution.py:546
  11.3 11.2 %collective-permute-start.1 = (bf16[2,1,32,1024]{3,2,1,0:T(8,128)(2,1)S(1)}, bf16[2,1,32,1024]{3,2,1,0:T(8,128)(2,1)S(1)}, u32[]{:S(2)}, u32[]{:S(2)}) collective-permute-start(bf16[2,1,32,1024]{3,2,1,0:T(8,128)(2,1)S(1)} %get-tuple-element.58.refs_2_), channel_id=1, source_target_pairs={{0,2},{1,3},{2,0},{3,1},{4,6},{5,7},{6,4},{7,5},{8,10},{9,11},{10,... | collective-permute-start | bytes 393224 | tf_op jit(solution)/shard_map/ppermute | solution.py:546
  13.9 8.6 %collective-permute-start.2 = (bf16[2,1,32,1024]{3,2,1,0:T(8,128)(2,1)S(1)}, bf16[2,1,32,1024]{3,2,1,0:T(8,128)(2,1)S(1)}, u32[]{:S(2)}, u32[]{:S(2)}) collective-permute-start(bf16[2,1,32,1024]{3,2,1,0:T(8,128)(2,1)S(1)} %get-tuple-element.59.refs_3_), channel_id=1, source_target_pairs={{0,3},{1,0},{2,1},{3,2},{4,7},{5,4},{6,5},{7,6},{8,11},{9,8},{10,9... | collective-permute-start | bytes 393224 | tf_op jit(solution)/shard_map/ppermute | solution.py:546
  23.1 7.7 %collective-permute-start.4 = (bf16[1,128,1024]{2,1,0:T(8,128)(2,1)S(1)}, bf16[1,128,1024]{2,1,0:T(8,128)(2,1)S(1)}, u32[]{:S(2)}, u32[]{:S(2)}) collective-permute-start(bf16[1,128,1024]{2,1,0:T(8,128)(2,1)S(1)} %get-tuple-element.71), channel_id=1, source_target_pairs={{0,28},{4,0},{8,4},{12,8},{16,12},{20,16},{24,20},{28,24},{1,29},{... | collective-permute-start | bytes 786440 | tf_op jit(solution)/shard_map/ppermute | solution.py:528
  24.9 7.9 %collective-permute-start.3 = (bf16[1,128,1024]{2,1,0:T(8,128)(2,1)S(1)}, bf16[1,128,1024]{2,1,0:T(8,128)(2,1)S(1)}, u32[]{:S(2)}, u32[]{:S(2)}) collective-permute-start(bf16[1,128,1024]{2,1,0:T(8,128)(2,1)S(1)} %get-tuple-element.70.refs_2_), channel_id=1, source_target_pairs={{0,4},{4,8},{8,12},{12,16},{16,20},{20,24},{24,28},{28,0},{1,5},{5... | collective-permute-start | bytes 786440 | tf_op jit(solution)/shard_map/ppermute | solution.py:528
  24.9 14.6 %collective-permute-start.11 = (bf16[2,1,32,1024]{3,2,1,0:T(8,128)(2,1)S(1)}, bf16[2,1,32,1024]{3,2,1,0:T(8,128)(2,1)S(1)}, u32[]{:S(2)}, u32[]{:S(2)}) collective-permute-start(bf16[2,1,32,1024]{3,2,1,0:T(8,128)(2,1)S(1)} %get-tuple-element.66.refs_5_), channel_id=1, source_target_pairs={{0,1},{1,2},{2,3},{3,0},{4,5},{5,6},{6,7},{7,4},{8,9},{9,10},{10,1... | collective-permute-start | bytes 393224 | tf_op jit(solution)/shard_map/ppermute | solution.py:546
  28.3 12.7 %collective-permute-start.12 = (bf16[2,1,32,1024]{3,2,1,0:T(8,128)(2,1)S(1)}, bf16[2,1,32,1024]{3,2,1,0:T(8,128)(2,1)S(1)}, u32[]{:S(2)}, u32[]{:S(2)}) collective-permute-start(bf16[2,1,32,1024]{3,2,1,0:T(8,128)(2,1)S(1)} %get-tuple-element.67.refs_6_), channel_id=1, source_target_pairs={{0,2},{1,3},{2,0},{3,1},{4,6},{5,7},{6,4},{7,5},{8,10},{9,11},{10,... | collective-permute-start | bytes 393224 | tf_op jit(solution)/shard_map/ppermute | solution.py:546
  34.1 20.8 %collective-permute-start.7 = (bf16[2,128,512]{2,1,0:T(8,128)(2,1)S(1)}, bf16[2,128,512]{2,1,0:T(8,128)(2,1)S(1)}, u32[]{:S(2)}, u32[]{:S(2)}) collective-permute-start(bf16[2,128,512]{2,1,0:T(8,128)(2,1)S(1)} %get-tuple-element.82.refs_4_), channel_id=1, source_target_pairs={{0,1},{1,0},{2,3},{3,2},{4,5},{5,4},{6,7},{7,6},{8,9},{9,8},{10,11... | collective-permute-start | bytes 786440 | tf_op jit(solution)/shard_map/ppermute | solution.py:558
  37.5 15.6 %collective-permute-start.13 = (bf16[2,1,32,1024]{3,2,1,0:T(8,128)(2,1)S(1)}, bf16[2,1,32,1024]{3,2,1,0:T(8,128)(2,1)S(1)}, u32[]{:S(2)}, u32[]{:S(2)}) collective-permute-start(bf16[2,1,32,1024]{3,2,1,0:T(8,128)(2,1)S(1)} %get-tuple-element.68.refs_7_), channel_id=1, source_target_pairs={{0,3},{1,0},{2,1},{3,2},{4,7},{5,4},{6,5},{7,6},{8,11},{9,8},{10,9... | collective-permute-start | bytes 393224 | tf_op jit(solution)/shard_map/ppermute | solution.py:546
  38.5 15.1 %collective-permute-start.16 = (bf16[2,32,1024]{2,1,0:T(8,128)(2,1)S(1)}, bf16[2,32,1024]{2,1,0:T(8,128)(2,1)S(1)}, u32[]{:S(2)}, u32[]{:S(2)}) collective-permute-start(bf16[2,32,1024]{2,1,0:T(8,128)(2,1)S(1)} %get-tuple-element.74.refs_1_), channel_id=1, source_target_pairs={{0,1},{1,2},{2,3},{3,0},{4,5},{5,6},{6,7},{7,4},{8,9},{9,10},{10,1... | collective-permute-start | bytes 393224 | tf_op jit(solution)/shard_map/ppermute | solution.py:546
  39.5 14.7 %collective-permute-start.17 = (bf16[2,32,1024]{2,1,0:T(8,128)(2,1)S(1)}, bf16[2,32,1024]{2,1,0:T(8,128)(2,1)S(1)}, u32[]{:S(2)}, u32[]{:S(2)}) collective-permute-start(bf16[2,32,1024]{2,1,0:T(8,128)(2,1)S(1)} %get-tuple-element.75.refs_2_), channel_id=1, source_target_pairs={{0,2},{1,3},{2,0},{3,1},{4,6},{5,7},{6,4},{7,5},{8,10},{9,11},{10,... | collective-permute-start | bytes 393224 | tf_op jit(solution)/shard_map/ppermute | solution.py:546
  41.1 13.5 %collective-permute-start.18 = (bf16[2,32,1024]{2,1,0:T(8,128)(2,1)S(1)}, bf16[2,32,1024]{2,1,0:T(8,128)(2,1)S(1)}, u32[]{:S(2)}, u32[]{:S(2)}) collective-permute-start(bf16[2,32,1024]{2,1,0:T(8,128)(2,1)S(1)} %get-tuple-element.76.refs_3_), channel_id=1, source_target_pairs={{0,3},{1,0},{2,1},{3,2},{4,7},{5,4},{6,5},{7,6},{8,11},{9,8},{10,9... | collective-permute-start | bytes 393224 | tf_op jit(solution)/shard_map/ppermute | solution.py:546
  53.1 19.5 %collective-permute-start.10 = (bf16[2,128,768]{2,1,0:T(8,128)(2,1)S(1)}, bf16[2,128,768]{2,1,0:T(8,128)(2,1)S(1)}, u32[]{:S(2)}, u32[]{:S(2)}) collective-permute-start(bf16[2,128,768]{2,1,0:T(8,128)(2,1)S(1)} %get-tuple-element.84.refs_6_.mine), channel_id=1, source_target_pairs={{0,28},{4,0},{8,4},{12,8},{16,12},{20,16},{24,20},{28,24},{1,29},{... | collective-permute-start | bytes 1179656 | tf_op jit(solution)/shard_map/ppermute | solution.py:528
  53.7 19.0 %collective-permute-start.9 = (bf16[2,128,768]{2,1,0:T(8,128)(2,1)S(1)}, bf16[2,128,768]{2,1,0:T(8,128)(2,1)S(1)}, u32[]{:S(2)}, u32[]{:S(2)}) collective-permute-start(bf16[2,128,768]{2,1,0:T(8,128)(2,1)S(1)} %get-tuple-element.84.refs_6_.mine), channel_id=1, source_target_pairs={{0,4},{4,8},{8,12},{12,16},{16,20},{20,24},{24,28},{28,0},{1,5},{5... | collective-permute-start | bytes 1179656 | tf_op jit(solution)/shard_map/ppermute | solution.py:528
  54.6 15.8 %collective-permute-start.14 = (bf16[1,128,1024]{2,1,0:T(8,128)(2,1)S(1)}, bf16[1,128,1024]{2,1,0:T(8,128)(2,1)S(1)}, u32[]{:S(2)}, u32[]{:S(2)}) collective-permute-start(bf16[1,128,1024]{2,1,0:T(8,128)(2,1)S(1)} %get-tuple-element.86), channel_id=1, source_target_pairs={{0,4},{4,8},{8,12},{12,16},{16,20},{20,24},{24,28},{28,0},{1,5},{5... | collective-permute-start | bytes 786440 | tf_op jit(solution)/shard_map/ppermute | solution.py:528
  54.9 15.5 %collective-permute-start.15 = (bf16[1,128,1024]{2,1,0:T(8,128)(2,1)S(1)}, bf16[1,128,1024]{2,1,0:T(8,128)(2,1)S(1)}, u32[]{:S(2)}, u32[]{:S(2)}) collective-permute-start(bf16[1,128,1024]{2,1,0:T(8,128)(2,1)S(1)} %get-tuple-element.87), channel_id=1, source_target_pairs={{0,28},{4,0},{8,4},{12,8},{16,12},{20,16},{24,20},{28,24},{1,29},{... | collective-permute-start | bytes 786440 | tf_op jit(solution)/shard_map/ppermute | solution.py:528
  57.2 18.0 %collective-permute-start.19 = (bf16[2,32,1024]{2,1,0:T(8,128)(2,1)S(1)}, bf16[2,32,1024]{2,1,0:T(8,128)(2,1)S(1)}, u32[]{:S(2)}, u32[]{:S(2)}) collective-permute-start(bf16[2,32,1024]{2,1,0:T(8,128)(2,1)S(1)} %get-tuple-element.78.refs_5_), channel_id=1, source_target_pairs={{0,1},{1,2},{2,3},{3,0},{4,5},{5,6},{6,7},{7,4},{8,9},{9,10},{10,1... | collective-permute-start | bytes 393224 | tf_op jit(solution)/shard_map/ppermute | solution.py:546
  79.6 12.5 %collective-permute-start.25 = (bf16[2,128,768]{2,1,0:T(8,128)(2,1)S(1)}, bf16[2,128,768]{2,1,0:T(8,128)(2,1)S(1)}, u32[]{:S(2)}, u32[]{:S(2)}) collective-permute-start(bf16[2,128,768]{2,1,0:T(8,128)(2,1)S(1)} %get-tuple-element.93.mine), channel_id=1, source_target_pairs={{0,28},{4,0},{8,4},{12,8},{16,12},{20,16},{24,20},{28,24},{1,29},{... | collective-permute-start | bytes 1179656 | tf_op jit(solution)/shard_map/ppermute | solution.py:528
  81.3 13.6 %collective-permute-start.24 = (bf16[2,128,768]{2,1,0:T(8,128)(2,1)S(1)}, bf16[2,128,768]{2,1,0:T(8,128)(2,1)S(1)}, u32[]{:S(2)}, u32[]{:S(2)}) collective-permute-start(bf16[2,128,768]{2,1,0:T(8,128)(2,1)S(1)} %get-tuple-element.93.mine), channel_id=1, source_target_pairs={{0,4},{4,8},{8,12},{12,16},{16,20},{20,24},{24,28},{28,0},{1,5},{5... | collective-permute-start | bytes 1179656 | tf_op jit(solution)/shard_map/ppermute | solution.py:528
  81.3 8.5 %collective-permute-start.22 = (bf16[2,128,512]{2,1,0:T(8,128)(2,1)S(1)}, bf16[2,128,512]{2,1,0:T(8,128)(2,1)S(1)}, u32[]{:S(2)}, u32[]{:S(2)}) collective-permute-start(bf16[2,128,512]{2,1,0:T(8,128)(2,1)S(1)} %get-tuple-element.91), channel_id=1, source_target_pairs={{0,1},{1,0},{2,3},{3,2},{4,5},{5,4},{6,7},{7,6},{8,9},{9,8},{10,11... | collective-permute-start | bytes 786440 | tf_op jit(solution)/shard_map/ppermute | solution.py:558
  82.1 8.9 %collective-permute-start.23 = (bf16[2,128,512]{2,1,0:T(8,128)(2,1)S(1)}, bf16[2,128,512]{2,1,0:T(8,128)(2,1)S(1)}, u32[]{:S(2)}, u32[]{:S(2)}) collective-permute-start(bf16[2,128,512]{2,1,0:T(8,128)(2,1)S(1)} %get-tuple-element.92), channel_id=1, source_target_pairs={{0,4},{1,2},{2,1},{3,7},{4,0},{5,6},{6,5},{7,3},{8,12},{9,10},{10,... | collective-permute-start | bytes 786440 | tf_op jit(solution)/shard_map/ppermute | solution.py:557
  82.4 17.2 %collective-permute-start.32 = (bf16[32,1024]{1,0:T(8,128)(2,1)S(1)}, bf16[32,1024]{1,0:T(8,128)(2,1)S(1)}, u32[]{:S(2)}, u32[]{:S(2)}) collective-permute-start(bf16[32,1024]{1,0:T(8,128)(2,1)S(1)} %get-tuple-element.104), channel_id=1, source_target_pairs={{0,3},{1,0},{2,1},{3,2},{4,7},{5,4},{6,5},{7,6},{8,11},{9,8},{10,9... | collective-permute-start | bytes 196616 | tf_op jit(solution)/shard_map/ppermute | solution.py:546
  89.8 9.8 %collective-permute-start.33 = (bf16[32,1024]{1,0:T(8,128)(2,1)S(1)}, bf16[32,1024]{1,0:T(8,128)(2,1)S(1)}, u32[]{:S(2)}, u32[]{:S(2)}) collective-permute-start(bf16[32,1024]{1,0:T(8,128)(2,1)S(1)} %get-tuple-element.105), channel_id=1, source_target_pairs={{0,2},{1,3},{2,0},{3,1},{4,6},{5,7},{6,4},{7,5},{8,10},{9,11},{10,... | collective-permute-start | bytes 196616 | tf_op jit(solution)/shard_map/ppermute | solution.py:546
  91.1 9.8 %collective-permute-start.34 = (bf16[32,1024]{1,0:T(8,128)(2,1)S(1)}, bf16[32,1024]{1,0:T(8,128)(2,1)S(1)}, u32[]{:S(2)}, u32[]{:S(2)}) collective-permute-start(bf16[32,1024]{1,0:T(8,128)(2,1)S(1)} %get-tuple-element.106), channel_id=1, source_target_pairs={{0,1},{1,2},{2,3},{3,0},{4,5},{5,6},{6,7},{7,4},{8,9},{9,10},{10,1... | collective-permute-start | bytes 196616 | tf_op jit(solution)/shard_map/ppermute | solution.py:546
  92.1 11.6 %collective-permute-start.29 = (bf16[32,1024]{1,0:T(8,128)(2,1)S(1)}, bf16[32,1024]{1,0:T(8,128)(2,1)S(1)}, u32[]{:S(2)}, u32[]{:S(2)}) collective-permute-start(bf16[32,1024]{1,0:T(8,128)(2,1)S(1)} %get-tuple-element.100), channel_id=1, source_target_pairs={{0,3},{1,0},{2,1},{3,2},{4,7},{5,4},{6,5},{7,6},{8,11},{9,8},{10,9... | collective-permute-start | bytes 196616 | tf_op jit(solution)/shard_map/ppermute | solution.py:546
  98.7 17.6 %collective-permute-start.26 = (bf16[2,32,1024]{2,1,0:T(8,128)(2,1)S(1)}, bf16[2,32,1024]{2,1,0:T(8,128)(2,1)S(1)}, u32[]{:S(2)}, u32[]{:S(2)}) collective-permute-start(bf16[2,32,1024]{2,1,0:T(8,128)(2,1)S(1)} %get-tuple-element.96), channel_id=1, source_target_pairs={{0,3},{1,0},{2,1},{3,2},{4,7},{5,4},{6,5},{7,6},{8,11},{9,8},{10,9... | collective-permute-start | bytes 393224 | tf_op jit(solution)/shard_map/ppermute | solution.py:546
  99.6 16.8 %collective-permute-start.27 = (bf16[2,32,1024]{2,1,0:T(8,128)(2,1)S(1)}, bf16[2,32,1024]{2,1,0:T(8,128)(2,1)S(1)}, u32[]{:S(2)}, u32[]{:S(2)}) collective-permute-start(bf16[2,32,1024]{2,1,0:T(8,128)(2,1)S(1)} %get-tuple-element.97), channel_id=1, source_target_pairs={{0,2},{1,3},{2,0},{3,1},{4,6},{5,7},{6,4},{7,5},{8,10},{9,11},{10,... | collective-permute-start | bytes 393224 | tf_op jit(solution)/shard_map/ppermute | solution.py:546
  99.6 16.8 %collective-permute-start.28 = (bf16[2,32,1024]{2,1,0:T(8,128)(2,1)S(1)}, bf16[2,32,1024]{2,1,0:T(8,128)(2,1)S(1)}, u32[]{:S(2)}, u32[]{:S(2)}) collective-permute-start(bf16[2,32,1024]{2,1,0:T(8,128)(2,1)S(1)} %get-tuple-element.98), channel_id=1, source_target_pairs={{0,1},{1,2},{2,3},{3,0},{4,5},{5,6},{6,7},{7,4},{8,9},{9,10},{10,1... | collective-permute-start | bytes 393224 | tf_op jit(solution)/shard_map/ppermute | solution.py:546
  100.9 14.1 %collective-permute-start.30 = (bf16[32,1024]{1,0:T(8,128)(2,1)S(1)}, bf16[32,1024]{1,0:T(8,128)(2,1)S(1)}, u32[]{:S(2)}, u32[]{:S(2)}) collective-permute-start(bf16[32,1024]{1,0:T(8,128)(2,1)S(1)} %get-tuple-element.101), channel_id=1, source_target_pairs={{0,2},{1,3},{2,0},{3,1},{4,6},{5,7},{6,4},{7,5},{8,10},{9,11},{10,... | collective-permute-start | bytes 196616 | tf_op jit(solution)/shard_map/ppermute | solution.py:546
  103.8 11.2 %collective-permute-start.31 = (bf16[32,1024]{1,0:T(8,128)(2,1)S(1)}, bf16[32,1024]{1,0:T(8,128)(2,1)S(1)}, u32[]{:S(2)}, u32[]{:S(2)}) collective-permute-start(bf16[32,1024]{1,0:T(8,128)(2,1)S(1)} %get-tuple-element.102), channel_id=1, source_target_pairs={{0,1},{1,2},{2,3},{3,0},{4,5},{5,6},{6,7},{7,4},{8,9},{9,10},{10,1... | collective-permute-start | bytes 196616 | tf_op jit(solution)/shard_map/ppermute | solution.py:546
  (14 other events, 241.4 us)

commit v4 on v3

--- a/solution.py
+++ b/solution.py
@@ -117,9 +117,7 @@
     first_ok = first_nb >= 0
     first_spread = laplace_cells(history[:, 0], first_pos, first_ok)
     first_in = jnp.concatenate([history, first_spread[:, None]], 1)
-    first_back, _, _ = advance(
-        lax.all_to_all(first_in, "grp", split_axis=3, concat_axis=2, tiled=True)
-    )
+    first_back, _, _ = advance(lax.all_to_all(first_in, "grp", split_axis=3, concat_axis=2, tiled=True))
     first_step = 1.0 - 0.5 * refined[my_slots].astype(jnp.float32)
     first_state = (
         history[:, 0].astype(jnp.float32)
@@ -137,9 +135,7 @@
     newest = moved_carried[:, 0]
     second_spread = laplace_cells(newest, second_pos, second_ok)
     second_in = jnp.concatenate([moved_carried, second_spread[:, None]], 1)
-    second_back, _, _ = advance(
-        lax.all_to_all(second_in, "grp", split_axis=3, concat_axis=2, tiled=True)
-    )
+    second_back, _, _ = advance(lax.all_to_all(second_in, "grp", split_axis=3, concat_axis=2, tiled=True))
     second_state = (
         newest.astype(jnp.float32) + second_step[:, None, None] * second_back.astype(jnp.float32)
     ).astype(jnp.bfloat16)
@@ -184,9 +180,9 @@
     return [pl.BlockSpec(memory_space=VMEM)] * count
 
 
-def plan_kernel(per_dev, place, face_patch, refined, dest_slot, *refs):
+def plan_kernel(per_dev, face_patch, refined, dest_slot, *refs):
     plan = refs[-1]
-    dom, grp = place[0], place[1]
+    dom, grp = lax.axis_index("dom"), lax.axis_index("grp")
     patches = dest_slot.shape[0]
     plan[0] = dom
     plan[1] = grp
@@ -243,39 +239,44 @@
         store(above)
 
 
-def send_kernel(plan, up_in, down_in, up_out, down_out):
-    up_out[...] = up_in[0]
-    down_out[...] = down_in[0]
-
-
-def early_pack_kernel(size, states, place, *refs):
+def send_kernel(first, plan, history, up_out, down_out):
+    last = first + up_out.shape[0]
+    up_out[...] = history[plan[2], first:last]
+    down_out[...] = history[plan[3], first:last]
+
+
+def early_pack_kernel(size, first, states, *refs):
+    grp = lax.axis_index("grp")
     for k in range(1, size + 1):
         k = k % size
         out = refs[k - size]
-        for here, there in slab_lanes(lax.rem(place[1] + k, size), size):
+        for here, there in slab_lanes(lax.rem(grp + k, size), size):
             for t in range(states):
                 for j in range(out.shape[0]):
-                    out[j, t, :, here] = refs[t][j, 0, :, there]
-
-
-def pack_kernel(size, states, plan, below, above, *refs):
-    per_dev = refs[0].shape[0]
+                    out[j, t, :, here] = refs[0][j, first + t, :, there]
+
+
+def pack_kernel(size, first, plan, history, below, above, *refs):
+    per_dev = history.shape[0]
     outs = refs[-size * per_dev :]
     for j in range(per_dev):
-        for t in range(states):
-
-            def store(source):
+        for t in range(below.shape[0]):
+
+            def store(row, source):
                 for k in range(1, size + 1):
                     k = k % size
                     for here, there in slab_lanes(lax.rem(plan[1] + k, size), size):
-                        outs[j * size + k][t, :, here] = source[0, :, there]
-
-            settle(plan, j, refs[t], below.at[pl.ds(t, 1)], above.at[pl.ds(t, 1)], store)
-
-
-def emit_edges(plan, slab, lay, a_out, b_out, f_out):
+                        outs[j * size + k][t, :, here] = source[row, :, there]
+
+            settle(
+                plan, j, history, below, above,
+                lambda source: store(first + t if source.shape[0] == history.shape[1] else t, source),
+            )
+
+
+def emit_edges(plan, patches, slab, lay, a_out, b_out, f_out):
     even = lax.rem(plan[1], 2) == 0
-    for j in range(slab.shape[0]):
+    for j in patches:
         @pl.when(even)
         def _():
             a_out[j] = slab[j, :, PLANE : 3 * PLANE]
@@ -315,7 +316,7 @@
             slab[j] = source[0]
 
         settle(plan, j, old, below, above, store)
-    emit_edges(plan, slab, lay, a_out, b_out, f_out)
+    emit_edges(plan, range(slab.shape[0]), slab, lay, a_out, b_out, f_out)
 
 
 def laplacian(plan, slab, a_in, b_in, mine, below, above, put, flat, spread, first_row):
@@ -412,8 +413,8 @@
             inputs[rows, j * SLAB : (j + 1) * SLAB] = pieces[k][t]
 
 
-def first_kernel(size, plan, put, flat, w_in, bias, w_out, slab, a_in, b_in, mine, below, above, old, old_below, old_above, *refs):
-    pieces, (inputs, state), backs = refs[:size], refs[size : size + 2], refs[size + 2 :]
+def first_kernel(size, plan, lay, put, flat, w_in, bias, w_out, slab, a_in, b_in, mine, below, above, old, old_below, old_above, *refs):
+    pieces, (inputs, state), edges, backs = refs[:size], refs[size : size + 2], refs[size + 2 : size + 5], refs[size + 5 :]
     per_dev, channels = slab.shape[0], slab.shape[1]
     early = old.shape[1]
     for j in range(per_dev):
@@ -429,20 +430,20 @@
     laplacian(plan, slab, a_in, b_in, mine, below, above, put, flat, inputs, HIST * channels)
     network(plan, 0, inputs, slab, w_in, bias, w_out, state)
     emit_back(plan, state, 0, backs)
-
-
-def rest_kernel(size, early, plan, lay, w_in, bias, w_out, slab, ready, passed, *refs):
-    pieces = refs[:size]
-    inputs, state, a_out, b_out, f_out = refs[size : size + 5]
-    backs = refs[size + 5 :]
+    emit_edges(plan, range(1), state, lay, *edges)
+
+
+def rest_kernel(size, early, plan, lay, w_in, bias, w_out, slab, *refs):
+    pieces = refs[5:-5 - size * (slab.shape[0] - 1)]
+    inputs, state, *edges = refs[5 + len(pieces) : 10 + len(pieces)]
+    backs = refs[10 + len(pieces) :]
     per_dev = slab.shape[0]
     for j in range(1, per_dev):
         fill_late(plan, j, pieces[(j - 1) * size : j * size], inputs, 1 + early)
-    state[0] = ready[0]
+        network(plan, j, inputs, slab, w_in, bias, w_out, state)
+    emit_edges(plan, range(1, per_dev), state, lay, *edges)
     for j in range(1, per_dev):
-        network(plan, j, inputs, slab, w_in, bias, w_out, state)
         emit_back(plan, state, j, backs[(j - 1) * size : j * size])
-    emit_edges(plan, state, lay, a_out, b_out, f_out)
 
 
 def second_kernel(size, plan, put, flat, w_in, bias, w_out, slab, a_in, b_in, mine, below, above, passed, *refs):
@@ -478,7 +479,6 @@
     smem = pl.BlockSpec(memory_space=SMEM)
     anywhere = pl.BlockSpec(memory_space=pl.ANY)
     shape = jax.ShapeDtypeStruct
-    place = jnp.stack([lax.axis_index("dom"), lax.axis_index("grp")]).astype(jnp.int32)
     up_ring = [(i, (i + 1) % doms) for i in range(doms)]
     down_ring = [(i, (i - 1) % doms) for i in range(doms)]
 
@@ -486,14 +486,14 @@
         return pl.BlockSpec((per_dev, 1, width, cells), lambda i: (0, t, 0, 0))
 
     def early_pack(first, states, *after):
+        whole = lax.slice_in_dim(history, 0, states, axis=1) if first == 0 else history
         return pl.pallas_call(
-            functools.partial(early_pack_kernel, size, states),
-            grid=(1,),
+            functools.partial(early_pack_kernel, size, first, states),
             out_shape=[shape((per_dev, states, width, SLAB), bf16)] * size,
-            in_specs=[smem] + [state_block(first + t) for t in range(states)] + [anywhere] * len(after),
+            in_specs=vmem_specs(1) + [anywhere] * len(after),
             out_specs=vmem_specs(size),
             compiler_params=grant(SMALL),
-        )(place, *([history] * states), *after)
+        )(whole, *after)
 
     early = 1
     late = hist - 1 - early
@@ -501,44 +501,32 @@
     plan = pl.pallas_call(
         functools.partial(plan_kernel, per_dev),
         out_shape=shape((PLAN_SIZE,), jnp.int32),
-        in_specs=[smem] * 4 + [anywhere] * size,
+        in_specs=[smem] * 3 + [anywhere] * size,
         out_specs=smem,
         compiler_params=grant(SMALL),
         name="plan",
-    )(place, face_patch.T, refined, dest_slot, *newest)
+    )(face_patch.T, refined, dest_slot, *newest)
 
     def movers(first, states):
-        block = (1, 1, width, cells)
         return pl.pallas_call(
-            send_kernel,
-            grid_spec=pltpu.PrefetchScalarGridSpec(
-                num_scalar_prefetch=1,
-                grid=(states,),
-                in_specs=[
-                    pl.BlockSpec(block, lambda i, plan: (plan[2], first + i, 0, 0)),
-                    pl.BlockSpec(block, lambda i, plan: (plan[3], first + i, 0, 0)),
-                ],
-                out_specs=[pl.BlockSpec((1, width, cells), lambda i, plan: (i, 0, 0))] * 2,
-            ),
+            functools.partial(send_kernel, first),
             out_shape=[shape((states, width, cells), bf16)] * 2,
+            in_specs=[smem] + vmem_specs(1),
+            out_specs=vmem_specs(2),
             compiler_params=grant(SMALL),
-        )(plan, history, history)
+        )(plan, history)
 
     def across_dom(up, down):
         return lax.ppermute(up, "dom", up_ring), lax.ppermute(down, "dom", down_ring)
 
     def pack(first, states, below, above, *after):
-        block = (states, width, SLAB)
         return pl.pallas_call(
-            functools.partial(pack_kernel, size, states),
-            grid=(1,),
-            out_shape=[shape(block, bf16)] * (size * per_dev),
-            in_specs=[smem] + vmem_specs(2)
-            + [state_block(first + t) for t in range(states)]
-            + [anywhere] * len(after),
+            functools.partial(pack_kernel, size, first),
+            out_shape=[shape((states, width, SLAB), bf16)] * (size * per_dev),
+            in_specs=[smem] + vmem_specs(3) + [anywhere] * len(after),
             out_specs=vmem_specs(size * per_dev),
             compiler_params=grant(SMALL),
-        )(plan, below, above, *([history] * states), *after)
+        )(plan, history, below, above, *after)
 
     def across_grp(pieces, sign):
         moved = [pieces[0]]
@@ -611,27 +599,29 @@
     below1, above1 = across_dom(up1, down1)
 
     inputs = shape(((hist + 1) * channels, per_dev * SLAB), bf16)
-    stacked, ready, *back0 = pl.pallas_call(
+    stacked, slab1, *rest = pl.pallas_call(
         functools.partial(first_kernel, size),
-        out_shape=[inputs, shape((1, channels, SLAB), bf16)] + [back_shape] * size,
-        in_specs=[smem] + vmem_specs(14 + size),
-        out_specs=vmem_specs(2 + size),
+        out_shape=[inputs, slab_shape] + edge_shapes + [back_shape] * size,
+        in_specs=[smem] + vmem_specs(15 + size),
+        out_specs=vmem_specs(5 + size),
         compiler_params=grant(LARGE),
         name="first",
     )(
-        plan, put, flat, w_first, bias, w_out_t, slab0, *exchange(*edges),
+        plan, lay, put, flat, w_first, bias, w_out_t, slab0, *exchange(*edges),
         old1, below1, above1, *late0,
     )
-    back0 = across_grp(back0, -1)
+    edges = rest[:3]
+    back0 = across_grp(rest[3:], -1)
+    others = size * (per_dev - 1)
     stacked, slab1, *rest = pl.pallas_call(
         functools.partial(rest_kernel, size, early),
-        out_shape=[inputs, slab_shape] + edge_shapes + [back_shape] * (size * (per_dev - 1)),
-        in_specs=[smem] + vmem_specs(7 + size * (per_dev - 1)),
-        out_specs=vmem_specs(5 + size * (per_dev - 1)),
-        input_output_aliases={7: 0},
+        out_shape=[inputs, slab_shape] + edge_shapes + [back_shape] * others,
+        in_specs=[smem] + vmem_specs(10 + others),
+        out_specs=vmem_specs(5 + others),
+        input_output_aliases={6 + i: i for i in range(5)},
         compiler_params=grant(LARGE),
         name="rest",
-    )(plan, lay, w_first, bias, w_out_t, slab0, ready, stacked, *late1)
+    )(plan, lay, w_first, bias, w_out_t, slab0, stacked, slab1, *edges, *late1)
     parts = exchange(*rest[:3])
     back1 = across_grp(rest[3:], -1)
     *back2, stacked = pl.pallas_call(

time: 118 us -> 116 us (0.983)
  Pallas kernels: 18.4 us -> 17 us
    unnamed x22 -> x20, local copies, waits for them, and re-layouts: 3.66 us -> 2.03 us
    slice x0 -> x1, local copies, waits for them, and re-layouts: none -> 1.23 us  [early_pack(): lax.slice_in_dim(history, 0, states, axis=1)]
where the time goes in v4:
time: 116 us
  starting transfers between devices  51.5 us (44%)
  waiting for transfers between devices  44.1 us (38%)
  Pallas kernels  17 us (15%)
  local copies, waits for them, and re-layouts  3.26 us (3%)
    ppermute x21, starting transfers between devices, across_grp(): lax.ppermute(pieces[k], 'grp', [(i, (i + sign * k) % size) for i in range...  36.8 us
    ppermute x21, waiting for transfers between devices, across_grp(): lax.ppermute(pieces[k], 'grp', [(i, (i + sign * k) % size) for i in range...  30.5 us
    ppermute x5, starting transfers between devices, across_dom(): lax.ppermute(down, 'dom', down_ring)  9.88 us
    ppermute x5, waiting for transfers between devices, across_dom(): lax.ppermute(up, 'dom', up_ring)  7.51 us
    ppermute x2, waiting for transfers between devices, exchange(): a_in = lax.ppermute(a_out, 'grp', pair_a)  5.86 us
    ppermute x2, starting transfers between devices, exchange(): a_in = lax.ppermute(a_out, 'grp', pair_a)  4.27 us
    pallas_call x1, Pallas kernels, local_folded(): pl.pallas_call(functools.partial(second_kernel, size), out_shape=[shape((...  3.8 us
    pallas_call x1, Pallas kernels, local_folded(): pl.pallas_call(functools.partial(first_kernel, size), out_shape=[inputs,...  2.83 us
  transfers between devices with their start and end apart: 35, of which 10 were waited for; matrix products, arithmetic and copies ran while one was open for 0% of the time, Pallas kernels for 10%

profile of v4, /device:TPU:0, one launch (start us, length us, event | category | flops | bytes accessed | tf_op | source)
XLA Modules:
  0.0 116.1 jit_solution(18093403903685193682)
XLA Ops:
  3.3 1.3 %plan.1 = s32[64]{0:T(128)S(1)} custom-call(s32[6,16]{1,0:T(8,128)S(1)} %bitcast.2, s32[16]{0:T(128)S(1)} %copy-done.8, s32[16]{0:T(128)S(1)} %copy-done.9, bf16[2,1,32,1024]{3,2,1,0:T(8,128)(2,1)S(1)} %get-tuple-element.59.refs_0_, bf16[2,1,32,1024]{3,2,1,0:T(8,128)(2,1)S(1)} %get-tuple-element.60.refs_1_, ...), custom_call_target="tpu_custom_call" | custom-call | tf_op jit(solution)/shard_map/plan/pallas_call | solution.py:501
  5.2 3.4 %collective-permute-start.6 = (bf16[2,32,4096]{2,1,0:T(8,128)(2,1)S(1)}, bf16[2,32,4096]{2,1,0:T(8,128)(2,1)S(1)}, u32[]{:S(2)}, u32[]{:S(2)}) collective-permute-start(bf16[2,32,4096]{2,1,0:T(8,128)(2,1)S(1)} %get-tuple-element.75), channel_id=1, source_target_pairs={{0,28},{4,0},{8,4},{12,8},{16,12},{20,16},{24,20},{28,24},{1,29},{... | collective-permute-start | bytes 1572872 | tf_op jit(solution)/shard_map/ppermute | solution.py:520
  8.6 1.6 %collective-permute-start = (bf16[2,1,32,1024]{3,2,1,0:T(8,128)(2,1)S(1)}, bf16[2,1,32,1024]{3,2,1,0:T(8,128)(2,1)S(1)}, u32[]{:S(2)}, u32[]{:S(2)}) collective-permute-start(bf16[2,1,32,1024]{3,2,1,0:T(8,128)(2,1)S(1)} %get-tuple-element.60.refs_1_), channel_id=1, source_target_pairs={{0,1},{1,2},{2,3},{3,0},{4,5},{5,6},{6,7},{7,4},{8,9},{9,10},{10,1... | collective-permute-start | bytes 393224 | tf_op jit(solution)/shard_map/ppermute | solution.py:534
  10.2 2.6 %collective-permute-start.1 = (bf16[2,1,32,1024]{3,2,1,0:T(8,128)(2,1)S(1)}, bf16[2,1,32,1024]{3,2,1,0:T(8,128)(2,1)S(1)}, u32[]{:S(2)}, u32[]{:S(2)}) collective-permute-start(bf16[2,1,32,1024]{3,2,1,0:T(8,128)(2,1)S(1)} %get-tuple-element.61.refs_2_), channel_id=1, source_target_pairs={{0,2},{1,3},{2,0},{3,1},{4,6},{5,7},{6,4},{7,5},{8,10},{9,11},{10,... | collective-permute-start | bytes 393224 | tf_op jit(solution)/shard_map/ppermute | solution.py:534
  12.8 1.3 %collective-permute-start.2 = (bf16[2,1,32,1024]{3,2,1,0:T(8,128)(2,1)S(1)}, bf16[2,1,32,1024]{3,2,1,0:T(8,128)(2,1)S(1)}, u32[]{:S(2)}, u32[]{:S(2)}) collective-permute-start(bf16[2,1,32,1024]{3,2,1,0:T(8,128)(2,1)S(1)} %get-tuple-element.62.refs_3_), channel_id=1, source_target_pairs={{0,3},{1,0},{2,1},{3,2},{4,7},{5,4},{6,5},{7,6},{8,11},{9,8},{10,9... | collective-permute-start | bytes 393224 | tf_op jit(solution)/shard_map/ppermute | solution.py:534
  14.2 2.7 %collective-permute-done.refs_1_ = bf16[2,1,32,1024]{3,2,1,0:T(8,128)(2,1)S(1)} collective-permute-done((bf16[2,1,32,1024]{3,2,1,0:T(8,128)(2,1)S(1)}, bf16[2,1,32,1024]{3,2,1,0:T(8,128)(2,1)S(1)}, u32[]{:S(2)}, u32[]{:S(2)}) %collective-permute-start) | collective-permute-done | bytes 131104 | tf_op jit(solution)/shard_map/ppermute | solution.py:534
  16.9 4.5 %collective-permute-done.1.refs_2_ = bf16[2,1,32,1024]{3,2,1,0:T(8,128)(2,1)S(1)} collective-permute-done((bf16[2,1,32,1024]{3,2,1,0:T(8,128)(2,1)S(1)}, bf16[2,1,32,1024]{3,2,1,0:T(8,128)(2,1)S(1)}, u32[]{:S(2)}, u32[]{:S(2)}) %collective-permute-start.1) | collective-permute-done | bytes 131104 | tf_op jit(solution)/shard_map/ppermute | solution.py:534
  22.0 1.8 %collective-permute-start.4 = (bf16[1,128,1024]{2,1,0:T(8,128)(2,1)S(1)}, bf16[1,128,1024]{2,1,0:T(8,128)(2,1)S(1)}, u32[]{:S(2)}, u32[]{:S(2)}) collective-permute-start(bf16[1,128,1024]{2,1,0:T(8,128)(2,1)S(1)} %get-tuple-element.74), channel_id=1, source_target_pairs={{0,28},{4,0},{8,4},{12,8},{16,12},{20,16},{24,20},{28,24},{1,29},{... | collective-permute-start | bytes 786440 | tf_op jit(solution)/shard_map/ppermute | solution.py:520
  23.9 3.4 %collective-permute-start.11 = (bf16[2,1,32,1024]{3,2,1,0:T(8,128)(2,1)S(1)}, bf16[2,1,32,1024]{3,2,1,0:T(8,128)(2,1)S(1)}, u32[]{:S(2)}, u32[]{:S(2)}) collective-permute-start(bf16[2,1,32,1024]{3,2,1,0:T(8,128)(2,1)S(1)} %get-tuple-element.69.refs_5_), channel_id=1, source_target_pairs={{0,1},{1,2},{2,3},{3,0},{4,5},{5,6},{6,7},{7,4},{8,9},{9,10},{10,1... | collective-permute-start | bytes 393224 | tf_op jit(solution)/shard_map/ppermute | solution.py:534
  27.3 1.4 %collective-permute-start.12 = (bf16[2,1,32,1024]{3,2,1,0:T(8,128)(2,1)S(1)}, bf16[2,1,32,1024]{3,2,1,0:T(8,128)(2,1)S(1)}, u32[]{:S(2)}, u32[]{:S(2)}) collective-permute-start(bf16[2,1,32,1024]{3,2,1,0:T(8,128)(2,1)S(1)} %get-tuple-element.70.refs_6_), channel_id=1, source_target_pairs={{0,2},{1,3},{2,0},{3,1},{4,6},{5,7},{6,4},{7,5},{8,10},{9,11},{10,... | collective-permute-start | bytes 393224 | tf_op jit(solution)/shard_map/ppermute | solution.py:534
  29.8 2.0 %collective-permute-done.3.below = bf16[1,128,1024]{2,1,0:T(8,128)(2,1)S(1)} collective-permute-done((bf16[1,128,1024]{2,1,0:T(8,128)(2,1)S(1)}, bf16[1,128,1024]{2,1,0:T(8,128)(2,1)S(1)}, u32[]{:S(2)}, u32[]{:S(2)}) %collective-permute-start.3) | collective-permute-done | bytes 262176 | tf_op jit(solution)/shard_map/ppermute | solution.py:520
  33.0 3.4 %collective-permute-start.7 = (bf16[2,128,512]{2,1,0:T(8,128)(2,1)S(1)}, bf16[2,128,512]{2,1,0:T(8,128)(2,1)S(1)}, u32[]{:S(2)}, u32[]{:S(2)}) collective-permute-start(bf16[2,128,512]{2,1,0:T(8,128)(2,1)S(1)} %get-tuple-element.85.refs_4_), channel_id=1, source_target_pairs={{0,1},{1,0},{2,3},{3,2},{4,5},{5,4},{6,7},{7,6},{8,9},{9,8},{10,11... | collective-permute-start | bytes 786440 | tf_op jit(solution)/shard_map/ppermute | solution.py:546
  38.5 1.5 %collective-permute-start.17 = (bf16[2,32,1024]{2,1,0:T(8,128)(2,1)S(1)}, bf16[2,32,1024]{2,1,0:T(8,128)(2,1)S(1)}, u32[]{:S(2)}, u32[]{:S(2)}) collective-permute-start(bf16[2,32,1024]{2,1,0:T(8,128)(2,1)S(1)} %get-tuple-element.78.refs_2_), channel_id=1, source_target_pairs={{0,2},{1,3},{2,0},{3,1},{4,6},{5,7},{6,4},{7,5},{8,10},{9,11},{10,... | collective-permute-start | bytes 393224 | tf_op jit(solution)/shard_map/ppermute | solution.py:534
  40.0 1.4 %collective-permute-start.18 = (bf16[2,32,1024]{2,1,0:T(8,128)(2,1)S(1)}, bf16[2,32,1024]{2,1,0:T(8,128)(2,1)S(1)}, u32[]{:S(2)}, u32[]{:S(2)}) collective-permute-start(bf16[2,32,1024]{2,1,0:T(8,128)(2,1)S(1)} %get-tuple-element.79.refs_3_), channel_id=1, source_target_pairs={{0,3},{1,0},{2,1},{3,2},{4,7},{5,4},{6,5},{7,6},{8,11},{9,8},{10,9... | collective-permute-start | bytes 393224 | tf_op jit(solution)/shard_map/ppermute | solution.py:534
  41.4 10.7 %collective-permute-done.13.refs_3_ = bf16[2,1,32,1024]{3,2,1,0:T(8,128)(2,1)S(1)} collective-permute-done((bf16[2,1,32,1024]{3,2,1,0:T(8,128)(2,1)S(1)}, bf16[2,1,32,1024]{3,2,1,0:T(8,128)(2,1)S(1)}, u32[]{:S(2)}, u32[]{:S(2)}) %collective-permute-start.13) | collective-permute-done | bytes 131104 | tf_op jit(solution)/shard_map/ppermute | solution.py:534
  53.8 2.4 %collective-permute-start.15 = (bf16[1,128,1024]{2,1,0:T(8,128)(2,1)S(1)}, bf16[1,128,1024]{2,1,0:T(8,128)(2,1)S(1)}, u32[]{:S(2)}, u32[]{:S(2)}) collective-permute-start(bf16[1,128,1024]{2,1,0:T(8,128)(2,1)S(1)} %get-tuple-element.90), channel_id=1, source_target_pairs={{0,28},{4,0},{8,4},{12,8},{16,12},{20,16},{24,20},{28,24},{1,29},{... | collective-permute-start | bytes 786440 | tf_op jit(solution)/shard_map/ppermute | solution.py:520
  56.2 7.6 %collective-permute-start.19 = (bf16[2,32,1024]{2,1,0:T(8,128)(2,1)S(1)}, bf16[2,32,1024]{2,1,0:T(8,128)(2,1)S(1)}, u32[]{:S(2)}, u32[]{:S(2)}) collective-permute-start(bf16[2,32,1024]{2,1,0:T(8,128)(2,1)S(1)} %get-tuple-element.81.refs_5_), channel_id=1, source_target_pairs={{0,1},{1,2},{2,3},{3,0},{4,5},{5,6},{6,7},{7,4},{8,9},{9,10},{10,1... | collective-permute-start | bytes 393224 | tf_op jit(solution)/shard_map/ppermute | solution.py:534
  63.8 5.5 %collective-permute-done.14.old_below = bf16[1,128,1024]{2,1,0:T(8,128)(2,1)S(1)} collective-permute-done((bf16[1,128,1024]{2,1,0:T(8,128)(2,1)S(1)}, bf16[1,128,1024]{2,1,0:T(8,128)(2,1)S(1)}, u32[]{:S(2)}, u32[]{:S(2)}) %collective-permute-start.14) | collective-permute-done | bytes 262176 | tf_op jit(solution)/shard_map/ppermute | solution.py:520
  69.3 1.9 %collective-permute-start.21 = (bf16[2,32,1024]{2,1,0:T(8,128)(2,1)S(1)}, bf16[2,32,1024]{2,1,0:T(8,128)(2,1)S(1)}, u32[]{:S(2)}, u32[]{:S(2)}) collective-permute-start(bf16[2,32,1024]{2,1,0:T(8,128)(2,1)S(1)} %get-tuple-element.83.refs_7_), channel_id=1, source_target_pairs={{0,3},{1,0},{2,1},{3,2},{4,7},{5,4},{6,5},{7,6},{8,11},{9,8},{10,9... | collective-permute-start | bytes 393224 | tf_op jit(solution)/shard_map/ppermute | solution.py:534
  71.6 2.8 %first.1 = (bf16[640,2048]{1,0:T(8,128)(2,1)S(1)}, bf16[2,128,1024]{2,1,0:T(8,128)(2,1)S(1)}, bf16[2,128,512]{2,1,0:T(8,128)(2,1)S(1)}, bf16[2,128,512]{2,1,0:T(...) custom-call(s32[64]{0:T(128)S(1)} %plan.1, ...), custom_call_target="tpu_custom_call" | custom-call | tf_op jit(solution)/shard_map/first/pallas_call | solution.py:602
  74.5 1.5 %collective-permute-done.20.refs_7_ = bf16[2,32,1024]{2,1,0:T(8,128)(2,1)S(1)} collective-permute-done((bf16[2,32,1024]{2,1,0:T(8,128)(2,1)S(1)}, bf16[2,32,1024]{2,1,0:T(8,128)(2,1)S(1)}, u32[]{:S(2)}, u32[]{:S(2)}) %collective-permute-start.20) | collective-permute-done | bytes 131104 | tf_op jit(solution)/shard_map/ppermute | solution.py:534
  75.9 2.1 %rest.1 = (bf16[640,2048]{1,0:T(8,128)(2,1)S(1)}, bf16[2,128,1024]{2,1,0:T(8,128)(2,1)S(1)}, bf16[2,128,512]{2,1,0:T(8,128)(2,1)S(1)}, bf16[2,128,512]{2,1,0:T(8...) custom-call(s32[64]{0:T(128)S(1)} %plan.1, ...), custom_call_target="tpu_custom_call", output_to_operand_aliasing={{0}: (6, {}), {1}: (7, {}), {2}: (8, {}), {3}: (9, {}), {4}... | custom-call | tf_op jit(solution)/shard_map/rest/pallas_call | solution.py:616
  78.1 1.7 %collective-permute-start.25 = (bf16[2,128,768]{2,1,0:T(8,128)(2,1)S(1)}, bf16[2,128,768]{2,1,0:T(8,128)(2,1)S(1)}, u32[]{:S(2)}, u32[]{:S(2)}) collective-permute-start(bf16[2,128,768]{2,1,0:T(8,128)(2,1)S(1)} %get-tuple-element.99.mine), channel_id=1, source_target_pairs={{0,28},{4,0},{8,4},{12,8},{16,12},{20,16},{24,20},{28,24},{1,29},{... | collective-permute-start | bytes 1179656 | tf_op jit(solution)/shard_map/ppermute | solution.py:520
  80.8 1.6 %collective-permute-start.32 = (bf16[32,1024]{1,0:T(8,128)(2,1)S(1)}, bf16[32,1024]{1,0:T(8,128)(2,1)S(1)}, u32[]{:S(2)}, u32[]{:S(2)}) collective-permute-start(bf16[32,1024]{1,0:T(8,128)(2,1)S(1)} %get-tuple-element.110), channel_id=1, source_target_pairs={{0,3},{1,0},{2,1},{3,2},{4,7},{5,4},{6,5},{7,6},{8,11},{9,8},{10,9... | collective-permute-start | bytes 196616 | tf_op jit(solution)/shard_map/ppermute | solution.py:534
  82.4 5.9 %collective-permute-done.22.a_in = bf16[2,128,512]{2,1,0:T(8,128)(2,1)S(1)} collective-permute-done((bf16[2,128,512]{2,1,0:T(8,128)(2,1)S(1)}, bf16[2,128,512]{2,1,0:T(8,128)(2,1)S(1)}, u32[]{:S(2)}, u32[]{:S(2)}) %collective-permute-start.22) | collective-permute-done | bytes 262176 | tf_op jit(solution)/shard_map/ppermute | solution.py:546
  88.2 1.3 %collective-permute-start.33 = (bf16[32,1024]{1,0:T(8,128)(2,1)S(1)}, bf16[32,1024]{1,0:T(8,128)(2,1)S(1)}, u32[]{:S(2)}, u32[]{:S(2)}) collective-permute-start(bf16[32,1024]{1,0:T(8,128)(2,1)S(1)} %get-tuple-element.111), channel_id=1, source_target_pairs={{0,2},{1,3},{2,0},{3,1},{4,6},{5,7},{6,4},{7,5},{8,10},{9,11},{10,... | collective-permute-start | bytes 196616 | tf_op jit(solution)/shard_map/ppermute | solution.py:534
  90.6 2.8 %collective-permute-start.29 = (bf16[32,1024]{1,0:T(8,128)(2,1)S(1)}, bf16[32,1024]{1,0:T(8,128)(2,1)S(1)}, u32[]{:S(2)}, u32[]{:S(2)}) collective-permute-start(bf16[32,1024]{1,0:T(8,128)(2,1)S(1)} %get-tuple-element.106), channel_id=1, source_target_pairs={{0,3},{1,0},{2,1},{3,2},{4,7},{5,4},{6,5},{7,6},{8,11},{9,8},{10,9... | collective-permute-start | bytes 196616 | tf_op jit(solution)/shard_map/ppermute | solution.py:534
  93.4 3.8 %second.1 = (bf16[2,32,1024]{2,1,0:T(8,128)(2,1)S(1)}, bf16[2,32,1024]{2,1,0:T(8,128)(2,1)S(1)}, bf16[2,32,1024]{2,1,0:T(8,128)(2,1)S(1)}, bf16[2,32,1024]{2,1,0:T(8,128)(2,1)S(1)}, bf16[640,2048]{1,0:T(8,128)(2,1)S(1)}) custom-call(s32[64]{0:T(128)S(1)} %plan.1, bf16[256,1024]{1,0:T(8,128)(2,1)S(1)} %copy-done.2, ...), custom_call_target="tpu_custom_call", output_to_operand_aliasing={{4}: (12, {})} | custom-call | tf_op jit(solution)/shard_map/second/pallas_call | solution.py:627
  99.3 2.9 %collective-permute-start.30 = (bf16[32,1024]{1,0:T(8,128)(2,1)S(1)}, bf16[32,1024]{1,0:T(8,128)(2,1)S(1)}, u32[]{:S(2)}, u32[]{:S(2)}) collective-permute-start(bf16[32,1024]{1,0:T(8,128)(2,1)S(1)} %get-tuple-element.107), channel_id=1, source_target_pairs={{0,2},{1,3},{2,0},{3,1},{4,6},{5,7},{6,4},{7,5},{8,10},{9,11},{10,... | collective-permute-start | bytes 196616 | tf_op jit(solution)/shard_map/ppermute | solution.py:534
  102.5 10.8 %collective-permute-done.30.refs_2_ = bf16[32,1024]{1,0:T(8,128)(2,1)S(1)} collective-permute-done((bf16[32,1024]{1,0:T(8,128)(2,1)S(1)}, bf16[32,1024]{1,0:T(8,128)(2,1)S(1)}, u32[]{:S(2)}, u32[]{:S(2)}) %collective-permute-start.30) | collective-permute-done | bytes 65568 | tf_op jit(solution)/shard_map/ppermute | solution.py:534
  113.4 1.4 %shard_map.106.refs_4_ = bf16[2,2,32,4096]{3,2,1,0:T(8,128)(2,1)} custom-call(s32[64]{0:T(128)S(1)} %plan.1, bf16[32,1024]{1,0:T(8,128)(2,1)S(1)} %get-tuple-element.105.refs_0_, bf16[32,1024]{1,0:T(8,128)(2,1)S(1)} %collective-permute-done.29.refs_1_, bf16[32,1024]{1,0:T(8,128)(2,1)S(1)} %collective-permute-done.30.refs_2_, ...), custom_call_target="tpu_custom_call" | custom-call | tf_op jit(solution)/shard_map/pallas_call | solution.py:639
  114.7 1.4 %shard_map.107 = bf16[2,2,32,4096]{3,2,1,0:T(8,128)(2,1)} custom-call(s32[64]{0:T(128)S(1)} %plan.1, bf16[2,32,1024]{2,1,0:T(8,128)(2,1)S(1)} %get-tuple-element.101.refs_0_, bf16[2,32,1024]{2,1,0:T(8,128)(2,1)S(1)} %collective-permute-done.26.refs_1_, bf16[2,32,1024]{2,1,0:T(8,128)(2,1)S(1)} %collective-permute-done.27.refs_2_, ...), custom_call_target="tpu_custom_call", output_to_operand_aliasing={{}: (5, {})} | custom-call | tf_op jit(solution)/shard_map/pallas_call | solution.py:639
  (73 shorter events, 15.5 us)
Async XLA Ops:
  5.2 22.0 %collective-permute-start.6 = (bf16[2,32,4096]{2,1,0:T(8,128)(2,1)S(1)}, bf16[2,32,4096]{2,1,0:T(8,128)(2,1)S(1)}, u32[]{:S(2)}, u32[]{:S(2)}) collective-permute-start(bf16[2,32,4096]{2,1,0:T(8,128)(2,1)S(1)} %get-tuple-element.75), channel_id=1, source_target_pairs={{0,28},{4,0},{8,4},{12,8},{16,12},{20,16},{24,20},{28,24},{1,29},{... | collective-permute-start | bytes 1572872 | tf_op jit(solution)/shard_map/ppermute | solution.py:520
  8.6 20.0 %collective-permute-start.5 = (bf16[2,32,4096]{2,1,0:T(8,128)(2,1)S(1)}, bf16[2,32,4096]{2,1,0:T(8,128)(2,1)S(1)}, u32[]{:S(2)}, u32[]{:S(2)}) collective-permute-start(bf16[2,32,4096]{2,1,0:T(8,128)(2,1)S(1)} %get-tuple-element.67.refs_1_), channel_id=1, source_target_pairs={{0,4},{4,8},{8,12},{12,16},{16,20},{20,24},{24,28},{28,0},{1,5},{5... | collective-permute-start | bytes 1572872 | tf_op jit(solution)/shard_map/ppermute | solution.py:520
  8.6 8.3 %collective-permute-start = (bf16[2,1,32,1024]{3,2,1,0:T(8,128)(2,1)S(1)}, bf16[2,1,32,1024]{3,2,1,0:T(8,128)(2,1)S(1)}, u32[]{:S(2)}, u32[]{:S(2)}) collective-permute-start(bf16[2,1,32,1024]{3,2,1,0:T(8,128)(2,1)S(1)} %get-tuple-element.60.refs_1_), channel_id=1, source_target_pairs={{0,1},{1,2},{2,3},{3,0},{4,5},{5,6},{6,7},{7,4},{8,9},{9,10},{10,1... | collective-permute-start | bytes 393224 | tf_op jit(solution)/shard_map/ppermute | solution.py:534
  10.2 11.2 %collective-permute-start.1 = (bf16[2,1,32,1024]{3,2,1,0:T(8,128)(2,1)S(1)}, bf16[2,1,32,1024]{3,2,1,0:T(8,128)(2,1)S(1)}, u32[]{:S(2)}, u32[]{:S(2)}) collective-permute-start(bf16[2,1,32,1024]{3,2,1,0:T(8,128)(2,1)S(1)} %get-tuple-element.61.refs_2_), channel_id=1, source_target_pairs={{0,2},{1,3},{2,0},{3,1},{4,6},{5,7},{6,4},{7,5},{8,10},{9,11},{10,... | collective-permute-start | bytes 393224 | tf_op jit(solution)/shard_map/ppermute | solution.py:534
  12.8 8.6 %collective-permute-start.2 = (bf16[2,1,32,1024]{3,2,1,0:T(8,128)(2,1)S(1)}, bf16[2,1,32,1024]{3,2,1,0:T(8,128)(2,1)S(1)}, u32[]{:S(2)}, u32[]{:S(2)}) collective-permute-start(bf16[2,1,32,1024]{3,2,1,0:T(8,128)(2,1)S(1)} %get-tuple-element.62.refs_3_), channel_id=1, source_target_pairs={{0,3},{1,0},{2,1},{3,2},{4,7},{5,4},{6,5},{7,6},{8,11},{9,8},{10,9... | collective-permute-start | bytes 393224 | tf_op jit(solution)/shard_map/ppermute | solution.py:534
  22.0 7.7 %collective-permute-start.4 = (bf16[1,128,1024]{2,1,0:T(8,128)(2,1)S(1)}, bf16[1,128,1024]{2,1,0:T(8,128)(2,1)S(1)}, u32[]{:S(2)}, u32[]{:S(2)}) collective-permute-start(bf16[1,128,1024]{2,1,0:T(8,128)(2,1)S(1)} %get-tuple-element.74), channel_id=1, source_target_pairs={{0,28},{4,0},{8,4},{12,8},{16,12},{20,16},{24,20},{28,24},{1,29},{... | collective-permute-start | bytes 786440 | tf_op jit(solution)/shard_map/ppermute | solution.py:520
  23.9 7.9 %collective-permute-start.3 = (bf16[1,128,1024]{2,1,0:T(8,128)(2,1)S(1)}, bf16[1,128,1024]{2,1,0:T(8,128)(2,1)S(1)}, u32[]{:S(2)}, u32[]{:S(2)}) collective-permute-start(bf16[1,128,1024]{2,1,0:T(8,128)(2,1)S(1)} %get-tuple-element.73.refs_0_), channel_id=1, source_target_pairs={{0,4},{4,8},{8,12},{12,16},{16,20},{20,24},{24,28},{28,0},{1,5},{5... | collective-permute-start | bytes 786440 | tf_op jit(solution)/shard_map/ppermute | solution.py:520
  23.9 14.6 %collective-permute-start.11 = (bf16[2,1,32,1024]{3,2,1,0:T(8,128)(2,1)S(1)}, bf16[2,1,32,1024]{3,2,1,0:T(8,128)(2,1)S(1)}, u32[]{:S(2)}, u32[]{:S(2)}) collective-permute-start(bf16[2,1,32,1024]{3,2,1,0:T(8,128)(2,1)S(1)} %get-tuple-element.69.refs_5_), channel_id=1, source_target_pairs={{0,1},{1,2},{2,3},{3,0},{4,5},{5,6},{6,7},{7,4},{8,9},{9,10},{10,1... | collective-permute-start | bytes 393224 | tf_op jit(solution)/shard_map/ppermute | solution.py:534
  27.3 12.7 %collective-permute-start.12 = (bf16[2,1,32,1024]{3,2,1,0:T(8,128)(2,1)S(1)}, bf16[2,1,32,1024]{3,2,1,0:T(8,128)(2,1)S(1)}, u32[]{:S(2)}, u32[]{:S(2)}) collective-permute-start(bf16[2,1,32,1024]{3,2,1,0:T(8,128)(2,1)S(1)} %get-tuple-element.70.refs_6_), channel_id=1, source_target_pairs={{0,2},{1,3},{2,0},{3,1},{4,6},{5,7},{6,4},{7,5},{8,10},{9,11},{10,... | collective-permute-start | bytes 393224 | tf_op jit(solution)/shard_map/ppermute | solution.py:534
  33.0 20.8 %collective-permute-start.7 = (bf16[2,128,512]{2,1,0:T(8,128)(2,1)S(1)}, bf16[2,128,512]{2,1,0:T(8,128)(2,1)S(1)}, u32[]{:S(2)}, u32[]{:S(2)}) collective-permute-start(bf16[2,128,512]{2,1,0:T(8,128)(2,1)S(1)} %get-tuple-element.85.refs_4_), channel_id=1, source_target_pairs={{0,1},{1,0},{2,3},{3,2},{4,5},{5,4},{6,7},{7,6},{8,9},{9,8},{10,11... | collective-permute-start | bytes 786440 | tf_op jit(solution)/shard_map/ppermute | solution.py:546
  36.5 15.6 %collective-permute-start.13 = (bf16[2,1,32,1024]{3,2,1,0:T(8,128)(2,1)S(1)}, bf16[2,1,32,1024]{3,2,1,0:T(8,128)(2,1)S(1)}, u32[]{:S(2)}, u32[]{:S(2)}) collective-permute-start(bf16[2,1,32,1024]{3,2,1,0:T(8,128)(2,1)S(1)} %get-tuple-element.71.refs_7_), channel_id=1, source_target_pairs={{0,3},{1,0},{2,1},{3,2},{4,7},{5,4},{6,5},{7,6},{8,11},{9,8},{10,9... | collective-permute-start | bytes 393224 | tf_op jit(solution)/shard_map/ppermute | solution.py:534
  37.5 15.1 %collective-permute-start.16 = (bf16[2,32,1024]{2,1,0:T(8,128)(2,1)S(1)}, bf16[2,32,1024]{2,1,0:T(8,128)(2,1)S(1)}, u32[]{:S(2)}, u32[]{:S(2)}) collective-permute-start(bf16[2,32,1024]{2,1,0:T(8,128)(2,1)S(1)} %get-tuple-element.77.refs_1_), channel_id=1, source_target_pairs={{0,1},{1,2},{2,3},{3,0},{4,5},{5,6},{6,7},{7,4},{8,9},{9,10},{10,1... | collective-permute-start | bytes 393224 | tf_op jit(solution)/shard_map/ppermute | solution.py:534
  38.5 14.7 %collective-permute-start.17 = (bf16[2,32,1024]{2,1,0:T(8,128)(2,1)S(1)}, bf16[2,32,1024]{2,1,0:T(8,128)(2,1)S(1)}, u32[]{:S(2)}, u32[]{:S(2)}) collective-permute-start(bf16[2,32,1024]{2,1,0:T(8,128)(2,1)S(1)} %get-tuple-element.78.refs_2_), channel_id=1, source_target_pairs={{0,2},{1,3},{2,0},{3,1},{4,6},{5,7},{6,4},{7,5},{8,10},{9,11},{10,... | collective-permute-start | bytes 393224 | tf_op jit(solution)/shard_map/ppermute | solution.py:534
  40.0 13.5 %collective-permute-start.18 = (bf16[2,32,1024]{2,1,0:T(8,128)(2,1)S(1)}, bf16[2,32,1024]{2,1,0:T(8,128)(2,1)S(1)}, u32[]{:S(2)}, u32[]{:S(2)}) collective-permute-start(bf16[2,32,1024]{2,1,0:T(8,128)(2,1)S(1)} %get-tuple-element.79.refs_3_), channel_id=1, source_target_pairs={{0,3},{1,0},{2,1},{3,2},{4,7},{5,4},{6,5},{7,6},{8,11},{9,8},{10,9... | collective-permute-start | bytes 393224 | tf_op jit(solution)/shard_map/ppermute | solution.py:534
  52.0 19.5 %collective-permute-start.10 = (bf16[2,128,768]{2,1,0:T(8,128)(2,1)S(1)}, bf16[2,128,768]{2,1,0:T(8,128)(2,1)S(1)}, u32[]{:S(2)}, u32[]{:S(2)}) collective-permute-start(bf16[2,128,768]{2,1,0:T(8,128)(2,1)S(1)} %get-tuple-element.87.refs_6_.mine), channel_id=1, source_target_pairs={{0,28},{4,0},{8,4},{12,8},{16,12},{20,16},{24,20},{28,24},{1,29},{... | collective-permute-start | bytes 1179656 | tf_op jit(solution)/shard_map/ppermute | solution.py:520
  52.6 19.0 %collective-permute-start.9 = (bf16[2,128,768]{2,1,0:T(8,128)(2,1)S(1)}, bf16[2,128,768]{2,1,0:T(8,128)(2,1)S(1)}, u32[]{:S(2)}, u32[]{:S(2)}) collective-permute-start(bf16[2,128,768]{2,1,0:T(8,128)(2,1)S(1)} %get-tuple-element.87.refs_6_.mine), channel_id=1, source_target_pairs={{0,4},{4,8},{8,12},{12,16},{16,20},{20,24},{24,28},{28,0},{1,5},{5... | collective-permute-start | bytes 1179656 | tf_op jit(solution)/shard_map/ppermute | solution.py:520
  53.5 15.8 %collective-permute-start.14 = (bf16[1,128,1024]{2,1,0:T(8,128)(2,1)S(1)}, bf16[1,128,1024]{2,1,0:T(8,128)(2,1)S(1)}, u32[]{:S(2)}, u32[]{:S(2)}) collective-permute-start(bf16[1,128,1024]{2,1,0:T(8,128)(2,1)S(1)} %get-tuple-element.89), channel_id=1, source_target_pairs={{0,4},{4,8},{8,12},{12,16},{16,20},{20,24},{24,28},{28,0},{1,5},{5... | collective-permute-start | bytes 786440 | tf_op jit(solution)/shard_map/ppermute | solution.py:520
  53.8 15.5 %collective-permute-start.15 = (bf16[1,128,1024]{2,1,0:T(8,128)(2,1)S(1)}, bf16[1,128,1024]{2,1,0:T(8,128)(2,1)S(1)}, u32[]{:S(2)}, u32[]{:S(2)}) collective-permute-start(bf16[1,128,1024]{2,1,0:T(8,128)(2,1)S(1)} %get-tuple-element.90), channel_id=1, source_target_pairs={{0,28},{4,0},{8,4},{12,8},{16,12},{20,16},{24,20},{28,24},{1,29},{... | collective-permute-start | bytes 786440 | tf_op jit(solution)/shard_map/ppermute | solution.py:520
  56.2 18.3 %collective-permute-start.19 = (bf16[2,32,1024]{2,1,0:T(8,128)(2,1)S(1)}, bf16[2,32,1024]{2,1,0:T(8,128)(2,1)S(1)}, u32[]{:S(2)}, u32[]{:S(2)}) collective-permute-start(bf16[2,32,1024]{2,1,0:T(8,128)(2,1)S(1)} %get-tuple-element.81.refs_5_), channel_id=1, source_target_pairs={{0,1},{1,2},{2,3},{3,0},{4,5},{5,6},{6,7},{7,4},{8,9},{9,10},{10,1... | collective-permute-start | bytes 393224 | tf_op jit(solution)/shard_map/ppermute | solution.py:534
  78.1 12.5 %collective-permute-start.25 = (bf16[2,128,768]{2,1,0:T(8,128)(2,1)S(1)}, bf16[2,128,768]{2,1,0:T(8,128)(2,1)S(1)}, u32[]{:S(2)}, u32[]{:S(2)}) collective-permute-start(bf16[2,128,768]{2,1,0:T(8,128)(2,1)S(1)} %get-tuple-element.99.mine), channel_id=1, source_target_pairs={{0,28},{4,0},{8,4},{12,8},{16,12},{20,16},{24,20},{28,24},{1,29},{... | collective-permute-start | bytes 1179656 | tf_op jit(solution)/shard_map/ppermute | solution.py:520
  79.8 13.6 %collective-permute-start.24 = (bf16[2,128,768]{2,1,0:T(8,128)(2,1)S(1)}, bf16[2,128,768]{2,1,0:T(8,128)(2,1)S(1)}, u32[]{:S(2)}, u32[]{:S(2)}) collective-permute-start(bf16[2,128,768]{2,1,0:T(8,128)(2,1)S(1)} %get-tuple-element.99.mine), channel_id=1, source_target_pairs={{0,4},{4,8},{8,12},{12,16},{16,20},{20,24},{24,28},{28,0},{1,5},{5... | collective-permute-start | bytes 1179656 | tf_op jit(solution)/shard_map/ppermute | solution.py:520
  79.8 8.5 %collective-permute-start.22 = (bf16[2,128,512]{2,1,0:T(8,128)(2,1)S(1)}, bf16[2,128,512]{2,1,0:T(8,128)(2,1)S(1)}, u32[]{:S(2)}, u32[]{:S(2)}) collective-permute-start(bf16[2,128,512]{2,1,0:T(8,128)(2,1)S(1)} %get-tuple-element.97), channel_id=1, source_target_pairs={{0,1},{1,0},{2,3},{3,2},{4,5},{5,4},{6,7},{7,6},{8,9},{9,8},{10,11... | collective-permute-start | bytes 786440 | tf_op jit(solution)/shard_map/ppermute | solution.py:546
  80.6 8.9 %collective-permute-start.23 = (bf16[2,128,512]{2,1,0:T(8,128)(2,1)S(1)}, bf16[2,128,512]{2,1,0:T(8,128)(2,1)S(1)}, u32[]{:S(2)}, u32[]{:S(2)}) collective-permute-start(bf16[2,128,512]{2,1,0:T(8,128)(2,1)S(1)} %get-tuple-element.98), channel_id=1, source_target_pairs={{0,4},{1,2},{2,1},{3,7},{4,0},{5,6},{6,5},{7,3},{8,12},{9,10},{10,... | collective-permute-start | bytes 786440 | tf_op jit(solution)/shard_map/ppermute | solution.py:545
  80.8 17.3 %collective-permute-start.32 = (bf16[32,1024]{1,0:T(8,128)(2,1)S(1)}, bf16[32,1024]{1,0:T(8,128)(2,1)S(1)}, u32[]{:S(2)}, u32[]{:S(2)}) collective-permute-start(bf16[32,1024]{1,0:T(8,128)(2,1)S(1)} %get-tuple-element.110), channel_id=1, source_target_pairs={{0,3},{1,0},{2,1},{3,2},{4,7},{5,4},{6,5},{7,6},{8,11},{9,8},{10,9... | collective-permute-start | bytes 196616 | tf_op jit(solution)/shard_map/ppermute | solution.py:534
  88.2 9.8 %collective-permute-start.33 = (bf16[32,1024]{1,0:T(8,128)(2,1)S(1)}, bf16[32,1024]{1,0:T(8,128)(2,1)S(1)}, u32[]{:S(2)}, u32[]{:S(2)}) collective-permute-start(bf16[32,1024]{1,0:T(8,128)(2,1)S(1)} %get-tuple-element.111), channel_id=1, source_target_pairs={{0,2},{1,3},{2,0},{3,1},{4,6},{5,7},{6,4},{7,5},{8,10},{9,11},{10,... | collective-permute-start | bytes 196616 | tf_op jit(solution)/shard_map/ppermute | solution.py:534
  89.5 9.8 %collective-permute-start.34 = (bf16[32,1024]{1,0:T(8,128)(2,1)S(1)}, bf16[32,1024]{1,0:T(8,128)(2,1)S(1)}, u32[]{:S(2)}, u32[]{:S(2)}) collective-permute-start(bf16[32,1024]{1,0:T(8,128)(2,1)S(1)} %get-tuple-element.112), channel_id=1, source_target_pairs={{0,1},{1,2},{2,3},{3,0},{4,5},{5,6},{6,7},{7,4},{8,9},{9,10},{10,1... | collective-permute-start | bytes 196616 | tf_op jit(solution)/shard_map/ppermute | solution.py:534
  90.6 11.6 %collective-permute-start.29 = (bf16[32,1024]{1,0:T(8,128)(2,1)S(1)}, bf16[32,1024]{1,0:T(8,128)(2,1)S(1)}, u32[]{:S(2)}, u32[]{:S(2)}) collective-permute-start(bf16[32,1024]{1,0:T(8,128)(2,1)S(1)} %get-tuple-element.106), channel_id=1, source_target_pairs={{0,3},{1,0},{2,1},{3,2},{4,7},{5,4},{6,5},{7,6},{8,11},{9,8},{10,9... | collective-permute-start | bytes 196616 | tf_op jit(solution)/shard_map/ppermute | solution.py:534
  97.2 17.6 %collective-permute-start.26 = (bf16[2,32,1024]{2,1,0:T(8,128)(2,1)S(1)}, bf16[2,32,1024]{2,1,0:T(8,128)(2,1)S(1)}, u32[]{:S(2)}, u32[]{:S(2)}) collective-permute-start(bf16[2,32,1024]{2,1,0:T(8,128)(2,1)S(1)} %get-tuple-element.102), channel_id=1, source_target_pairs={{0,3},{1,0},{2,1},{3,2},{4,7},{5,4},{6,5},{7,6},{8,11},{9,8},{10,9... | collective-permute-start | bytes 393224 | tf_op jit(solution)/shard_map/ppermute | solution.py:534
  98.1 16.7 %collective-permute-start.27 = (bf16[2,32,1024]{2,1,0:T(8,128)(2,1)S(1)}, bf16[2,32,1024]{2,1,0:T(8,128)(2,1)S(1)}, u32[]{:S(2)}, u32[]{:S(2)}) collective-permute-start(bf16[2,32,1024]{2,1,0:T(8,128)(2,1)S(1)} %get-tuple-element.103), channel_id=1, source_target_pairs={{0,2},{1,3},{2,0},{3,1},{4,6},{5,7},{6,4},{7,5},{8,10},{9,11},{10,... | collective-permute-start | bytes 393224 | tf_op jit(solution)/shard_map/ppermute | solution.py:534
  98.1 16.7 %collective-permute-start.28 = (bf16[2,32,1024]{2,1,0:T(8,128)(2,1)S(1)}, bf16[2,32,1024]{2,1,0:T(8,128)(2,1)S(1)}, u32[]{:S(2)}, u32[]{:S(2)}) collective-permute-start(bf16[2,32,1024]{2,1,0:T(8,128)(2,1)S(1)} %get-tuple-element.104), channel_id=1, source_target_pairs={{0,1},{1,2},{2,3},{3,0},{4,5},{5,6},{6,7},{7,4},{8,9},{9,10},{10,1... | collective-permute-start | bytes 393224 | tf_op jit(solution)/shard_map/ppermute | solution.py:534
  99.3 14.0 %collective-permute-start.30 = (bf16[32,1024]{1,0:T(8,128)(2,1)S(1)}, bf16[32,1024]{1,0:T(8,128)(2,1)S(1)}, u32[]{:S(2)}, u32[]{:S(2)}) collective-permute-start(bf16[32,1024]{1,0:T(8,128)(2,1)S(1)} %get-tuple-element.107), channel_id=1, source_target_pairs={{0,2},{1,3},{2,0},{3,1},{4,6},{5,7},{6,4},{7,5},{8,10},{9,11},{10,... | collective-permute-start | bytes 196616 | tf_op jit(solution)/shard_map/ppermute | solution.py:534
  102.2 11.2 %collective-permute-start.31 = (bf16[32,1024]{1,0:T(8,128)(2,1)S(1)}, bf16[32,1024]{1,0:T(8,128)(2,1)S(1)}, u32[]{:S(2)}, u32[]{:S(2)}) collective-permute-start(bf16[32,1024]{1,0:T(8,128)(2,1)S(1)} %get-tuple-element.108), channel_id=1, source_target_pairs={{0,1},{1,2},{2,3},{3,0},{4,5},{5,6},{6,7},{7,4},{8,9},{9,10},{10,1... | collective-permute-start | bytes 196616 | tf_op jit(solution)/shard_map/ppermute | solution.py:534
  (13 other events, 250.1 us)
